TPU v7x, 32 devices: a whole 2x2x4 slice. The times are simulated.
32 devices in a mesh: dp: 4 (over z), expert: 2 (over core), hidden: 4 (over y, x).
Axes of the slice: x: 2, y: 2, z: 4, core: 2. Of those that a mesh axis runs over, the one named last changes fastest.
Arguments:
- patches: bfloat16 [8192, 768], P(('dp', 'expert'), 'hidden'), may hold values from -6 to 6
- cond: bfloat16 [256, 768], P(('dp', 'expert')), may hold values from -6 to 6
- seg_ids: int32 [32, 256], P(('dp', 'expert')), may hold values from 0 to 7, never falling along the last dimension, each value on 1 to 64 neighbouring positions
- seg_image: int32 [32, 8], P(('dp', 'expert')), may hold values from 0 to 31
- routes: int32 [8192, 2], P(('dp', 'expert')), may hold values from 0 to 7, all different within a row; in each aligned block of 1024 rows (0 to 1023, 1024 to 2047, ...) at most 384 rows name the same one
- gates: float32 [8192, 2], P(('dp', 'expert')), may hold values from 0.25 to 1
- grad_out: bfloat16 [8192, 768], P(('dp', 'expert'), 'hidden'), may hold values from -6 to 6
- w_ada: bfloat16 [768, 6, 768], P(None, None, 'hidden'), may hold values from -0.21875 to 0.21875
- w_qkv: bfloat16 [768, 3, 768], P(None, None, 'hidden'), may hold values from -0.21875 to 0.21875
- w_out: bfloat16 [768, 768], P('hidden'), may hold values from -1.25 to 1.25
- w_shared_in: bfloat16 [768, 3072], P(None, 'hidden'), may hold values from -0.21875 to 0.21875
- w_shared_out: bfloat16 [3072, 768], P('hidden'), may hold values from -0.109375 to 0.109375
- w_expert_in: bfloat16 [8, 768, 3072], P('expert', None, 'hidden'), may hold values from -0.21875 to 0.21875
- w_expert_out: bfloat16 [8, 3072, 768], P('expert', 'hidden'), may hold values from -0.109375 to 0.109375
Outputs:
- block_out: bfloat16 [8192, 768], P(('dp', 'expert'), 'hidden')
- grad_patches: bfloat16 [8192, 768], P(('dp', 'expert'), 'hidden')
- grad_ada: float32 [768, 6, 768], P(('dp', 'expert'), None, 'hidden')
- grad_qkv: float32 [768, 3, 768], P(('dp', 'expert'), None, 'hidden')
- grad_proj: float32 [768, 768], P('hidden', ('dp', 'expert'))
- grad_shared_in: float32 [768, 3072], P(('dp', 'expert'), 'hidden')
- grad_shared_out: float32 [3072, 768], P('hidden', ('dp', 'expert'))
- grad_expert_in: float32 [8, 768, 3072], P('expert', 'dp', 'hidden')
- grad_expert_out: float32 [8, 3072, 768], P('expert', 'hidden', 'dp')
Inputs may be any that keep to these rules, and one draw needn't show every extreme that they name: `routes`: within the rows of one device group no expert is named by more than 384 patches, a bound that some block reaches of them. `seg_ids`: along a row the segment number never falls; a segment has 1 to 64 patches. `seg_image`: A value names one of the 32 conditioning vectors of the same device group.
All inputs are finite; a program needn't handle non-finite values.
Results may differ from a plain program's by a relative error of at most 0.014.
The roundings to bfloat16 on the way count: a program that leaves them out, or rounds other values in their place, can miss the bound.
Values may be sent and summed in bfloat16 or wider, within the bound.
No kernel may reach another device: no remote copies, remote signals or barrier semaphores. Data moves between devices by JAX's collectives and lax.ppermute only.
A program may use at most 256 MiB of HBM per device.

v0:
```python
import functools

import jax
import jax.numpy as jnp
from jax import lax
from jax.experimental import pallas as pl
from jax.experimental.pallas import tpu as pltpu
from jax.sharding import PartitionSpec as P


D = 768
HEAD_DIM = 64
EXP_DEV = 4
CAP = 384
EPSILON = 1e-06
NEG_FILL = -1e30
BF = jnp.bfloat16
F32 = jnp.float32
GELU_C = 0.7978845608028654
GELU_A = 0.044715


def kernel_params():
    return pltpu.CompilerParams(vmem_limit_bytes=60 * 1024 * 1024)


def dot(a, b, lhs=1, rhs=0):
    return lax.dot_general(a, b, (((lhs,), (rhs,)), ((), ())), preferred_element_type=F32)


def gelu_pair(values):
    square = values * values
    inner = GELU_C * values * (1.0 + GELU_A * square)
    bent = jnp.tanh(inner)
    half = 0.5 * (1.0 + bent)
    slope = half + (0.5 * values) * (1.0 - bent * bent) * (GELU_C * (1.0 + (3.0 * GELU_A) * square))
    return values * half, slope


def normalize(values):
    centre = values - jnp.mean(values, axis=-1, keepdims=True)
    spread = lax.rsqrt(jnp.mean(centre * centre, axis=-1, keepdims=True) + EPSILON)
    return centre * spread, spread


def norm_back(upstream, unit, spread):
    return spread * (
        upstream
        - jnp.mean(upstream, axis=-1, keepdims=True)
        - unit * jnp.mean(upstream * unit, axis=-1, keepdims=True)
    )


def image_hot(image_col, count):
    lanes = lax.broadcasted_iota(jnp.int32, (image_col.shape[0], count), 1)
    return (image_col == lanes).astype(BF)


def probs_of(queries, keys, same):
    scores = dot(queries, keys, 1, 1) * (HEAD_DIM ** -0.5)
    scores = jnp.where(same, scores, NEG_FILL)
    raised = jnp.exp(scores - jnp.max(scores, axis=-1, keepdims=True))
    return raised * (1.0 / jnp.sum(raised, axis=-1, keepdims=True))


def attn_fwd_kernel(
    x_ref, img_ref, mod_ref, segc_ref, segr_ref, w_ref,
    n1_ref, qkv_ref, ctx_ref, attn_ref, mid_ref, n2_ref,
):
    step = pl.program_id(0)
    feat = ctx_ref.shape[2]
    images = mod_ref.shape[0]

    def mod(k):
        return dot(image_hot(img_ref[...], images), mod_ref[:, k * D:(k + 1) * D])

    @pl.when(step == 0)
    def _():
        unit, _ = normalize(x_ref[...].astype(F32))
        n1_ref[...] = (unit * (1.0 + mod(1)) + mod(0)).astype(BF)
        attn_ref[...] = jnp.zeros_like(attn_ref)

    qkv = dot(n1_ref[...], w_ref[0, :, : 3 * feat]).astype(BF)
    qkv_ref[0] = qkv
    same = segc_ref[...] == segr_ref[...]
    parts = []
    for a in range(feat // HEAD_DIM):
        lo = a * HEAD_DIM
        probs = probs_of(qkv[:, lo:lo + HEAD_DIM], qkv[:, feat + lo:feat + lo + HEAD_DIM], same)
        parts.append(dot(probs.astype(BF), qkv[:, 2 * feat + lo:2 * feat + lo + HEAD_DIM]).astype(BF))
    context = jnp.concatenate(parts, axis=1)
    ctx_ref[0] = context
    attn_ref[...] += dot(context, w_ref[0, :, 3 * feat:], 1, 1)

    @pl.when(step == pl.num_programs(0) - 1)
    def _():
        mid = x_ref[...].astype(F32) + mod(2) * attn_ref[...]
        mid_ref[...] = mid
        unit, _ = normalize(mid)
        n2_ref[...] = (unit * (1.0 + mod(4)) + mod(3)).astype(BF)


def fixed(*shape):
    return pl.BlockSpec(shape, lambda m: (0,) * len(shape))


def stepped(*shape):
    return pl.BlockSpec((1,) + shape, lambda m: (m,) + (0,) * len(shape))


def attn_forward(x_rows, img_col, mod, seg_col, seg_row, weights):
    rows = x_rows.shape[0]
    parts = weights.shape[0]
    feat = D // parts
    return pl.pallas_call(
        attn_fwd_kernel,
        grid=(parts,),
        in_specs=[
            fixed(rows, D), fixed(rows, 1), fixed(*mod.shape), fixed(rows, 1), fixed(1, rows),
            stepped(D, 4 * feat),
        ],
        out_specs=[
            fixed(rows, D), stepped(rows, 3 * feat), stepped(rows, feat),
            fixed(rows, D), fixed(rows, D), fixed(rows, D),
        ],
        out_shape=[
            jax.ShapeDtypeStruct((rows, D), BF),
            jax.ShapeDtypeStruct((parts, rows, 3 * feat), BF),
            jax.ShapeDtypeStruct((parts, rows, feat), BF),
            jax.ShapeDtypeStruct((rows, D), F32),
            jax.ShapeDtypeStruct((rows, D), F32),
            jax.ShapeDtypeStruct((rows, D), BF),
        ],
        compiler_params=kernel_params(),
        name="attn_fwd",
    )(x_rows, img_col, mod, seg_col, seg_row, weights)


def image_sum(hot, values):
    high = values.astype(BF)
    rest = values - high.astype(F32)
    middle = rest.astype(BF)
    low = (rest - middle.astype(F32)).astype(BF)
    return dot(hot, high, 0, 0) + (dot(hot, middle, 0, 0) + dot(hot, low, 0, 0))


def attn_bwd_kernel(
    gn2_ref, mid_ref, attn_ref, go_ref, x_ref, n1_ref, qkv_ref, ctx_ref, img_ref, mod_ref,
    segc_ref, segr_ref, w_ref, core_ref,
    gpatch_ref, gmod_ref, *rest,
):
    grad_refs, (gmid_ref, gattn_ref, gn1_ref) = rest[:-3], rest[-3:]
    step = pl.program_id(0)
    feat = ctx_ref.shape[2]
    images = mod_ref.shape[0]
    scale = HEAD_DIM ** -0.5

    def hot():
        return image_hot(img_ref[...], images)

    def mod(k):
        return dot(hot(), mod_ref[:, k * D:(k + 1) * D])

    @pl.when(step == 0)
    def _():
        unit, spread = normalize(mid_ref[...])
        gn2 = gn2_ref[...]
        gmid = go_ref[...].astype(F32) + norm_back(gn2 * (1.0 + mod(4)), unit, spread)
        gmid_ref[...] = gmid
        gattn_ref[...] = (mod(2) * gmid).astype(BF)
        gmod_ref[2] = image_sum(hot(), gmid * attn_ref[...])
        gmod_ref[3] = image_sum(hot(), gn2)
        gmod_ref[4] = image_sum(hot(), gn2 * unit)
        gn1_ref[...] = jnp.zeros_like(gn1_ref)

    gattn = gattn_ref[...]
    gctx = dot(gattn, w_ref[0, :, 3 * feat:]).astype(BF)
    same = segc_ref[...] == segr_ref[...]
    gq, gk, gv = [], [], []
    for a in range(feat // HEAD_DIM):
        lo = a * HEAD_DIM
        queries = qkv_ref[0, :, lo:lo + HEAD_DIM]
        keys = qkv_ref[0, :, feat + lo:feat + lo + HEAD_DIM]
        values = qkv_ref[0, :, 2 * feat + lo:2 * feat + lo + HEAD_DIM]
        gc = gctx[:, lo:lo + HEAD_DIM]
        probs = probs_of(queries, keys, same)
        gv.append(dot(probs.astype(BF), gc, 0, 0).astype(BF))
        gp = dot(gc, values, 1, 1)
        inner = jnp.sum(probs * gp, axis=-1, keepdims=True)
        gs = (probs * (gp - inner)).astype(BF)
        gq.append((dot(gs, keys) * scale).astype(BF))
        gk.append((dot(gs, queries, 0, 0) * scale).astype(BF))
    grows = jnp.concatenate(gq + gk + gv, axis=1)
    store_rows(grad_refs, core_ref[0], dot(n1_ref[...], grows, 0, 0), slice(0, 3 * feat))
    store_rows(grad_refs, core_ref[0], dot(gattn, ctx_ref[0], 0, 0), slice(3 * feat, 4 * feat))
    gn1_ref[...] += dot(grows, w_ref[0, :, : 3 * feat], 1, 1)

    @pl.when(step == pl.num_programs(0) - 1)
    def _():
        unit, spread = normalize(x_ref[...].astype(F32))
        gn1 = gn1_ref[...]
        back = norm_back(gn1 * (1.0 + mod(1)), unit, spread)
        gpatch_ref[...] = (gmid_ref[...] + back).astype(BF)
        gmod_ref[0] = image_sum(hot(), gn1)
        gmod_ref[1] = image_sum(hot(), gn1 * unit)


def store_rows(refs, core, values, cols):
    if len(refs) == 1:
        refs[0][0, :, cols] = values
        return
    mine, theirs = refs
    pieces, rows = mine.shape[1], mine.shape[2]
    for p in range(pieces):
        low = values[2 * p * rows:(2 * p + 1) * rows]
        high = values[(2 * p + 1) * rows:(2 * p + 2) * rows]
        mine[0, p, :, cols] = jnp.where(core == 0, low, high)
        theirs[0, p, :, cols] = jnp.where(core == 0, high, low)


def row_specs(parts, pieces, width, index):
    rows = D // (2 * pieces)
    if rows % 8:
        shape = (D, width)
        count = 1
    else:
        shape = (pieces, rows, width)
        count = 2
    spec = pl.BlockSpec((1,) + shape, lambda m: (index(m),) + (0,) * len(shape))
    return [spec] * count, [jax.ShapeDtypeStruct((parts,) + shape, F32)] * count


def smem():
    return pl.BlockSpec(memory_space=pltpu.SMEM)


def hbm():
    return pl.BlockSpec(memory_space=pl.ANY)


def fetch(refs, targets, sems):
    copies = [pltpu.make_async_copy(refs[i], targets[i], sems.at[i]) for i in range(len(refs))]
    for copy in copies:
        copy.start()
    for copy in copies:
        copy.wait()


def attn_backward(core, pieces, gn2, mid, attn, go, x_rows, n1, qkv, ctx, img_col, mod, seg_col, seg_row, weights):
    rows = x_rows.shape[0]
    parts = weights.shape[0]
    feat = D // parts
    images = mod.shape[0]
    whole = fixed(rows, D)
    specs, shapes = row_specs(parts, pieces, 4 * feat, lambda m: m)
    return pl.pallas_call(
        attn_bwd_kernel,
        grid=(parts,),
        in_specs=[
            whole, whole, whole, whole, whole, whole,
            stepped(rows, 3 * feat), stepped(rows, feat),
            fixed(rows, 1), fixed(*mod.shape), fixed(rows, 1), fixed(1, rows),
            stepped(D, 4 * feat), smem(),
        ],
        out_specs=[whole, fixed(5, images, D)] + specs,
        out_shape=[
            jax.ShapeDtypeStruct((rows, D), BF),
            jax.ShapeDtypeStruct((5, images, D), F32),
        ] + shapes,
        scratch_shapes=[
            pltpu.VMEM((rows, D), F32), pltpu.VMEM((rows, D), BF), pltpu.VMEM((rows, D), F32),
        ],
        compiler_params=kernel_params(),
        name="attn_bwd",
    )(gn2, mid, attn, go, x_rows, n1, qkv, ctx, img_col, mod, seg_col, seg_row, weights, core)


def finish_kernel(mid_ref, mlp_ref, go_ref, img_ref, gate_ref, out_ref, gmod_ref):
    hot = image_hot(img_ref[...], gate_ref.shape[0])
    mlp = mlp_ref[...]
    out_ref[...] = (mid_ref[...] + dot(hot, gate_ref[...]) * mlp).astype(BF)
    gmod_ref[...] = image_sum(hot, go_ref[...].astype(F32) * mlp)


def finish(mid, mlp, go, img_col, gate):
    return pl.pallas_call(
        finish_kernel,
        out_shape=[
            jax.ShapeDtypeStruct(mid.shape, BF),
            jax.ShapeDtypeStruct(gate.shape, F32),
        ],
        compiler_params=kernel_params(),
        name="finish",
    )(mid, mlp, go, img_col, gate)


def store_split(ref, values):
    pieces, rows = ref.shape[0], ref.shape[2]
    for p in range(pieces):
        ref[p, 0] = values[p * rows:(p + 1) * rows].astype(ref.dtype)


def expert_one_kernel(pos_ref, gate_ref, img_ref, gm_ref, win_ref, *rest, tiles, first, kept):
    pieces_in, rest = rest[:tiles], rest[tiles + 1 + kept:]
    rows_ref, act_ref, slope_ref, gslot_ref, gw_ref, n2_ref, go_ref, sems = rest
    local = first + pl.program_id(0)
    tokens = n2_ref.shape[1]
    images = gm_ref.shape[1]
    each = tiles // 4
    size = tokens // each

    @pl.when(pl.program_id(0) == 0)
    def _():
        targets = [
            ref.at[j, pl.ds(i * size, size)] for ref in (n2_ref, go_ref) for j in range(2) for i in range(each)
        ]
        fetch(pieces_in, targets, sems)

    def block(j, carry):
        where_ = pos_ref[pl.ds(j * EXP_DEV + local, 1), :]
        mask = lax.broadcasted_iota(jnp.int32, (CAP, tokens), 0) == where_
        pick = mask.astype(BF)
        rows = dot(pick, n2_ref[j]).astype(BF)
        slots = pl.ds(pl.multiple_of(j * CAP, CAP), CAP)
        rows_ref[0, slots, :] = rows
        gate = jnp.sum(jnp.where(mask, gate_ref[pl.ds(j * EXP_DEV + local, 1), :], 0.0), axis=1, keepdims=True)
        image = jnp.sum(jnp.where(mask, img_ref[pl.ds(j, 1), :], 0.0), axis=1, keepdims=True)
        hot = image_hot(image.astype(jnp.int32), images)
        grad = dot(hot, gm_ref[j]) * dot(pick, go_ref[j])
        gslot_ref[0, slots, :] = (gate * grad).astype(BF)
        value, slope = gelu_pair(dot(rows, win_ref[0]))
        act_ref[0, slots, :] = value.astype(BF)
        slope_ref[0, slots, :] = slope
        return carry

    lax.fori_loop(0, 2, block, 0)
    store_split(gw_ref, dot(gslot_ref[0], act_ref[0], 0, 0))


def expert_one(pos, gate, img, gate_mlp, w_in, tiles, after, pieces, first, kept):
    tokens = pos.shape[1]
    slots = 2 * CAP
    ff = w_in.shape[2]
    count = EXP_DEV // 2

    def shifted(*shape):
        return pl.BlockSpec((1,) + shape, lambda m: (m + first,) + (0,) * len(shape))

    fixed_ins = 5
    return pl.pallas_call(
        functools.partial(expert_one_kernel, tiles=len(tiles), first=first, kept=len(kept)),
        grid=(count,),
        in_specs=[
            fixed(2 * EXP_DEV, tokens), fixed(2 * EXP_DEV, tokens), fixed(2, tokens),
            fixed(*gate_mlp.shape), shifted(D, ff),
        ] + [hbm()] * (len(tiles) + 1 + len(kept)),
        out_specs=[
            shifted(slots, D), shifted(slots, ff), shifted(slots, ff), shifted(slots, D),
            pl.BlockSpec((pieces, 1, D // pieces, ff), lambda m: (0, m, 0, 0)),
        ],
        out_shape=[
            jax.ShapeDtypeStruct((EXP_DEV, slots, D), BF),
            jax.ShapeDtypeStruct((EXP_DEV, slots, ff), BF),
            jax.ShapeDtypeStruct((EXP_DEV, slots, ff), F32),
            jax.ShapeDtypeStruct((EXP_DEV, slots, D), BF),
            jax.ShapeDtypeStruct((pieces, count, D // pieces, ff), BF),
        ],
        scratch_shapes=[
            pltpu.VMEM((2, tokens, D), BF), pltpu.VMEM((2, tokens, D), BF),
            pltpu.SemaphoreType.DMA((len(tiles),)),
        ],
        input_output_aliases={fixed_ins + len(tiles) + 1 + i: i for i in range(len(kept))},
        compiler_params=kernel_params(),
        name="expert_one",
    )(pos, gate, img, gate_mlp, w_in, *tiles, after, *kept)


def expert_two_kernel(
    pos_ref, gate_ref, rows_ref, act_ref, slope_ref, gslot_ref, win_ref, wout_ref,
    gw_ref, gn_ref, mix_ref, gn_far_ref, mix_far_ref,
    gpre_ref, gn_acc, mix_acc,
):
    local = pl.program_id(0)
    count = pl.num_programs(0)
    tokens = pos_ref.shape[0]
    lanes = lax.broadcasted_iota(jnp.int32, pos_ref.shape, 1)

    @pl.when(local == 0)
    def _():
        for ref in (gn_ref, mix_ref, gn_acc, mix_acc):
            ref[...] = jnp.zeros_like(ref)

    for j, (gn, mix) in enumerate(((gn_ref, mix_ref), (gn_acc, mix_acc))):
        slots = slice(j * CAP, (j + 1) * CAP)
        grad_pre = (slope_ref[0, slots, :] * dot(gslot_ref[0, slots, :], wout_ref[0], 1, 1)).astype(BF)
        gpre_ref[slots, :] = grad_pre
        grad_in = dot(grad_pre, win_ref[0], 1, 1).astype(BF)
        result = dot(act_ref[0, slots, :], wout_ref[0]).astype(BF)
        here = lanes == j * count + local
        where_ = jnp.sum(jnp.where(here, pos_ref[...], 0), axis=1, keepdims=True)
        gate = jnp.sum(jnp.where(here, gate_ref[...], 0.0), axis=1, keepdims=True)
        pick = (lax.broadcasted_iota(jnp.int32, (tokens, CAP), 1) == where_).astype(BF)
        gn[...] += dot(pick, grad_in)
        mix[...] += gate * dot(pick, result)
    store_split(gw_ref, dot(rows_ref[0], gpre_ref[...], 0, 0))

    @pl.when(local == count - 1)
    def _():
        gn_far_ref[...] = gn_acc[...].astype(BF)
        mix_far_ref[...] = mix_acc[...].astype(BF)


def expert_two(pos, gate, rows, act, slope, gslot, w_in, w_out, pieces):
    tokens = pos.shape[0]
    slots = 2 * CAP
    ff = w_in.shape[2]
    whole = fixed(tokens, D)
    return pl.pallas_call(
        expert_two_kernel,
        grid=(EXP_DEV,),
        in_specs=[
            fixed(tokens, 2 * EXP_DEV), fixed(tokens, 2 * EXP_DEV),
            stepped(slots, D), stepped(slots, ff), stepped(slots, ff), stepped(slots, D),
            stepped(D, ff), stepped(ff, D),
        ],
        out_specs=[
            pl.BlockSpec((pieces, 1, D // pieces, ff), lambda m: (0, m, 0, 0)),
            whole, whole, whole, whole,
        ],
        out_shape=[
            jax.ShapeDtypeStruct((pieces, EXP_DEV, D // pieces, ff), BF),
            jax.ShapeDtypeStruct((tokens, D), F32),
            jax.ShapeDtypeStruct((tokens, D), F32),
            jax.ShapeDtypeStruct((tokens, D), BF),
            jax.ShapeDtypeStruct((tokens, D), BF),
        ],
        scratch_shapes=[
            pltpu.VMEM((slots, ff), BF), pltpu.VMEM((tokens, D), F32), pltpu.VMEM((tokens, D), F32),
        ],
        compiler_params=kernel_params(),
        name="expert_two",
    )(pos, gate, rows, act, slope, gslot, w_in, w_out)


def shared_kernel(img_ref, gm_ref, win_ref, wout_ref, core_ref, *rest, tiles):
    pieces_in, out_ref, gn_ref = rest[:tiles], rest[tiles], rest[tiles + 1]
    gw_refs, rest = rest[tiles + 2:-6], rest[-6:]
    n2_ref, go_ref, act_ref, gs_ref, gpre_ref, sems = rest
    step = pl.program_id(0)
    ff = win_ref.shape[1]
    rows = out_ref.shape[0]
    here = pl.ds(pl.multiple_of(step * rows, rows), rows)

    @pl.when(step == 0)
    def _():
        each = tiles // 2
        fetch(pieces_in, [ref.at[pl.ds(i * rows, rows)] for ref in (n2_ref, go_ref) for i in range(each)], sems)

    value, slope = gelu_pair(dot(n2_ref[here, :], win_ref[...]))
    act = value.astype(BF)
    act_ref[here, :] = act
    out_ref[...] = dot(act, wout_ref[...])
    gate = dot(image_hot(img_ref[...], gm_ref.shape[0]), gm_ref[...])
    grad = (gate * go_ref[here, :].astype(F32)).astype(BF)
    gs_ref[here, :] = grad
    gpre = (slope * dot(grad, wout_ref[...], 1, 1)).astype(BF)
    gpre_ref[here, :] = gpre
    gn_ref[...] = dot(gpre, win_ref[...], 1, 1)

    @pl.when(step == pl.num_programs(0) - 1)
    def _():
        store_rows(gw_refs, core_ref[0], dot(n2_ref[...], gpre_ref[...], 0, 0), slice(0, ff))
        store_rows(gw_refs, core_ref[0], dot(gs_ref[...], act_ref[...], 0, 0), slice(ff, 2 * ff))


def shared_both(core, pieces, tiles, img_col, gate_mlp, w_in, w_out):
    rows = tiles[0].shape[0]
    steps = len(tiles) // 2
    tokens = rows * steps
    ff = w_in.shape[1]
    moving = pl.BlockSpec((rows, D), lambda m: (m, 0))
    specs, shapes = row_specs(1, pieces, 2 * ff, lambda m: 0)
    return pl.pallas_call(
        functools.partial(shared_kernel, tiles=len(tiles)),
        grid=(steps,),
        in_specs=[
            pl.BlockSpec((rows, 1), lambda m: (m, 0)),
            fixed(*gate_mlp.shape), fixed(D, ff), fixed(ff, D), smem(),
        ] + [hbm()] * len(tiles),
        out_specs=[moving, moving] + specs,
        out_shape=[
            jax.ShapeDtypeStruct((tokens, D), F32),
            jax.ShapeDtypeStruct((tokens, D), F32),
        ] + shapes,
        scratch_shapes=[
            pltpu.VMEM((tokens, D), BF), pltpu.VMEM((tokens, D), BF),
            pltpu.VMEM((tokens, ff), BF), pltpu.VMEM((tokens, D), BF), pltpu.VMEM((tokens, ff), BF),
            pltpu.SemaphoreType.DMA((len(tiles),)),
        ],
        compiler_params=kernel_params(),
        name="shared_both",
    )(img_col, gate_mlp, w_in, w_out, core, *tiles)


def block(
    patches, cond, seg_ids, seg_image, routes, gates, grad_out,
    w_ada, w_qkv, w_out, w_shared_in, w_shared_out, w_expert_in, w_expert_out,
):
    tokens, feat = patches.shape
    parts = D // feat
    rows = tokens // parts
    image_count = cond.shape[0]
    pieces = lax.axis_size("dp")
    me = lax.axis_index("hidden")
    core = lax.axis_index("expert")
    bit_low = (me & 1) == 1
    bit_high = (me & 2) == 2

    def turned(items):
        a, b, c, d = items
        a, b = jnp.where(bit_low, b, a), jnp.where(bit_low, a, b)
        c, d = jnp.where(bit_low, d, c), jnp.where(bit_low, c, d)
        return [
            jnp.where(bit_high, c, a), jnp.where(bit_high, d, b),
            jnp.where(bit_high, a, c), jnp.where(bit_high, b, d),
        ]

    def across(value, mask):
        return lax.ppermute(value, "hidden", [(i, i ^ mask) for i in range(parts)])

    def other_core(value):
        return lax.ppermute(value, "expert", [(0, 1), (1, 0)])

    def exchanged(items):
        return [items[0]] + [across(items[m], m) for m in range(1, parts)]

    def gathered(value):
        return [value] + [across(value, m) for m in range(1, parts)]

    def blocks(value):
        return [value[i * rows:(i + 1) * rows] for i in range(parts)]

    def to_rows(value):
        return jnp.concatenate(turned(exchanged(turned(blocks(value)))), axis=1)

    def to_cols(value):
        cuts = [value[:, i * feat:(i + 1) * feat] for i in range(parts)]
        return jnp.concatenate(turned(exchanged(turned(cuts))), axis=0)

    packed = jnp.concatenate([w_qkv.reshape(D, 3 * feat), w_out.T], axis=1)
    half = lax.dynamic_slice_in_dim(packed, core * (D // 2), D // 2, axis=0)
    shards = [packed]
    for m in range(1, parts):
        mine = across(half, m)
        theirs = other_core(mine)
        first = core == 0
        shards.append(
            jnp.concatenate([jnp.where(first, mine, theirs), jnp.where(first, theirs, mine)], axis=0)
        )
    weights = jnp.stack(shards)

    x_rows = to_rows(patches)
    silu_cond = jax.nn.silu(cond.astype(F32)).astype(BF)
    mod_own = jnp.einsum("id,dkc->ikc", silu_cond, w_ada, preferred_element_type=F32).astype(BF)
    mod = jnp.concatenate(turned(gathered(mod_own)), axis=2).reshape(image_count, 6 * D)
    gate_own = mod[:, 5 * D:]
    gate_both = jnp.stack([gate_own, other_core(gate_own)])
    go_rows = to_rows(grad_out)
    go_own = gathered(go_rows)
    go_far = [other_core(tile) for tile in go_own]

    seg_turned = jnp.concatenate(turned(jnp.split(seg_ids, parts, axis=0)), axis=0)
    image_turned = jnp.concatenate(turned(jnp.split(seg_image, parts, axis=0)), axis=0)
    seg_hot = seg_turned[:, :, None] == jnp.arange(seg_image.shape[1], dtype=jnp.int32)
    tok_image = jnp.sum(jnp.where(seg_hot, image_turned[:, None, :], 0), axis=2).reshape(tokens)
    routes_turned = jnp.concatenate(turned(blocks(routes)), axis=0).T
    gates_turned = jnp.concatenate(turned(blocks(gates)), axis=0).T
    expert_ids = jnp.arange(2 * EXP_DEV, dtype=jnp.int32)[:, None]
    named = [routes_turned[k][None, :] == expert_ids for k in range(2)]
    hot = named[0] | named[1]
    slot = jnp.cumsum(hot.astype(jnp.int32), axis=1) - 1
    pos_all = jnp.where(hot, slot, -1)
    gate_all = jnp.where(named[0], gates_turned[0][None], jnp.where(named[1], gates_turned[1][None], 0.0))

    def for_experts(table):
        low, high = table[:EXP_DEV], table[EXP_DEV:]
        mine = jnp.where(core == 0, low, high)
        away = jnp.where(core == 0, high, low)
        return mine, away

    pos_mine, pos_away = for_experts(pos_all.astype(F32))
    gate_mine, gate_away = for_experts(gate_all)
    meta = other_core(jnp.concatenate([pos_away, gate_away, tok_image.astype(F32)[None]], axis=0))
    pos = jnp.concatenate([pos_mine, meta[:EXP_DEV]], axis=0).astype(jnp.int32)
    gate_rows = jnp.concatenate([gate_mine, meta[EXP_DEV:2 * EXP_DEV]], axis=0)
    img_rows = jnp.stack([tok_image.astype(F32), meta[2 * EXP_DEV]])
    img_col = tok_image[:, None]
    img_own = img_col[:rows]
    seg_row = seg_turned[:1]
    seg_col = seg_row.reshape(rows, 1)

    n1, qkv, ctx, attn, mid, n2 = attn_forward(x_rows, img_own, mod, seg_col, seg_row, weights)
    n2_own = gathered(n2)
    n2_far = [other_core(tile) for tile in n2_own]

    core_id = core.reshape(1).astype(jnp.int32)
    shared_out, gn_shared, *gw_shared = shared_both(
        core_id, pieces, n2_own + go_own, img_col, gate_own, w_shared_in, w_shared_out
    )

    def core_half(parts_of):
        if len(parts_of) == 1:
            values = parts_of[0]
            cut = values.reshape(values.shape[0], pieces, 2, D // (2 * pieces), values.shape[2])
            low, high = cut[:, :, 0], cut[:, :, 1]
            parts_of = jnp.where(core == 0, low, high), jnp.where(core == 0, high, low)
        return parts_of[0] + other_core(parts_of[1])

    def over_dp(values):
        return lax.psum_scatter(values, "dp", scatter_dimension=0, tiled=False).astype(F32)

    half_shared = core_half(gw_shared)[0].astype(BF)
    grad_shared = over_dp(half_shared)

    tiles = n2_own + n2_far + go_own + go_far
    *kept, gw_out_low = expert_one(
        pos, gate_rows, img_rows, gate_both, w_expert_in, tiles, gn_shared, pieces, 0, []
    )
    ge_out_low = over_dp(gw_out_low)
    *kept, gw_out_high = expert_one(
        pos, gate_rows, img_rows, gate_both, w_expert_in, tiles, gn_shared, pieces, EXP_DEV // 2, kept
    )
    ge_out_high = over_dp(gw_out_high)
    gw_in, gn_near, mix_near, gn_far, mix_far = expert_two(
        pos.T, gate_rows.T, *kept, w_expert_in, w_expert_out, pieces
    )
    grad_expert_in = over_dp(gw_in)

    def row_total(near, far, extra):
        from_core = other_core(far).astype(F32)
        cut = blocks(near + extra + from_core)
        out = cut[0]
        for m in range(1, parts):
            moved = across(cut[m].astype(BF), m)
            out = out + moved.astype(F32)
        return out

    gn2 = row_total(gn_near, gn_far, gn_shared)
    mlp = row_total(mix_near, mix_far, shared_out)

    gpatch, gmod_five, *gw_attn = attn_backward(
        core_id, pieces, gn2, mid, attn, go_rows, x_rows, n1, qkv, ctx, img_own, mod, seg_col, seg_row, weights
    )
    out_rows, gmod_last = finish(mid, mlp, go_rows, img_own, gate_own)
    block_out = to_cols(out_rows)
    grad_patches = to_cols(gpatch)

    gmod = jnp.concatenate([gmod_five, gmod_last[None]], axis=0)
    cuts = turned([gmod[:, :, i * feat:(i + 1) * feat] for i in range(parts)])
    got = exchanged(cuts)
    grad_image = (got[0] + got[1] + got[2] + got[3]).astype(BF)
    ada_rows = D // (2 * pieces)
    place = lax.axis_index("dp") * 2 + core

    def everyone(value):
        if pieces > 8 or pieces & (pieces - 1):
            return lax.all_gather(value, ("dp", "expert"), axis=0, tiled=False)
        pair = jnp.stack([value, other_core(value)])
        pairs = [pair]
        for m in range(1, pieces):
            pairs.append(lax.ppermute(pair, "dp", [(i, i ^ m) for i in range(pieces)]))
        return jnp.concatenate(pairs, axis=0)

    silu_mine = lax.dynamic_slice_in_dim(everyone(silu_cond), place * ada_rows, ada_rows, axis=2)
    grad_ada = jnp.einsum("gid,gkic->dkc", silu_mine, everyone(grad_image), preferred_element_type=F32)

    attn_half = core_half(gw_attn)
    attn_sum = attn_half[0]
    for m in range(1, parts):
        attn_sum = attn_sum + across(attn_half[m].astype(BF), m).astype(F32)
    grad_attn = over_dp(attn_sum.astype(BF))
    ff = w_shared_in.shape[1]
    return (
        block_out,
        grad_patches,
        grad_ada,
        grad_attn[:, : 3 * feat].reshape(ada_rows, 3, feat),
        grad_attn[:, 3 * feat:].T,
        grad_shared[:, :ff],
        grad_shared[:, ff:].T,
        grad_expert_in,
        jnp.swapaxes(jnp.concatenate([ge_out_low, ge_out_high], axis=0), 1, 2),
    )


def solution(mesh):
    rows = P(("dp", "expert"), None)
    tiles = P(("dp", "expert"), "hidden")
    return jax.shard_map(
        block,
        mesh=mesh,
        in_specs=(
            tiles, rows, rows, rows, rows, rows, tiles,
            P(None, None, "hidden"),
            P(None, None, "hidden"),
            P("hidden", None),
            P(None, "hidden"),
            P("hidden", None),
            P("expert", None, "hidden"),
            P("expert", "hidden", None),
        ),
        out_specs=(
            tiles,
            tiles,
            P(("dp", "expert"), None, "hidden"),
            P(("dp", "expert"), None, "hidden"),
            P("hidden", ("dp", "expert")),
            P(("dp", "expert"), "hidden"),
            P("hidden", ("dp", "expert")),
            P("expert", "dp", "hidden"),
            P("expert", "hidden", "dp"),
        ),
        check_vma=False,
    )
```

profile of v0, /device:TPU:8, one launch (start us, length us, event | category | flops | bytes accessed | tf_op | source)
XLA Modules:
  0.0 465.8 jit_solution(7649827857328524973)
XLA Ops:
  16.5 2.4 collective-permute-start.10
  23.7 2.4 collective-permute-start.21
  28.6 8.1 %collective-permute-done.23 = bf16[256,192]{1,0:T(8,128)(2,1)S(1)} collective-permute-done((bf16[256,192]{1,0:T(8,128)(2,1)S(1)}, bf16[256,192]{1,0:T(8,128)(2,1)S(1)}, u32[]{:S(2)}, u32[]{:S(2)}) %collective-permute-start.23) | collective-permute-done | bytes 98336 | tf_op jit(solution)/shard_map/ppermute | solution.py:529
  40.5 9.7 %collective-permute-done.22 = bf16[256,192]{1,0:T(8,128)(2,1)S(1)} collective-permute-done((bf16[256,192]{1,0:T(8,128)(2,1)S(1)}, bf16[256,192]{1,0:T(8,128)(2,1)S(1)}, u32[]{:S(2)}, u32[]{:S(2)}) %collective-permute-start.22) | collective-permute-done | bytes 98336 | tf_op jit(solution)/shard_map/ppermute | solution.py:529
  50.1 2.5 collective-permute-start
  54.9 2.4 collective-permute-done
  60.5 9.6 %collective-permute-done.6 = bf16[384,768]{1,0:T(8,128)(2,1)S(1)} collective-permute-done((bf16[384,768]{1,0:T(8,128)(2,1)}, bf16[384,768]{1,0:T(8,128)(2,1)S(1)}, u32[]{:S(2)}, u32[]{:S(2)}) %collective-permute-start.6) | collective-permute-done | bytes 589856 | tf_op jit(solution)/shard_map/ppermute | solution.py:529
  74.4 2.5 pad_maximum_fusion.w_ref
  76.9 9.5 %attn_fwd.1 = (bf16[256,768]{1,0:T(8,128)(2,1)}, bf16[4,256,576]{2,1,0:T(8,128)(2,1)}, bf16[4,256,192]{2,1,0:T(8,128)(2,1)}, f32[256,768]{1,0:T(8,128)}, f32[256,768]{1,0:T(8,128)}, /*index=5*/bf16[256,768]{1,0:T(8,128)(2,1)}) custom-call(bf16[256,768]{1,0:T(8,128)(2,1)} %pad_maximum_fusion.4.x_ref, s32[256,1]{1,0:T(8,128)} %copy.143.img_ref, ...), custom_call_target="tpu_custom_call" | custom-call | tf_op jit(solution)/shard_map/attn_fwd/pallas_call | solution.py:115
  92.5 7.1 %collective-permute-done.16.rest_3_ = bf16[256,768]{1,0:T(8,128)(2,1)S(1)} collective-permute-done((bf16[256,768]{1,0:T(8,128)(2,1)}, bf16[256,768]{1,0:T(8,128)(2,1)S(1)}, u32[]{:S(2)}, u32[]{:S(2)}) %collective-permute-start.16) | collective-permute-done | bytes 393248 | tf_op jit(solution)/shard_map/ppermute | solution.py:529
  99.6 7.2 %collective-permute-done.15.rest_2_ = bf16[256,768]{1,0:T(8,128)(2,1)S(1)} collective-permute-done((bf16[256,768]{1,0:T(8,128)(2,1)}, bf16[256,768]{1,0:T(8,128)(2,1)S(1)}, u32[]{:S(2)}, u32[]{:S(2)}) %collective-permute-start.15) | collective-permute-done | bytes 393248 | tf_op jit(solution)/shard_map/ppermute | solution.py:529
  107.7 16.2 %shared_both.1 = (f32[1024,768]{1,0:T(8,128)}, f32[1024,768]{1,0:T(8,128)}, f32[1,4,96,1536]{3,2,1,0:T(8,128)}, f32[1,4,96,1536]{3,2,1,0:T(8,128)}) custom-call(s32[1024,1]{1,0:T(8,128)} %bitcast.114, bf16[32,768]{1,0:T(8,128)(2,1)} %get-tuple-element.205.gm_ref.gate_ref, bf16[768,768]{1,0:T(8,128)(2,1)} %win_ref.4, bf16[768,768]{1,0:T(8,128)(2,1)} %wout_ref.2, ...), custom_call_target="tpu_custom_call" | custom-call | tf_op jit(solution)/shard_map/shared_both/pallas_call | solution.py:483
  124.1 2.3 reduce-window.6
  126.8 2.0 collective-permute-done.60
  128.9 3.8 fusion.1
  139.7 1.8 copy.145
  142.8 1.8 copy.146
  149.2 19.8 %expert_one.2 = (bf16[4,768,768]{2,1,0:T(8,128)(2,1)}, bf16[4,768,768]{2,1,0:T(8,128)(2,1)}, f32[4,768,768]{2,1,0:T(8,128)}, bf16[4,768,768]{2,1,0:T(8,128)(2,1)}, bf16[4,2,192,768]{3,2,1,0:T(8,128)(2,1)}) custom-call(s32[8,1024]{1,0:T(8,128)} %maximum_convert_fusion.pos_ref, f32[8,1024]{1,0:T(8,128)} %pad_maximum_fusion.11.gate_ref, ...), custom_call_target="tpu_custom_call" | custom-call | tf_op jit(solution)/shard_map/expert_one/pallas_call | solution.py:350
  169.0 19.2 %expert_one.3 = (bf16[4,768,768]{2,1,0:T(8,128)(2,1)}, bf16[4,768,768]{2,1,0:T(8,128)(2,1)}, f32[4,768,768]{2,1,0:T(8,128)}, bf16[4,768,768]{2,1,0:T(8,128)(2,1)}, bf16[4,2,192,768]{3,2,1,0:T(8,128)(2,1)}) custom-call(s32[8,1024]{1,0:T(8,128)} %maximum_convert_fusion.pos_ref, ...), custom_call_target="tpu_custom_call", output_to_operand_aliasing={{0}: (22, {}), {1}: (23, {}), {2}: (24, {}), {3}: (25, {})} | custom-call | tf_op jit(solution)/shard_map/expert_one/pallas_call | solution.py:350
  188.2 40.9 %expert_two.1 = (bf16[4,4,192,768]{3,2,1,0:T(8,128)(2,1)}, f32[1024,768]{1,0:T(8,128)}, f32[1024,768]{1,0:T(8,128)}, bf16[1024,768]{1,0:T(8,128)(2,1)}, bf16[1024,768]{1,0:T(8,128)(2,1)}) custom-call(s32[1024,8]{1,0:T(8,128)} %bitcast.112, f32[1024,8]{1,0:T(8,128)} %bitcast.113, bf16[4,768,768]{2,1,0:T(8,128)(2,1)} %get-tuple-element.47.rows_ref, ...), custom_call_target="tpu_custom_call" | custom-call | tf_op jit(solution)/shard_map/expert_two/pallas_call | solution.py:418
  229.4 3.5 collective-permute-done.38
  233.0 2.9 fusion.31
  239.6 8.5 %collective-permute-done.39 = bf16[256,768]{1,0:T(8,128)(2,1)S(1)} collective-permute-done((bf16[256,768]{1,0:T(8,128)(2,1)S(1)}, bf16[256,768]{1,0:T(8,128)(2,1)S(1)}, u32[]{:S(2)}, u32[]{:S(2)}) %collective-permute-start.39) | collective-permute-done | bytes 393248 | tf_op jit(solution)/shard_map/ppermute | solution.py:529
  248.1 8.4 %collective-permute-done.41 = bf16[256,768]{1,0:T(8,128)(2,1)S(1)} collective-permute-done((bf16[256,768]{1,0:T(8,128)(2,1)S(1)}, bf16[256,768]{1,0:T(8,128)(2,1)S(1)}, u32[]{:S(2)}, u32[]{:S(2)}) %collective-permute-start.41) | collective-permute-done | bytes 393248 | tf_op jit(solution)/shard_map/ppermute | solution.py:529
  258.9 20.0 %attn_bwd.1 = (bf16[256,768]{1,0:T(8,128)(2,1)}, f32[5,32,768]{2,1,0:T(8,128)}, f32[4,4,96,768]{3,2,1,0:T(8,128)}, f32[4,4,96,768]{3,2,1,0:T(8,128)}) custom-call(f32[256,768]{1,0:T(8,128)} %fusion.7.gn2_ref, f32[256,768]{1,0:T(8,128)} %get-tuple-element.40.mid_ref, f32[256,768]{1,0:T(8,128)} %get-tuple-element.57.attn_ref, bf16[256,768]{1,0:T(8,128)(2,1)} %copy-done.3, ...), custom_call_target="tpu_custom_call" | custom-call | tf_op jit(solution)/shard_map/attn_bwd/pallas_call | solution.py:256
  279.1 8.2 %collective-permute-done.56 = f32[4,4,96,768]{3,2,1,0:T(8,128)} collective-permute-done((f32[4,4,96,768]{3,2,1,0:T(8,128)}, f32[4,4,96,768]{3,2,1,0:T(8,128)}, u32[]{:S(2)}, u32[]{:S(2)}) %collective-permute-start.56) | collective-permute-done | bytes 4718624 | tf_op jit(solution)/shard_map/ppermute | solution.py:532
  287.2 4.6 fusion.26
  292.5 1.7 collective-permute-start.59
  295.5 12.7 %collective-permute-done.57 = bf16[4,96,768]{2,1,0:T(8,128)(2,1)S(1)} collective-permute-done((bf16[4,96,768]{2,1,0:T(8,128)(2,1)S(1)}, bf16[4,96,768]{2,1,0:T(8,128)(2,1)S(1)}, u32[]{:S(2)}, u32[]{:S(2)}) %collective-permute-start.57) | collective-permute-done | bytes 589856 | tf_op jit(solution)/shard_map/ppermute | solution.py:529
  308.2 12.1 %collective-permute-done.59 = bf16[4,96,768]{2,1,0:T(8,128)(2,1)S(1)} collective-permute-done((bf16[4,96,768]{2,1,0:T(8,128)(2,1)S(1)}, bf16[4,96,768]{2,1,0:T(8,128)(2,1)S(1)}, u32[]{:S(2)}, u32[]{:S(2)}) %collective-permute-start.59) | collective-permute-done | bytes 589856 | tf_op jit(solution)/shard_map/ppermute | solution.py:529
  324.0 3.2 collective-permute-done.45
  327.2 1.7 collective-permute-start.48
  328.9 2.5 collective-permute-start.46
  331.4 2.9 fusion.32
  338.1 8.6 %collective-permute-done.47 = bf16[2,32,768]{2,1,0:T(8,128)(2,1)S(1)} collective-permute-done((bf16[2,32,768]{2,1,0:T(8,128)(2,1)S(1)}, bf16[2,32,768]{2,1,0:T(8,128)(2,1)S(1)}, u32[]{:S(2)}, u32[]{:S(2)}) %collective-permute-start.47) | collective-permute-done | bytes 98336 | tf_op jit(solution)/shard_map/ppermute | solution.py:671
  346.8 7.5 %collective-permute-done.34 = bf16[256,768]{1,0:T(8,128)(2,1)S(1)} collective-permute-done((bf16[256,768]{1,0:T(8,128)(2,1)S(1)}, bf16[256,768]{1,0:T(8,128)(2,1)S(1)}, u32[]{:S(2)}, u32[]{:S(2)}) %collective-permute-start.34) | collective-permute-done | bytes 393248 | tf_op jit(solution)/shard_map/ppermute | solution.py:529
  356.8 2.7 finish.1
  361.4 1.7 collective-permute-start.35
  365.1 1.7 collective-permute-start.42
  376.0 2.2 collective-permute-done.43
  378.4 4.1 collective-permute-done.50
  384.1 2.9 collective-permute-start.54
  387.5 24.1 %collective-permute-done.53 = bf16[2,6,32,192]{3,2,1,0:T(8,128)(2,1)S(1)} collective-permute-done((bf16[2,6,32,192]{3,2,1,0:T(8,128)(2,1)S(1)}, bf16[2,6,32,192]{3,2,1,0:T(8,128)(2,1)S(1)}, u32[]{:S(2)}, u32[]{:S(2)}) %collective-permute-start.53) | collective-permute-done | bytes 147488 | tf_op jit(solution)/shard_map/ppermute | solution.py:671
  411.7 8.5 %collective-permute-done.54 = bf16[2,6,32,192]{3,2,1,0:T(8,128)(2,1)S(1)} collective-permute-done((bf16[2,6,32,192]{3,2,1,0:T(8,128)(2,1)S(1)}, bf16[2,6,32,192]{3,2,1,0:T(8,128)(2,1)S(1)}, u32[]{:S(2)}, u32[]{:S(2)}) %collective-permute-start.54) | collective-permute-done | bytes 147488 | tf_op jit(solution)/shard_map/ppermute | solution.py:671
  420.2 2.1 convolution_bitcast_fusion
  424.1 2.8 convert_bitcast_fusion
  429.8 26.4 %reduce-scatter.10.cloned.1.call-done = bf16[1,4,192,768]{3,2,1,0:T(8,128)(2,1)} async-done(((bf16[4,4,192,768]{3,2,1,0:T(8,128)(2,1)}), bf16[1,4,192,768]{3,2,1,0:T(8,128)(2,1)}) %reduce-scatter.10.cloned.1.call-update) | async-done | bytes 1179664 | tf_op jit(solution)/shard_map/reduce_scatter | solution.py:620
  456.2 2.9 bitcast_convert_fusion
  (297 shorter events, 88.5 us)
Async XLA Ops:
  7.2 415.1 %reduce-scatter.8.cloned.1.call-start = ((), (), s32[]{:S(2)}) async-start(), calls=%async_computation.6 | async-start | bytes 1474560 | tf_op jit(solution)/shard_map/reduce_scatter | solution.py:620
  10.2 12.9 %collective-permute-start.5 = (bf16[32,6,192]{2,0,1:T(8,128)(2,1)}, bf16[32,6,192]{2,0,1:T(8,128)(2,1)}, u32[]{:S(2)}, u32[]{:S(2)}) collective-permute-start(bf16[32,6,192]{2,0,1:T(8,128)(2,1)} %convolution_convert_fusion), channel_id=1, source_target_pairs={{0,1},{1,0},{2,3},{3,2},{4,5},{5,4},{6,7},{7,6},{8,9},{9,8},{10,11... | collective-permute-start | bytes 221192 | tf_op jit(solution)/shard_map/ppermute | solution.py:529
  11.6 12.0 %collective-permute-start.4 = (bf16[32,6,192]{2,0,1:T(8,128)(2,1)}, bf16[32,6,192]{2,0,1:T(8,128)(2,1)}, u32[]{:S(2)}, u32[]{:S(2)}) collective-permute-start(bf16[32,6,192]{2,0,1:T(8,128)(2,1)} %convolution_convert_fusion), channel_id=1, source_target_pairs={{0,2},{1,3},{2,0},{3,1},{4,6},{5,7},{6,4},{7,5},{8,10},{9,11},{10,... | collective-permute-start | bytes 221192 | tf_op jit(solution)/shard_map/ppermute | solution.py:529
  13.2 13.0 %collective-permute-start.3 = (bf16[32,6,192]{2,0,1:T(8,128)(2,1)}, bf16[32,6,192]{2,0,1:T(8,128)(2,1)}, u32[]{:S(2)}, u32[]{:S(2)}) collective-permute-start(bf16[32,6,192]{2,0,1:T(8,128)(2,1)} %convolution_convert_fusion), channel_id=1, source_target_pairs={{0,3},{1,2},{2,1},{3,0},{4,7},{5,6},{6,5},{7,4},{8,11},{9,10},{10,... | collective-permute-start | bytes 221192 | tf_op jit(solution)/shard_map/ppermute | solution.py:529
  16.5 42.5 %collective-permute-start.10 = (bf16[384,768]{1,0:T(8,128)(2,1)}, bf16[384,768]{1,0:T(8,128)(2,1)}, u32[]{:S(2)}, u32[]{:S(2)}) collective-permute-start(bf16[384,768]{1,0:T(8,128)(2,1)} %fusion.10), channel_id=1, source_target_pairs={{0,3},{1,2},{2,1},{3,0},{4,7},{5,6},{6,5},{7,4},{8,11},{9,10},{10,... | collective-permute-start | bytes 1769480 | tf_op jit(solution)/shard_map/ppermute | solution.py:529
  18.9 40.1 %collective-permute-start.8 = (bf16[384,768]{1,0:T(8,128)(2,1)}, bf16[384,768]{1,0:T(8,128)(2,1)}, u32[]{:S(2)}, u32[]{:S(2)}) collective-permute-start(bf16[384,768]{1,0:T(8,128)(2,1)} %fusion.10), channel_id=1, source_target_pairs={{0,2},{1,3},{2,0},{3,1},{4,6},{5,7},{6,4},{7,5},{8,10},{9,11},{10,... | collective-permute-start | bytes 1769480 | tf_op jit(solution)/shard_map/ppermute | solution.py:529
  23.1 13.6 %collective-permute-start.23 = (bf16[256,192]{1,0:T(8,128)(2,1)S(1)}, bf16[256,192]{1,0:T(8,128)(2,1)S(1)}, u32[]{:S(2)}, u32[]{:S(2)}) collective-permute-start(bf16[256,192]{1,0:T(8,128)(2,1)S(1)} %get-tuple-element.176), channel_id=1, source_target_pairs={{0,1},{1,0},{2,3},{3,2},{4,5},{5,4},{6,7},{7,6},{8,9},{9,8},{10,11... | collective-permute-start | bytes 294920 | tf_op jit(solution)/shard_map/ppermute | solution.py:529
  23.7 15.3 %collective-permute-start.21 = (bf16[256,192]{1,0:T(8,128)(2,1)S(1)}, bf16[256,192]{1,0:T(8,128)(2,1)S(1)}, u32[]{:S(2)}, u32[]{:S(2)}) collective-permute-start(bf16[256,192]{1,0:T(8,128)(2,1)S(1)} %get-tuple-element.177), channel_id=1, source_target_pairs={{0,3},{1,2},{2,1},{3,0},{4,7},{5,6},{6,5},{7,4},{8,11},{9,10},{10,... | collective-permute-start | bytes 294920 | tf_op jit(solution)/shard_map/ppermute | solution.py:529
  26.1 24.0 %collective-permute-start.22 = (bf16[256,192]{1,0:T(8,128)(2,1)S(1)}, bf16[256,192]{1,0:T(8,128)(2,1)S(1)}, u32[]{:S(2)}, u32[]{:S(2)}) collective-permute-start(bf16[256,192]{1,0:T(8,128)(2,1)S(1)} %get-tuple-element.178), channel_id=1, source_target_pairs={{0,2},{1,3},{2,0},{3,1},{4,6},{5,7},{6,4},{7,5},{8,10},{9,11},{10,... | collective-permute-start | bytes 294920 | tf_op jit(solution)/shard_map/ppermute | solution.py:529
  36.6 16.2 %collective-permute-start.2 = (bf16[256,192]{1,0:T(8,128)(2,1)S(1)}, bf16[256,192]{1,0:T(8,128)(2,1)S(1)}, u32[]{:S(2)}, u32[]{:S(2)}) collective-permute-start(bf16[256,192]{1,0:T(8,128)(2,1)S(1)} %get-tuple-element.179), channel_id=1, source_target_pairs={{0,1},{1,0},{2,3},{3,2},{4,5},{5,4},{6,7},{7,6},{8,9},{9,8},{10,11... | collective-permute-start | bytes 294920 | tf_op jit(solution)/shard_map/ppermute | solution.py:529
  39.0 14.5 %collective-permute-start.1 = (bf16[256,192]{1,0:T(8,128)(2,1)S(1)}, bf16[256,192]{1,0:T(8,128)(2,1)S(1)}, u32[]{:S(2)}, u32[]{:S(2)}) collective-permute-start(bf16[256,192]{1,0:T(8,128)(2,1)S(1)} %get-tuple-element.180), channel_id=1, source_target_pairs={{0,2},{1,3},{2,0},{3,1},{4,6},{5,7},{6,4},{7,5},{8,10},{9,11},{10,... | collective-permute-start | bytes 294920 | tf_op jit(solution)/shard_map/ppermute | solution.py:529
  52.9 17.2 %collective-permute-start.6 = (bf16[384,768]{1,0:T(8,128)(2,1)}, bf16[384,768]{1,0:T(8,128)(2,1)S(1)}, u32[]{:S(2)}, u32[]{:S(2)}) collective-permute-start(bf16[384,768]{1,0:T(8,128)(2,1)} %fusion.10), channel_id=1, source_target_pairs={{0,1},{1,0},{2,3},{3,2},{4,5},{5,4},{6,7},{7,6},{8,9},{9,8},{10,11... | collective-permute-start | bytes 1769480 | tf_op jit(solution)/shard_map/ppermute | solution.py:529
  53.5 35.0 %collective-permute-start.26 = (bf16[256,768]{1,0:T(8,128)(2,1)S(1)}, bf16[256,768]{1,0:T(8,128)(2,1)S(1)}, u32[]{:S(2)}, u32[]{:S(2)}) collective-permute-start(bf16[256,768]{1,0:T(8,128)(2,1)S(1)} %pad_maximum_fusion.5.rest_4_.rest_8_.go_ref), channel_id=1, source_target_pairs={{0,3},{1,2},{2,1},{3,0},{4,7},{5,6},{6,5},{7,4},{8,11},{9,10},{10,... | collective-permute-start | bytes 1179656 | tf_op jit(solution)/shard_map/ppermute | solution.py:529
  57.4 35.1 %collective-permute-start.25 = (bf16[256,768]{1,0:T(8,128)(2,1)S(1)}, bf16[256,768]{1,0:T(8,128)(2,1)S(1)}, u32[]{:S(2)}, u32[]{:S(2)}) collective-permute-start(bf16[256,768]{1,0:T(8,128)(2,1)S(1)} %pad_maximum_fusion.5.rest_4_.rest_8_.go_ref), channel_id=1, source_target_pairs={{0,2},{1,3},{2,0},{3,1},{4,6},{5,7},{6,4},{7,5},{8,10},{9,11},{10,... | collective-permute-start | bytes 1179656 | tf_op jit(solution)/shard_map/ppermute | solution.py:529
  58.9 12.7 %collective-permute-start.11 = (bf16[384,768]{1,0:T(8,128)(2,1)}, bf16[384,768]{1,0:T(8,128)(2,1)S(1)}, u32[]{:S(2)}, u32[]{:S(2)}) collective-permute-start(bf16[384,768]{1,0:T(8,128)(2,1)} %collective-permute-done.10), channel_id=1, source_target_pairs={{0,4},{4,0},{1,5},{5,1},{2,6},{6,2},{3,7},{7,3},{8,12},{12,8},{9,1... | collective-permute-start | bytes 1769480 | tf_op jit(solution)/shard_map/ppermute | solution.py:532
  59.0 13.9 %collective-permute-start.9 = (bf16[384,768]{1,0:T(8,128)(2,1)}, bf16[384,768]{1,0:T(8,128)(2,1)S(1)}, u32[]{:S(2)}, u32[]{:S(2)}) collective-permute-start(bf16[384,768]{1,0:T(8,128)(2,1)} %collective-permute-done.8), channel_id=1, source_target_pairs={{0,4},{4,0},{1,5},{5,1},{2,6},{6,2},{3,7},{7,3},{8,12},{12,8},{9,1... | collective-permute-start | bytes 1769480 | tf_op jit(solution)/shard_map/ppermute | solution.py:532
  70.1 22.4 %collective-permute-start.24 = (bf16[256,768]{1,0:T(8,128)(2,1)S(1)}, bf16[256,768]{1,0:T(8,128)(2,1)S(1)}, u32[]{:S(2)}, u32[]{:S(2)}) collective-permute-start(bf16[256,768]{1,0:T(8,128)(2,1)S(1)} %pad_maximum_fusion.5.rest_4_.rest_8_.go_ref), channel_id=1, source_target_pairs={{0,1},{1,0},{2,3},{3,2},{4,5},{5,4},{6,7},{7,6},{8,9},{9,8},{10,11... | collective-permute-start | bytes 1179656 | tf_op jit(solution)/shard_map/ppermute | solution.py:529
  86.4 13.2 %collective-permute-start.16 = (bf16[256,768]{1,0:T(8,128)(2,1)}, bf16[256,768]{1,0:T(8,128)(2,1)S(1)}, u32[]{:S(2)}, u32[]{:S(2)}) collective-permute-start(bf16[256,768]{1,0:T(8,128)(2,1)} %get-tuple-element.41.rest_0_), channel_id=1, source_target_pairs={{0,3},{1,2},{2,1},{3,0},{4,7},{5,6},{6,5},{7,4},{8,11},{9,10},{10,... | collective-permute-start | bytes 1179656 | tf_op jit(solution)/shard_map/ppermute | solution.py:529
  86.9 19.9 %collective-permute-start.15 = (bf16[256,768]{1,0:T(8,128)(2,1)}, bf16[256,768]{1,0:T(8,128)(2,1)S(1)}, u32[]{:S(2)}, u32[]{:S(2)}) collective-permute-start(bf16[256,768]{1,0:T(8,128)(2,1)} %get-tuple-element.41.rest_0_), channel_id=1, source_target_pairs={{0,2},{1,3},{2,0},{3,1},{4,6},{5,7},{6,4},{7,5},{8,10},{9,11},{10,... | collective-permute-start | bytes 1179656 | tf_op jit(solution)/shard_map/ppermute | solution.py:529
  88.5 18.3 %collective-permute-start.14 = (bf16[256,768]{1,0:T(8,128)(2,1)}, bf16[256,768]{1,0:T(8,128)(2,1)S(1)}, u32[]{:S(2)}, u32[]{:S(2)}) collective-permute-start(bf16[256,768]{1,0:T(8,128)(2,1)} %get-tuple-element.41.rest_0_), channel_id=1, source_target_pairs={{0,1},{1,0},{2,3},{3,2},{4,5},{5,4},{6,7},{7,6},{8,9},{9,8},{10,11... | collective-permute-start | bytes 1179656 | tf_op jit(solution)/shard_map/ppermute | solution.py:529
  132.8 291.4 %reduce-scatter.14.cloned.1.call-start = ((), (), s32[]{:S(2)}) async-start(), calls=%async_computation.9 | async-start | bytes 2949120 | tf_op jit(solution)/shard_map/reduce_scatter | solution.py:620
  137.1 11.1 %collective-permute-start.28 = (bf16[256,768]{1,0:T(8,128)(2,1)S(1)}, bf16[256,768]{1,0:T(8,128)(2,1)}, u32[]{:S(2)}, u32[]{:S(2)}) collective-permute-start(bf16[256,768]{1,0:T(8,128)(2,1)S(1)} %copy-done.10), channel_id=1, source_target_pairs={{0,4},{4,0},{1,5},{5,1},{2,6},{6,2},{3,7},{7,3},{8,12},{12,8},{9,1... | collective-permute-start | bytes 1179656 | tf_op jit(solution)/shard_map/ppermute | solution.py:532
  137.3 10.9 %collective-permute-start.17 = (bf16[256,768]{1,0:T(8,128)(2,1)S(1)}, bf16[256,768]{1,0:T(8,128)(2,1)}, u32[]{:S(2)}, u32[]{:S(2)}) collective-permute-start(bf16[256,768]{1,0:T(8,128)(2,1)S(1)} %copy-done.11), channel_id=1, source_target_pairs={{0,4},{4,0},{1,5},{5,1},{2,6},{6,2},{3,7},{7,3},{8,12},{12,8},{9,1... | collective-permute-start | bytes 1179656 | tf_op jit(solution)/shard_map/ppermute | solution.py:532
  137.7 10.4 %collective-permute-start.20 = (bf16[256,768]{1,0:T(8,128)(2,1)S(1)}, bf16[256,768]{1,0:T(8,128)(2,1)S(1)}, u32[]{:S(2)}, u32[]{:S(2)}) collective-permute-start(bf16[256,768]{1,0:T(8,128)(2,1)S(1)} %copy-done.13), channel_id=1, source_target_pairs={{0,4},{4,0},{1,5},{5,1},{2,6},{6,2},{3,7},{7,3},{8,12},{12,8},{9,1... | collective-permute-start | bytes 1179656 | tf_op jit(solution)/shard_map/ppermute | solution.py:532
  137.9 10.2 %collective-permute-start.19 = (bf16[256,768]{1,0:T(8,128)(2,1)S(1)}, bf16[256,768]{1,0:T(8,128)(2,1)S(1)}, u32[]{:S(2)}, u32[]{:S(2)}) collective-permute-start(bf16[256,768]{1,0:T(8,128)(2,1)S(1)} %copy-done.15), channel_id=1, source_target_pairs={{0,4},{4,0},{1,5},{5,1},{2,6},{6,2},{3,7},{7,3},{8,12},{12,8},{9,1... | collective-permute-start | bytes 1179656 | tf_op jit(solution)/shard_map/ppermute | solution.py:532
  138.4 9.8 %collective-permute-start.18 = (bf16[256,768]{1,0:T(8,128)(2,1)S(1)}, bf16[256,768]{1,0:T(8,128)(2,1)S(1)}, u32[]{:S(2)}, u32[]{:S(2)}) collective-permute-start(bf16[256,768]{1,0:T(8,128)(2,1)S(1)} %copy-done.17), channel_id=1, source_target_pairs={{0,4},{4,0},{1,5},{5,1},{2,6},{6,2},{3,7},{7,3},{8,12},{12,8},{9,1... | collective-permute-start | bytes 1179656 | tf_op jit(solution)/shard_map/ppermute | solution.py:532
  229.4 194.8 %reduce-scatter.12.cloned.1.call-start = ((), (), s32[]{:S(2)}) async-start(), calls=%async_computation.8 | async-start | bytes 2949120 | tf_op jit(solution)/shard_map/reduce_scatter | solution.py:620
  236.0 12.1 %collective-permute-start.39 = (bf16[256,768]{1,0:T(8,128)(2,1)S(1)}, bf16[256,768]{1,0:T(8,128)(2,1)S(1)}, u32[]{:S(2)}, u32[]{:S(2)}) collective-permute-start(bf16[256,768]{1,0:T(8,128)(2,1)S(1)} %get-tuple-element.148), channel_id=1, source_target_pairs={{0,1},{1,0},{2,3},{3,2},{4,5},{5,4},{6,7},{7,6},{8,9},{9,8},{10,11... | collective-permute-start | bytes 1179656 | tf_op jit(solution)/shard_map/ppermute | solution.py:529
  237.3 19.1 %collective-permute-start.41 = (bf16[256,768]{1,0:T(8,128)(2,1)S(1)}, bf16[256,768]{1,0:T(8,128)(2,1)S(1)}, u32[]{:S(2)}, u32[]{:S(2)}) collective-permute-start(bf16[256,768]{1,0:T(8,128)(2,1)S(1)} %get-tuple-element.149), channel_id=1, source_target_pairs={{0,3},{1,2},{2,1},{3,0},{4,7},{5,6},{6,5},{7,4},{8,11},{9,10},{10,... | collective-permute-start | bytes 1179656 | tf_op jit(solution)/shard_map/ppermute | solution.py:529
  238.8 19.0 %collective-permute-start.40 = (bf16[256,768]{1,0:T(8,128)(2,1)S(1)}, bf16[256,768]{1,0:T(8,128)(2,1)S(1)}, u32[]{:S(2)}, u32[]{:S(2)}) collective-permute-start(bf16[256,768]{1,0:T(8,128)(2,1)S(1)} %get-tuple-element.150), channel_id=1, source_target_pairs={{0,2},{1,3},{2,0},{3,1},{4,6},{5,7},{6,4},{7,5},{8,10},{9,11},{10,... | collective-permute-start | bytes 1179656 | tf_op jit(solution)/shard_map/ppermute | solution.py:529
  279.0 147.9 %reduce-scatter.6.cloned.1.call-start = ((), (), s32[]{:S(2)}) async-start(), calls=%async_computation.5 | async-start | bytes 737280 | tf_op jit(solution)/shard_map/reduce_scatter | solution.py:620
  292.0 16.3 %collective-permute-start.57 = (bf16[4,96,768]{2,1,0:T(8,128)(2,1)S(1)}, bf16[4,96,768]{2,1,0:T(8,128)(2,1)S(1)}, u32[]{:S(2)}, u32[]{:S(2)}) collective-permute-start(bf16[4,96,768]{2,1,0:T(8,128)(2,1)S(1)} %get-tuple-element.145), channel_id=1, source_target_pairs={{0,1},{1,0},{2,3},{3,2},{4,5},{5,4},{6,7},{7,6},{8,9},{9,8},{10,11... | collective-permute-start | bytes 1769480 | tf_op jit(solution)/shard_map/ppermute | solution.py:529
  292.5 27.8 %collective-permute-start.59 = (bf16[4,96,768]{2,1,0:T(8,128)(2,1)S(1)}, bf16[4,96,768]{2,1,0:T(8,128)(2,1)S(1)}, u32[]{:S(2)}, u32[]{:S(2)}) collective-permute-start(bf16[4,96,768]{2,1,0:T(8,128)(2,1)S(1)} %get-tuple-element.146), channel_id=1, source_target_pairs={{0,3},{1,2},{2,1},{3,0},{4,7},{5,6},{6,5},{7,4},{8,11},{9,10},{10,... | collective-permute-start | bytes 1769480 | tf_op jit(solution)/shard_map/ppermute | solution.py:529
  294.3 27.5 %collective-permute-start.58 = (bf16[4,96,768]{2,1,0:T(8,128)(2,1)S(1)}, bf16[4,96,768]{2,1,0:T(8,128)(2,1)S(1)}, u32[]{:S(2)}, u32[]{:S(2)}) collective-permute-start(bf16[4,96,768]{2,1,0:T(8,128)(2,1)S(1)} %get-tuple-element.147), channel_id=1, source_target_pairs={{0,2},{1,3},{2,0},{3,1},{4,6},{5,7},{6,4},{7,5},{8,10},{9,11},{10,... | collective-permute-start | bytes 1769480 | tf_op jit(solution)/shard_map/ppermute | solution.py:529
  322.8 133.4 %reduce-scatter.10.cloned.1.call-start = ((), (), s32[]{:S(2)}) async-start(), calls=%async_computation.7 | async-start | bytes 5898240 | tf_op jit(solution)/shard_map/reduce_scatter | solution.py:620
  327.2 19.5 %collective-permute-start.48 = (bf16[2,32,768]{2,1,0:T(8,128)(2,1)S(1)}, bf16[2,32,768]{2,1,0:T(8,128)(2,1)S(1)}, u32[]{:S(2)}, u32[]{:S(2)}) collective-permute-start(bf16[2,32,768]{2,1,0:T(8,128)(2,1)S(1)} %pad_maximum_fusion.9), channel_id=1, source_target_pairs={{0,24},{8,16},{16,8},{24,0},{1,25},{9,17},{17,9},{25,1},{2,26},{10... | collective-permute-start | bytes 294920 | tf_op jit(solution)/shard_map/ppermute | solution.py:671
  328.9 9.1 %collective-permute-start.46 = (bf16[2,32,768]{2,1,0:T(8,128)(2,1)S(1)}, bf16[2,32,768]{2,1,0:T(8,128)(2,1)S(1)}, u32[]{:S(2)}, u32[]{:S(2)}) collective-permute-start(bf16[2,32,768]{2,1,0:T(8,128)(2,1)S(1)} %pad_maximum_fusion.9), channel_id=1, source_target_pairs={{0,8},{8,0},{16,24},{24,16},{1,9},{9,1},{17,25},{25,17},{2,10},{10... | collective-permute-start | bytes 294920 | tf_op jit(solution)/shard_map/ppermute | solution.py:671
  334.4 12.4 %collective-permute-start.32 = (bf16[256,768]{1,0:T(8,128)(2,1)S(1)}, bf16[256,768]{1,0:T(8,128)(2,1)S(1)}, u32[]{:S(2)}, u32[]{:S(2)}) collective-permute-start(bf16[256,768]{1,0:T(8,128)(2,1)S(1)} %get-tuple-element.151), channel_id=1, source_target_pairs={{0,1},{1,0},{2,3},{3,2},{4,5},{5,4},{6,7},{7,6},{8,9},{9,8},{10,11... | collective-permute-start | bytes 1179656 | tf_op jit(solution)/shard_map/ppermute | solution.py:529
  335.8 18.5 %collective-permute-start.34 = (bf16[256,768]{1,0:T(8,128)(2,1)S(1)}, bf16[256,768]{1,0:T(8,128)(2,1)S(1)}, u32[]{:S(2)}, u32[]{:S(2)}) collective-permute-start(bf16[256,768]{1,0:T(8,128)(2,1)S(1)} %get-tuple-element.152), channel_id=1, source_target_pairs={{0,3},{1,2},{2,1},{3,0},{4,7},{5,6},{6,5},{7,4},{8,11},{9,10},{10,... | collective-permute-start | bytes 1179656 | tf_op jit(solution)/shard_map/ppermute | solution.py:529
  337.2 18.5 %collective-permute-start.33 = (bf16[256,768]{1,0:T(8,128)(2,1)S(1)}, bf16[256,768]{1,0:T(8,128)(2,1)S(1)}, u32[]{:S(2)}, u32[]{:S(2)}) collective-permute-start(bf16[256,768]{1,0:T(8,128)(2,1)S(1)} %get-tuple-element.153), channel_id=1, source_target_pairs={{0,2},{1,3},{2,0},{3,1},{4,6},{5,7},{6,4},{7,5},{8,10},{9,11},{10,... | collective-permute-start | bytes 1179656 | tf_op jit(solution)/shard_map/ppermute | solution.py:529
  361.4 8.9 %collective-permute-start.35 = (bf16[256,192]{1,0:T(8,128)(2,1)S(1)}, bf16[256,192]{1,0:T(8,128)(2,1)S(1)}, u32[]{:S(2)}, u32[]{:S(2)}) collective-permute-start(bf16[256,192]{1,0:T(8,128)(2,1)S(1)} %get-tuple-element.188), channel_id=1, source_target_pairs={{0,3},{1,2},{2,1},{3,0},{4,7},{5,6},{6,5},{7,4},{8,11},{9,10},{10,... | collective-permute-start | bytes 294920 | tf_op jit(solution)/shard_map/ppermute | solution.py:529
  364.8 9.4 %collective-permute-start.44 = (bf16[256,192]{1,0:T(8,128)(2,1)S(1)}, bf16[256,192]{1,0:T(8,128)(2,1)S(1)}, u32[]{:S(2)}, u32[]{:S(2)}) collective-permute-start(bf16[256,192]{1,0:T(8,128)(2,1)S(1)} %get-tuple-element.182), channel_id=1, source_target_pairs={{0,1},{1,0},{2,3},{3,2},{4,5},{5,4},{6,7},{7,6},{8,9},{9,8},{10,11... | collective-permute-start | bytes 294920 | tf_op jit(solution)/shard_map/ppermute | solution.py:529
  365.1 10.9 %collective-permute-start.42 = (bf16[256,192]{1,0:T(8,128)(2,1)S(1)}, bf16[256,192]{1,0:T(8,128)(2,1)S(1)}, u32[]{:S(2)}, u32[]{:S(2)}) collective-permute-start(bf16[256,192]{1,0:T(8,128)(2,1)S(1)} %get-tuple-element.183), channel_id=1, source_target_pairs={{0,3},{1,2},{2,1},{3,0},{4,7},{5,6},{6,5},{7,4},{8,11},{9,10},{10,... | collective-permute-start | bytes 294920 | tf_op jit(solution)/shard_map/ppermute | solution.py:529
  367.5 10.7 %collective-permute-start.43 = (bf16[256,192]{1,0:T(8,128)(2,1)S(1)}, bf16[256,192]{1,0:T(8,128)(2,1)S(1)}, u32[]{:S(2)}, u32[]{:S(2)}) collective-permute-start(bf16[256,192]{1,0:T(8,128)(2,1)S(1)} %get-tuple-element.184), channel_id=1, source_target_pairs={{0,2},{1,3},{2,0},{3,1},{4,6},{5,7},{6,4},{7,5},{8,10},{9,11},{10,... | collective-permute-start | bytes 294920 | tf_op jit(solution)/shard_map/ppermute | solution.py:529
  371.9 10.6 %collective-permute-start.50 = (f32[6,32,192]{2,1,0:T(8,128)S(1)}, f32[6,32,192]{2,1,0:T(8,128)S(1)}, u32[]{:S(2)}, u32[]{:S(2)}) collective-permute-start(f32[6,32,192]{2,1,0:T(8,128)S(1)} %get-tuple-element.164), channel_id=1, source_target_pairs={{0,2},{1,3},{2,0},{3,1},{4,6},{5,7},{6,4},{7,5},{8,10},{9,11},{10,... | collective-permute-start | bytes 442376 | tf_op jit(solution)/shard_map/ppermute | solution.py:529
  384.0 36.2 %collective-permute-start.55 = (bf16[2,6,32,192]{3,2,1,0:T(8,128)(2,1)S(1)}, bf16[2,6,32,192]{3,2,1,0:T(8,128)(2,1)S(1)}, u32[]{:S(2)}, u32[]{:S(2)}) collective-permute-start(bf16[2,6,32,192]{3,2,1,0:T(8,128)(2,1)S(1)} %pad_maximum_fusion.7), channel_id=1, source_target_pairs={{0,24},{8,16},{16,8},{24,0},{1,25},{9,17},{17,9},{25,1},{2,26},{10... | collective-permute-start | bytes 442376 | tf_op jit(solution)/shard_map/ppermute | solution.py:671
  384.1 36.1 %collective-permute-start.54 = (bf16[2,6,32,192]{3,2,1,0:T(8,128)(2,1)S(1)}, bf16[2,6,32,192]{3,2,1,0:T(8,128)(2,1)S(1)}, u32[]{:S(2)}, u32[]{:S(2)}) collective-permute-start(bf16[2,6,32,192]{3,2,1,0:T(8,128)(2,1)S(1)} %pad_maximum_fusion.7), channel_id=1, source_target_pairs={{0,16},{8,24},{16,0},{24,8},{1,17},{9,25},{17,1},{25,9},{2,18},{10... | collective-permute-start | bytes 442376 | tf_op jit(solution)/shard_map/ppermute | solution.py:671
  387.0 24.7 %collective-permute-start.53 = (bf16[2,6,32,192]{3,2,1,0:T(8,128)(2,1)S(1)}, bf16[2,6,32,192]{3,2,1,0:T(8,128)(2,1)S(1)}, u32[]{:S(2)}, u32[]{:S(2)}) collective-permute-start(bf16[2,6,32,192]{3,2,1,0:T(8,128)(2,1)S(1)} %pad_maximum_fusion.7), channel_id=1, source_target_pairs={{0,8},{8,0},{16,24},{24,16},{1,9},{9,1},{17,25},{25,17},{2,10},{10... | collective-permute-start | bytes 442376 | tf_op jit(solution)/shard_map/ppermute | solution.py:671
  (63 other events, 491.4 us)
Sparse Core Ops, SparseCore 0:
  132.9 27.2 reduce-scatter.7
  229.5 47.0 reduce-scatter.13
  279.5 47.0 reduce-scatter.11
  328.7 22.8 reduce-scatter.5
  353.7 102.3 reduce-scatter.9
where the time goes:
time: 475 us; the launch traced here: 466 us
  waiting for transfers between devices  194 us (41%)
  Pallas kernels  128 us (27%)
  starting transfers between devices  58 us (12%)
  other arithmetic  46.3 us (10%)
  local copies, waits for them, and re-layouts  21.2 us (4%)
  between operations  15 us (3%)
    ppermute x36, waiting for transfers between devices, across(): return lax.ppermute(value, 'hidden', [(i, i ^ mask) for i in range(parts)])  107 us
    ppermute x36, starting transfers between devices, across(): return lax.ppermute(value, 'hidden', [(i, i ^ mask) for i in range(parts)])  45.5 us
    ppermute x6, waiting for transfers between devices, everyone(): pairs.append(lax.ppermute(pair, 'dp', [(i, i ^ m) for i in range(pieces)]))  41.2 us
    pallas_call x1, Pallas kernels, expert_two(): pl.pallas_call(expert_two_kernel, grid=(EXP_DEV,), in_specs=[fixed(tokens...  40.9 us
    pallas_call x2, Pallas kernels, expert_one(): pl.pallas_call(functools.partial(expert_one_kernel, tiles=len(tiles), fir...  39 us
    reduce_scatter x5, waiting for transfers between devices, over_dp(): lax.psum_scatter(values, 'dp', scatter_dimension=0, tiled=False).astype(F32)  26.4 us
    pallas_call x1, Pallas kernels, attn_backward(): pl.pallas_call(attn_bwd_kernel, grid=(parts,), in_specs=[whole, whole, wh...  20 us
    ppermute x19, waiting for transfers between devices, other_core(): return lax.ppermute(value, 'expert', [(0, 1), (1, 0)])  18.5 us
  transfers between devices with their start and end apart: 66, of which 32 were waited for; matrix products, arithmetic and copies ran while one was open for 12% of the time, Pallas kernels for 24%

commit v1 on v0

--- a/solution.py
+++ b/solution.py
@@ -64,10 +64,12 @@
 
 
 def attn_fwd_kernel(
-    x_ref, img_ref, mod_ref, segc_ref, segr_ref, w_ref,
-    n1_ref, qkv_ref, ctx_ref, attn_ref, mid_ref, n2_ref,
+    x_ref, img_ref, mod_ref, segc_ref, segr_ref, core_ref, *rest, shards, extras,
 ):
+    w_in, rest = rest[:shards], rest[shards + extras:]
+    n1_ref, qkv_ref, ctx_ref, attn_ref, mid_ref, n2_ref, w_ref, sems = rest
     step = pl.program_id(0)
+    fetch_weights(w_in, w_ref, core_ref[0], sems)
     feat = ctx_ref.shape[2]
     images = mod_ref.shape[0]
 
@@ -80,7 +82,7 @@
         n1_ref[...] = (unit * (1.0 + mod(1)) + mod(0)).astype(BF)
         attn_ref[...] = jnp.zeros_like(attn_ref)
 
-    qkv = dot(n1_ref[...], w_ref[0, :, : 3 * feat]).astype(BF)
+    qkv = dot(n1_ref[...], w_ref[step, :, : 3 * feat]).astype(BF)
     qkv_ref[0] = qkv
     same = segc_ref[...] == segr_ref[...]
     parts = []
@@ -90,7 +92,7 @@
         parts.append(dot(probs.astype(BF), qkv[:, 2 * feat + lo:2 * feat + lo + HEAD_DIM]).astype(BF))
     context = jnp.concatenate(parts, axis=1)
     ctx_ref[0] = context
-    attn_ref[...] += dot(context, w_ref[0, :, 3 * feat:], 1, 1)
+    attn_ref[...] += dot(context, w_ref[step, :, 3 * feat:], 1, 1)
 
     @pl.when(step == pl.num_programs(0) - 1)
     def _():
@@ -108,17 +110,15 @@
     return pl.BlockSpec((1,) + shape, lambda m: (m,) + (0,) * len(shape))
 
 
-def attn_forward(x_rows, img_col, mod, seg_col, seg_row, weights):
+def attn_forward(core, x_rows, img_col, mod, seg_col, seg_row, weights, extras, parts):
     rows = x_rows.shape[0]
-    parts = weights.shape[0]
     feat = D // parts
     return pl.pallas_call(
-        attn_fwd_kernel,
+        functools.partial(attn_fwd_kernel, shards=len(weights), extras=len(extras)),
         grid=(parts,),
         in_specs=[
-            fixed(rows, D), fixed(rows, 1), fixed(*mod.shape), fixed(rows, 1), fixed(1, rows),
-            stepped(D, 4 * feat),
-        ],
+            fixed(rows, D), fixed(rows, 1), fixed(*mod.shape), fixed(rows, 1), fixed(1, rows), smem(),
+        ] + [hbm()] * (len(weights) + len(extras)),
         out_specs=[
             fixed(rows, D), stepped(rows, 3 * feat), stepped(rows, feat),
             fixed(rows, D), fixed(rows, D), fixed(rows, D),
@@ -131,9 +131,10 @@
             jax.ShapeDtypeStruct((rows, D), F32),
             jax.ShapeDtypeStruct((rows, D), BF),
         ],
+        scratch_shapes=[pltpu.VMEM((parts, D, 4 * feat), BF), pltpu.SemaphoreType.DMA((len(weights),))],
         compiler_params=kernel_params(),
         name="attn_fwd",
-    )(x_rows, img_col, mod, seg_col, seg_row, weights)
+    )(x_rows, img_col, mod, seg_col, seg_row, core, *weights, *extras)
 
 
 def image_sum(hot, values):
@@ -146,11 +147,12 @@
 
 def attn_bwd_kernel(
     gn2_ref, mid_ref, attn_ref, go_ref, x_ref, n1_ref, qkv_ref, ctx_ref, img_ref, mod_ref,
-    segc_ref, segr_ref, w_ref, core_ref,
-    gpatch_ref, gmod_ref, *rest,
+    segc_ref, segr_ref, core_ref, *rest, shards,
 ):
-    grad_refs, (gmid_ref, gattn_ref, gn1_ref) = rest[:-3], rest[-3:]
+    w_in, (gpatch_ref, gmod_ref), rest = rest[:shards], rest[shards:shards + 2], rest[shards + 2:]
+    grad_refs, (gmid_ref, gattn_ref, gn1_ref, w_ref, sems) = rest[:-5], rest[-5:]
     step = pl.program_id(0)
+    fetch_weights(w_in, w_ref, core_ref[0], sems)
     feat = ctx_ref.shape[2]
     images = mod_ref.shape[0]
     scale = HEAD_DIM ** -0.5
@@ -174,7 +176,7 @@
         gn1_ref[...] = jnp.zeros_like(gn1_ref)
 
     gattn = gattn_ref[...]
-    gctx = dot(gattn, w_ref[0, :, 3 * feat:]).astype(BF)
+    gctx = dot(gattn, w_ref[step, :, 3 * feat:]).astype(BF)
     same = segc_ref[...] == segr_ref[...]
     gq, gk, gv = [], [], []
     for a in range(feat // HEAD_DIM):
@@ -191,9 +193,9 @@
         gq.append((dot(gs, keys) * scale).astype(BF))
         gk.append((dot(gs, queries, 0, 0) * scale).astype(BF))
     grows = jnp.concatenate(gq + gk + gv, axis=1)
-    store_rows(grad_refs, core_ref[0], dot(n1_ref[...], grows, 0, 0), slice(0, 3 * feat))
-    store_rows(grad_refs, core_ref[0], dot(gattn, ctx_ref[0], 0, 0), slice(3 * feat, 4 * feat))
-    gn1_ref[...] += dot(grows, w_ref[0, :, : 3 * feat], 1, 1)
+    store_rows(grad_refs, core_ref, dot(n1_ref[...], grows, 0, 0), slice(0, 3 * feat))
+    store_rows(grad_refs, core_ref, dot(gattn, ctx_ref[0], 0, 0), slice(3 * feat, 4 * feat))
+    gn1_ref[...] += dot(grows, w_ref[step, :, : 3 * feat], 1, 1)
 
     @pl.when(step == pl.num_programs(0) - 1)
     def _():
@@ -205,7 +207,7 @@
         gmod_ref[1] = image_sum(hot(), gn1 * unit)
 
 
-def store_rows(refs, core, values, cols):
+def store_rows(refs, core_ref, values, cols):
     if len(refs) == 1:
         refs[0][0, :, cols] = values
         return
@@ -214,8 +216,8 @@
     for p in range(pieces):
         low = values[2 * p * rows:(2 * p + 1) * rows]
         high = values[(2 * p + 1) * rows:(2 * p + 2) * rows]
-        mine[0, p, :, cols] = jnp.where(core == 0, low, high)
-        theirs[0, p, :, cols] = jnp.where(core == 0, high, low)
+        mine[0, p ^ core_ref[1], :, cols] = jnp.where(core_ref[0] == 0, low, high)
+        theirs[0, p ^ core_ref[1], :, cols] = jnp.where(core_ref[0] == 0, high, low)
 
 
 def row_specs(parts, pieces, width, index):
@@ -246,22 +248,60 @@
         copy.wait()
 
 
+def laid_out(refs, target):
+    places, start = [], 0
+    for ref in refs:
+        places.append(target.at[pl.ds(start, ref.shape[0])])
+        start += ref.shape[0]
+    return places
+
+
+def weight_copies(refs, w_ref, core, sems):
+    half = D // 2
+    mine = pl.multiple_of(core * half, half)
+    theirs = pl.multiple_of((1 - core) * half, half)
+    places = [(0, w_ref.at[0])]
+    for base in (mine, theirs):
+        for m in (1, 2):
+            places.append((m, w_ref.at[m, pl.ds(base, half)]))
+        for k in (0, 1):
+            places.append((3, w_ref.at[3, pl.ds(pl.multiple_of(base + k * (half // 2), half // 2), half // 2)]))
+    return [(m, pltpu.make_async_copy(ref, place, sems.at[i])) for i, (ref, (m, place)) in enumerate(zip(refs, places))]
+
+
+def fetch_weights(refs, w_ref, core, sems):
+    step = pl.program_id(0)
+    copies = weight_copies(refs, w_ref, core, sems)
+
+    @pl.when(step == 0)
+    def _():
+        for _, copy in copies:
+            copy.start()
+
+    for shard in range(w_ref.shape[0]):
+        @pl.when(step == shard)
+        def _():
+            for m, copy in copies:
+                if m == shard:
+                    copy.wait()
+
+
 def attn_backward(core, pieces, gn2, mid, attn, go, x_rows, n1, qkv, ctx, img_col, mod, seg_col, seg_row, weights):
     rows = x_rows.shape[0]
-    parts = weights.shape[0]
+    parts = qkv.shape[0]
     feat = D // parts
     images = mod.shape[0]
     whole = fixed(rows, D)
     specs, shapes = row_specs(parts, pieces, 4 * feat, lambda m: m)
     return pl.pallas_call(
-        attn_bwd_kernel,
+        functools.partial(attn_bwd_kernel, shards=len(weights)),
         grid=(parts,),
         in_specs=[
             whole, whole, whole, whole, whole, whole,
             stepped(rows, 3 * feat), stepped(rows, feat),
             fixed(rows, 1), fixed(*mod.shape), fixed(rows, 1), fixed(1, rows),
-            stepped(D, 4 * feat), smem(),
-        ],
+            smem(),
+        ] + [hbm()] * len(weights),
         out_specs=[whole, fixed(5, images, D)] + specs,
         out_shape=[
             jax.ShapeDtypeStruct((rows, D), BF),
@@ -269,10 +309,11 @@
         ] + shapes,
         scratch_shapes=[
             pltpu.VMEM((rows, D), F32), pltpu.VMEM((rows, D), BF), pltpu.VMEM((rows, D), F32),
+            pltpu.VMEM((parts, D, 4 * feat), BF), pltpu.SemaphoreType.DMA((len(weights),)),
         ],
         compiler_params=kernel_params(),
         name="attn_bwd",
-    )(gn2, mid, attn, go, x_rows, n1, qkv, ctx, img_col, mod, seg_col, seg_row, weights, core)
+    )(gn2, mid, attn, go, x_rows, n1, qkv, ctx, img_col, mod, seg_col, seg_row, core, *weights)
 
 
 def finish_kernel(mid_ref, mlp_ref, go_ref, img_ref, gate_ref, out_ref, gmod_ref):
@@ -307,13 +348,12 @@
     tokens = n2_ref.shape[1]
     images = gm_ref.shape[1]
     each = tiles // 4
-    size = tokens // each
 
     @pl.when(pl.program_id(0) == 0)
     def _():
-        targets = [
-            ref.at[j, pl.ds(i * size, size)] for ref in (n2_ref, go_ref) for j in range(2) for i in range(each)
-        ]
+        targets = []
+        for i, (ref, j) in enumerate(((n2_ref, 0), (n2_ref, 1), (go_ref, 0), (go_ref, 1))):
+            targets += laid_out(pieces_in[i * each:(i + 1) * each], ref.at[j])
         fetch(pieces_in, targets, sems)
 
     def block(j, carry):
@@ -454,7 +494,7 @@
     @pl.when(step == 0)
     def _():
         each = tiles // 2
-        fetch(pieces_in, [ref.at[pl.ds(i * rows, rows)] for ref in (n2_ref, go_ref) for i in range(each)], sems)
+        fetch(pieces_in, laid_out(pieces_in[:each], n2_ref) + laid_out(pieces_in[each:], go_ref), sems)
 
     value, slope = gelu_pair(dot(n2_ref[here, :], win_ref[...]))
     act = value.astype(BF)
@@ -469,14 +509,14 @@
 
     @pl.when(step == pl.num_programs(0) - 1)
     def _():
-        store_rows(gw_refs, core_ref[0], dot(n2_ref[...], gpre_ref[...], 0, 0), slice(0, ff))
-        store_rows(gw_refs, core_ref[0], dot(gs_ref[...], act_ref[...], 0, 0), slice(ff, 2 * ff))
+        store_rows(gw_refs, core_ref, dot(n2_ref[...], gpre_ref[...], 0, 0), slice(0, ff))
+        store_rows(gw_refs, core_ref, dot(gs_ref[...], act_ref[...], 0, 0), slice(ff, 2 * ff))
 
 
 def shared_both(core, pieces, tiles, img_col, gate_mlp, w_in, w_out):
     rows = tiles[0].shape[0]
-    steps = len(tiles) // 2
-    tokens = rows * steps
+    tokens = img_col.shape[0]
+    steps = tokens // rows
     ff = w_in.shape[1]
     moving = pl.BlockSpec((rows, D), lambda m: (m, 0))
     specs, shapes = row_specs(1, pieces, 2 * ff, lambda m: 0)
@@ -537,6 +577,11 @@
     def gathered(value):
         return [value] + [across(value, m) for m in range(1, parts)]
 
+    def passed_on(value):
+        one, two = across(value, 1), across(value, 2)
+        cut = value.shape[0] // 2
+        return [one, two, across(one[:cut], 2), across(two[cut:], 1)]
+
     def blocks(value):
         return [value[i * rows:(i + 1) * rows] for i in range(parts)]
 
@@ -549,15 +594,10 @@
 
     packed = jnp.concatenate([w_qkv.reshape(D, 3 * feat), w_out.T], axis=1)
     half = lax.dynamic_slice_in_dim(packed, core * (D // 2), D // 2, axis=0)
-    shards = [packed]
-    for m in range(1, parts):
-        mine = across(half, m)
-        theirs = other_core(mine)
-        first = core == 0
-        shards.append(
-            jnp.concatenate([jnp.where(first, mine, theirs), jnp.where(first, theirs, mine)], axis=0)
-        )
-    weights = jnp.stack(shards)
+    halves = passed_on(half)
+    weights = [packed] + halves + [other_core(part) for part in halves]
+    flip = lax.axis_index("dp") if pieces == 4 else jnp.zeros((), jnp.int32)
+    core_id = jnp.stack([core, flip]).astype(jnp.int32)
 
     x_rows = to_rows(patches)
     silu_cond = jax.nn.silu(cond.astype(F32)).astype(BF)
@@ -566,7 +606,7 @@
     gate_own = mod[:, 5 * D:]
     gate_both = jnp.stack([gate_own, other_core(gate_own)])
     go_rows = to_rows(grad_out)
-    go_own = gathered(go_rows)
+    go_own = [go_rows] + passed_on(go_rows)
     go_far = [other_core(tile) for tile in go_own]
 
     seg_turned = jnp.concatenate(turned(jnp.split(seg_ids, parts, axis=0)), axis=0)
@@ -599,11 +639,27 @@
     seg_row = seg_turned[:1]
     seg_col = seg_row.reshape(rows, 1)
 
-    n1, qkv, ctx, attn, mid, n2 = attn_forward(x_rows, img_own, mod, seg_col, seg_row, weights)
-    n2_own = gathered(n2)
+    ada_rows = D // (2 * pieces)
+    place = lax.axis_index("dp") * 2 + core
+
+    def everyone(value):
+        if pieces > 8 or pieces & (pieces - 1):
+            return lax.all_gather(value, ("dp", "expert"), axis=0, tiled=False)
+        own = [value]
+        for m in range(1, pieces):
+            own.append(lax.ppermute(value, "dp", [(i, i ^ m) for i in range(pieces)]))
+        own = jnp.stack(own)
+        return jnp.concatenate([own, other_core(own)], axis=0)
+
+    silu_mine = lax.dynamic_slice_in_dim(everyone(silu_cond), place * ada_rows, ada_rows, axis=2)
+    pos_cols, gate_cols = pos.T, gate_rows.T
+    n1, qkv, ctx, attn, mid, n2 = attn_forward(
+        core_id, x_rows, img_own, mod, seg_col, seg_row, weights,
+        [pos, gate_rows, img_rows, pos_cols, gate_cols, gate_both, img_col, silu_mine], parts,
+    )
+    n2_own = [n2] + passed_on(n2)
     n2_far = [other_core(tile) for tile in n2_own]
 
-    core_id = core.reshape(1).astype(jnp.int32)
     shared_out, gn_shared, *gw_shared = shared_both(
         core_id, pieces, n2_own + go_own, img_col, gate_own, w_shared_in, w_shared_out
     )
@@ -619,20 +675,27 @@
     def over_dp(values):
         return lax.psum_scatter(values, "dp", scatter_dimension=0, tiled=False).astype(F32)
 
-    half_shared = core_half(gw_shared)[0].astype(BF)
-    grad_shared = over_dp(half_shared)
+    def pieces_over_dp(values):
+        if pieces != 4:
+            return over_dp(values.astype(BF))
+        total = values[0]
+        for m in range(1, pieces):
+            moved = lax.ppermute(values[m].astype(BF), "dp", [(i, i ^ m) for i in range(pieces)])
+            total = total + moved.astype(F32)
+        return total
+
+    half_shared = core_half(gw_shared)[0]
+    grad_shared = pieces_over_dp(half_shared)
 
     tiles = n2_own + n2_far + go_own + go_far
-    *kept, gw_out_low = expert_one(
-        pos, gate_rows, img_rows, gate_both, w_expert_in, tiles, gn_shared, pieces, 0, []
-    )
+    *kept, gw_out_low = expert_one(pos, gate_rows, img_rows, gate_both, w_expert_in, tiles, gn_shared, pieces, 0, [])
     ge_out_low = over_dp(gw_out_low)
     *kept, gw_out_high = expert_one(
         pos, gate_rows, img_rows, gate_both, w_expert_in, tiles, gn_shared, pieces, EXP_DEV // 2, kept
     )
     ge_out_high = over_dp(gw_out_high)
     gw_in, gn_near, mix_near, gn_far, mix_far = expert_two(
-        pos.T, gate_rows.T, *kept, w_expert_in, w_expert_out, pieces
+        pos_cols, gate_cols, *kept, w_expert_in, w_expert_out, pieces
     )
     grad_expert_in = over_dp(gw_in)
 
@@ -659,26 +722,15 @@
     cuts = turned([gmod[:, :, i * feat:(i + 1) * feat] for i in range(parts)])
     got = exchanged(cuts)
     grad_image = (got[0] + got[1] + got[2] + got[3]).astype(BF)
-    ada_rows = D // (2 * pieces)
-    place = lax.axis_index("dp") * 2 + core
-
-    def everyone(value):
-        if pieces > 8 or pieces & (pieces - 1):
-            return lax.all_gather(value, ("dp", "expert"), axis=0, tiled=False)
-        pair = jnp.stack([value, other_core(value)])
-        pairs = [pair]
-        for m in range(1, pieces):
-            pairs.append(lax.ppermute(pair, "dp", [(i, i ^ m) for i in range(pieces)]))
-        return jnp.concatenate(pairs, axis=0)
-
-    silu_mine = lax.dynamic_slice_in_dim(everyone(silu_cond), place * ada_rows, ada_rows, axis=2)
-    grad_ada = jnp.einsum("gid,gkic->dkc", silu_mine, everyone(grad_image), preferred_element_type=F32)
+    image_all = everyone(grad_image)
+    grad_ada = jnp.einsum("gid,gkic->dkc", silu_mine, image_all, preferred_element_type=F32)
 
     attn_half = core_half(gw_attn)
     attn_sum = attn_half[0]
     for m in range(1, parts):
-        attn_sum = attn_sum + across(attn_half[m].astype(BF), m).astype(F32)
-    grad_attn = over_dp(attn_sum.astype(BF))
+        moved = across(attn_half[m].astype(BF), m)
+        attn_sum = attn_sum + moved.astype(F32)
+    grad_attn = pieces_over_dp(attn_sum)
     ff = w_shared_in.shape[1]
     return (
         block_out,

time: 475 us -> 434 us (0.914)
  the two profiles are of different devices: /device:TPU:8 before, /device:TPU:0 now
where the time goes in v1:
time: 434 us; the launch traced here: 426 us
  waiting for transfers between devices  144 us (33%)
  Pallas kernels  132 us (30%)
  starting transfers between devices  66.4 us (15%)
  other arithmetic  43.8 us (10%)
  local copies, waits for them, and re-layouts  23 us (5%)
  between operations  15.1 us (3%)
    ppermute x39, waiting for transfers between devices, across(): return lax.ppermute(value, 'hidden', [(i, i ^ mask) for i in range(parts)])  78.4 us
    ppermute x6, waiting for transfers between devices, pieces_over_dp(): lax.ppermute(values[m].astype(BF), 'dp', [(i, i ^ m) for i in range(piece...  52.8 us
    ppermute x39, starting transfers between devices, across(): return lax.ppermute(value, 'hidden', [(i, i ^ mask) for i in range(parts)])  45.7 us
    pallas_call x1, Pallas kernels, expert_two(): pl.pallas_call(expert_two_kernel, grid=(EXP_DEV,), in_specs=[fixed(tokens...  40.8 us
    pallas_call x2, Pallas kernels, expert_one(): pl.pallas_call(functools.partial(expert_one_kernel, tiles=len(tiles), fir...  39.1 us
    pallas_call x1, Pallas kernels, attn_backward(): pl.pallas_call(functools.partial(attn_bwd_kernel, shards=len(weights)), g...  21.6 us
    pallas_call x1, Pallas kernels, shared_both(): pl.pallas_call(functools.partial(shared_kernel, tiles=len(tiles)), grid=(...  16.8 us
    another operation x7, other arithmetic  14.6 us
  transfers between devices with their start and end apart: 76, of which 35 were waited for; matrix products, arithmetic and copies ran while one was open for 15% of the time, Pallas kernels for 22%

profile of v1, /device:TPU:0, one launch (start us, length us, event | category | flops | bytes accessed | tf_op | source)
XLA Modules:
  0.0 426.3 jit_solution(9813735085128756921)
XLA Ops:
  8.9 5.1 %collective-permute-start.18 = (bf16[32,768]{1,0:T(8,128)(2,1)S(1)}, bf16[32,768]{1,0:T(8,128)(2,1)}, u32[]{:S(2)}, u32[]{:S(2)}) collective-permute-start(bf16[32,768]{1,0:T(8,128)(2,1)S(1)} %get-tuple-element.144), channel_id=1, source_target_pairs={{0,24},{8,16},{16,8},{24,0},{1,25},{9,17},{17,9},{25,1},{2,26},{10... | collective-permute-start | bytes 147464 | tf_op jit(solution)/shard_map/ppermute | solution.py:650
  17.9 2.3 reduce-window.6
  22.7 1.7 collective-permute-start.5
  40.7 1.7 collective-permute-start.7
  52.5 10.3 %collective-permute-done.31 = bf16[256,192]{1,0:T(8,128)(2,1)S(1)} collective-permute-done((bf16[256,192]{1,0:T(8,128)(2,1)}, bf16[256,192]{1,0:T(8,128)(2,1)S(1)}, u32[]{:S(2)}, u32[]{:S(2)}) %collective-permute-start.31) | collective-permute-done | bytes 98336 | tf_op jit(solution)/shard_map/ppermute | solution.py:569
  65.4 1.7 collective-permute-start.1
  70.6 3.1 collective-permute-done
  78.3 2.4 collective-permute-done.8.rest_3_
  80.7 1.8 collective-permute-start.32
  86.0 10.6 %attn_fwd.1 = (bf16[256,768]{1,0:T(8,128)(2,1)}, bf16[4,256,576]{2,1,0:T(8,128)(2,1)}, bf16[4,256,192]{2,1,0:T(8,128)(2,1)}, f32[256,768]{1,0:T(8,128)}, f32[256,768]{1,0:T(8,128)}, /*index=5*/bf16[256,768]{1,0:T(8,128)(2,1)}) custom-call(bf16[256,768]{1,0:T(8,128)(2,1)} %pad_maximum_fusion.3.x_ref, s32[256,1]{1,0:T(8,128)} %copy.156.img_ref, ...), custom_call_target="tpu_custom_call" | custom-call | tf_op jit(solution)/shard_map/attn_fwd/pallas_call | solution.py:116
  96.6 1.7 collective-permute-start.21
  100.9 5.2 %collective-permute-done.35.rest_9_.rest_14_ = bf16[128,768]{1,0:T(8,128)(2,1)S(1)} collective-permute-done((bf16[128,768]{1,0:T(8,128)(2,1)S(1)}, bf16[128,768]{1,0:T(8,128)(2,1)S(1)}, u32[]{:S(2)}, u32[]{:S(2)}) %collective-permute-start.35) | collective-permute-done | bytes 196640 | tf_op jit(solution)/shard_map/ppermute | solution.py:569
  106.1 6.4 %collective-permute-done.34.rest_8_.rest_13_ = bf16[128,768]{1,0:T(8,128)(2,1)S(1)} collective-permute-done((bf16[128,768]{1,0:T(8,128)(2,1)S(1)}, bf16[128,768]{1,0:T(8,128)(2,1)S(1)}, u32[]{:S(2)}, u32[]{:S(2)}) %collective-permute-start.34) | collective-permute-done | bytes 196640 | tf_op jit(solution)/shard_map/ppermute | solution.py:569
  115.7 1.7 collective-permute-start.22
  118.0 3.7 collective-permute-done.23.rest_4_
  123.0 16.8 %shared_both.1 = (f32[1024,768]{1,0:T(8,128)}, f32[1024,768]{1,0:T(8,128)}, f32[1,4,96,1536]{3,2,1,0:T(8,128)}, f32[1,4,96,1536]{3,2,1,0:T(8,128)}) custom-call(s32[1024,1]{1,0:T(8,128)} %bitcast.132, bf16[32,768]{1,0:T(8,128)(2,1)} %copy-done.36, bf16[768,768]{1,0:T(8,128)(2,1)} %win_ref.4, bf16[768,768]{1,0:T(8,128)(2,1)} %wout_ref.2, ...), custom_call_target="tpu_custom_call" | custom-call | tf_op jit(solution)/shard_map/shared_both/pallas_call | solution.py:523
  140.7 19.9 %expert_one.2 = (bf16[4,768,768]{2,1,0:T(8,128)(2,1)}, bf16[4,768,768]{2,1,0:T(8,128)(2,1)}, f32[4,768,768]{2,1,0:T(8,128)}, bf16[4,768,768]{2,1,0:T(8,128)(2,1)}, bf16[4,2,192,768]{3,2,1,0:T(8,128)(2,1)}) custom-call(s32[8,1024]{1,0:T(8,128)} %copy-done.30, f32[8,1024]{1,0:T(8,128)} %copy-done.29, f32[2,1024]{1,0:T(2,128)} %pad_maximum_fusion.11.rest_11_.img_ref, ...), custom_call_target="tpu_custom_call" | custom-call | tf_op jit(solution)/shard_map/expert_one/pallas_call | solution.py:390
  160.6 19.3 %expert_one.3 = (bf16[4,768,768]{2,1,0:T(8,128)(2,1)}, bf16[4,768,768]{2,1,0:T(8,128)(2,1)}, f32[4,768,768]{2,1,0:T(8,128)}, bf16[4,768,768]{2,1,0:T(8,128)(2,1)}, bf16[4,2,192,768]{3,2,1,0:T(8,128)(2,1)}) custom-call(s32[8,1024]{1,0:T(8,128)} %copy-done.30, ...), custom_call_target="tpu_custom_call", output_to_operand_aliasing={{0}: (26, {}), {1}: (27, {}), {2}: (28, {}), {3}: (29, {})} | custom-call | tf_op jit(solution)/shard_map/expert_one/pallas_call | solution.py:390
  180.7 40.8 %expert_two.1 = (bf16[4,4,192,768]{3,2,1,0:T(8,128)(2,1)}, f32[1024,768]{1,0:T(8,128)}, f32[1024,768]{1,0:T(8,128)}, bf16[1024,768]{1,0:T(8,128)(2,1)}, bf16[1024,768]{1,0:T(8,128)(2,1)}) custom-call(s32[1024,8]{1,0:T(8,128)} %bitcast.128, f32[1024,8]{1,0:T(8,128)} %bitcast.130, bf16[4,768,768]{2,1,0:T(8,128)(2,1)} %get-tuple-element.47.rows_ref, ...), custom_call_target="tpu_custom_call" | custom-call | tf_op jit(solution)/shard_map/expert_two/pallas_call | solution.py:458
  222.1 3.2 collective-permute-done.48
  225.4 3.1 fusion.34
  229.7 2.2 collective-permute-start.51
  232.1 3.3 fusion.35
  235.4 5.2 %collective-permute-done.49 = bf16[256,768]{1,0:T(8,128)(2,1)S(1)} collective-permute-done((bf16[256,768]{1,0:T(8,128)(2,1)S(1)}, bf16[256,768]{1,0:T(8,128)(2,1)S(1)}, u32[]{:S(2)}, u32[]{:S(2)}) %collective-permute-start.49) | collective-permute-done | bytes 393248 | tf_op jit(solution)/shard_map/ppermute | solution.py:569
  240.6 8.9 %collective-permute-done.51 = bf16[256,768]{1,0:T(8,128)(2,1)S(1)} collective-permute-done((bf16[256,768]{1,0:T(8,128)(2,1)S(1)}, bf16[256,768]{1,0:T(8,128)(2,1)S(1)}, u32[]{:S(2)}, u32[]{:S(2)}) %collective-permute-start.51) | collective-permute-done | bytes 393248 | tf_op jit(solution)/shard_map/ppermute | solution.py:569
  251.9 21.6 %attn_bwd.1 = (bf16[256,768]{1,0:T(8,128)(2,1)}, f32[5,32,768]{2,1,0:T(8,128)}, f32[4,4,96,768]{3,2,1,0:T(8,128)}, f32[4,4,96,768]{3,2,1,0:T(8,128)}) custom-call(f32[256,768]{1,0:T(8,128)} %fusion.4.gn2_ref, f32[256,768]{1,0:T(8,128)} %get-tuple-element.40.mid_ref, f32[256,768]{1,0:T(8,128)} %get-tuple-element.57.attn_ref, bf16[256,768]{1,0:T(8,128)(2,1)} %copy-done.3, ...), custom_call_target="tpu_custom_call" | custom-call | tf_op jit(solution)/shard_map/attn_bwd/pallas_call | solution.py:296
  276.7 1.8 collective-permute-start.43
  278.5 8.5 %collective-permute-done.42 = bf16[256,768]{1,0:T(8,128)(2,1)S(1)} collective-permute-done((bf16[256,768]{1,0:T(8,128)(2,1)S(1)}, bf16[256,768]{1,0:T(8,128)(2,1)S(1)}, u32[]{:S(2)}, u32[]{:S(2)}) %collective-permute-start.42) | collective-permute-done | bytes 393248 | tf_op jit(solution)/shard_map/ppermute | solution.py:569
  287.0 7.7 %collective-permute-done.44 = bf16[256,768]{1,0:T(8,128)(2,1)S(1)} collective-permute-done((bf16[256,768]{1,0:T(8,128)(2,1)S(1)}, bf16[256,768]{1,0:T(8,128)(2,1)S(1)}, u32[]{:S(2)}, u32[]{:S(2)}) %collective-permute-start.44) | collective-permute-done | bytes 393248 | tf_op jit(solution)/shard_map/ppermute | solution.py:569
  297.1 2.7 finish.1
  302.2 2.2 collective-permute-start.45
  304.7 1.7 broadcast_select_fusion.70
  314.5 2.7 collective-permute-done.52
  323.6 2.7 collective-permute-done.56
  327.6 3.2 collective-permute-start.60
  332.1 2.4 fusion.27
  335.3 1.9 collective-permute-done.60
  337.3 3.1 collective-permute-start.72
  340.4 6.4 %collective-permute-done.59 = bf16[6,32,192]{2,1,0:T(8,128)(2,1)S(1)} collective-permute-done((bf16[6,32,192]{2,1,0:T(8,128)(2,1)S(1)}, bf16[6,32,192]{2,1,0:T(8,128)(2,1)S(1)}, u32[]{:S(2)}, u32[]{:S(2)}) %collective-permute-start.59) | collective-permute-done | bytes 73760 | tf_op jit(solution)/shard_map/ppermute | solution.py:650
  347.1 3.1 fusion.30
  351.8 14.4 %collective-permute-done.70 = bf16[96,1536]{1,0:T(8,128)(2,1)S(1)} collective-permute-done((bf16[96,1536]{1,0:T(8,128)(2,1)S(1)}, bf16[96,1536]{1,0:T(8,128)(2,1)S(1)}, u32[]{:S(2)}, u32[]{:S(2)}) %collective-permute-start.70) | collective-permute-done | bytes 294944 | tf_op jit(solution)/shard_map/ppermute | solution.py:683
  366.2 4.8 %collective-permute-done.72 = bf16[96,1536]{1,0:T(8,128)(2,1)S(1)} collective-permute-done((bf16[96,1536]{1,0:T(8,128)(2,1)S(1)}, bf16[96,1536]{1,0:T(8,128)(2,1)S(1)}, u32[]{:S(2)}, u32[]{:S(2)}) %collective-permute-start.72) | collective-permute-done | bytes 294944 | tf_op jit(solution)/shard_map/ppermute | solution.py:683
  372.2 24.7 %collective-permute-done.71 = bf16[96,1536]{1,0:T(8,128)(2,1)S(1)} collective-permute-done((bf16[96,1536]{1,0:T(8,128)(2,1)S(1)}, bf16[96,1536]{1,0:T(8,128)(2,1)S(1)}, u32[]{:S(2)}, u32[]{:S(2)}) %collective-permute-start.71) | collective-permute-done | bytes 294944 | tf_op jit(solution)/shard_map/ppermute | solution.py:683
  399.5 2.8 collective-permute-start.68
  402.9 2.8 convert_bitcast_fusion
  406.0 3.1 collective-permute-done.68
  409.1 5.6 %collective-permute-done.67 = bf16[96,768]{1,0:T(8,128)(2,1)S(1)} collective-permute-done((bf16[96,768]{1,0:T(8,128)(2,1)S(1)}, bf16[96,768]{1,0:T(8,128)(2,1)S(1)}, u32[]{:S(2)}, u32[]{:S(2)}) %collective-permute-start.67) | collective-permute-done | bytes 147488 | tf_op jit(solution)/shard_map/ppermute | solution.py:683
  416.6 2.9 bitcast_convert_fusion
  (330 shorter events, 96.3 us)
Async XLA Ops:
  7.2 395.7 %reduce-scatter.8.cloned.1.call-start = ((), (), s32[]{:S(2)}) async-start(), calls=%async_computation.5 | async-start | bytes 2949120 | tf_op jit(solution)/shard_map/reduce_scatter | solution.py:676
  8.9 35.0 %collective-permute-start.18 = (bf16[32,768]{1,0:T(8,128)(2,1)S(1)}, bf16[32,768]{1,0:T(8,128)(2,1)}, u32[]{:S(2)}, u32[]{:S(2)}) collective-permute-start(bf16[32,768]{1,0:T(8,128)(2,1)S(1)} %get-tuple-element.144), channel_id=1, source_target_pairs={{0,24},{8,16},{16,8},{24,0},{1,25},{9,17},{17,9},{25,1},{2,26},{10... | collective-permute-start | bytes 147464 | tf_op jit(solution)/shard_map/ppermute | solution.py:650
  13.9 26.8 %collective-permute-start.17 = (bf16[32,768]{1,0:T(8,128)(2,1)S(1)}, bf16[32,768]{1,0:T(8,128)(2,1)}, u32[]{:S(2)}, u32[]{:S(2)}) collective-permute-start(bf16[32,768]{1,0:T(8,128)(2,1)S(1)} %get-tuple-element.144), channel_id=1, source_target_pairs={{0,16},{8,24},{16,0},{24,8},{1,17},{9,25},{17,1},{25,9},{2,18},{10... | collective-permute-start | bytes 147464 | tf_op jit(solution)/shard_map/ppermute | solution.py:650
  13.9 25.1 %collective-permute-start.16 = (bf16[32,768]{1,0:T(8,128)(2,1)S(1)}, bf16[32,768]{1,0:T(8,128)(2,1)}, u32[]{:S(2)}, u32[]{:S(2)}) collective-permute-start(bf16[32,768]{1,0:T(8,128)(2,1)S(1)} %get-tuple-element.144), channel_id=1, source_target_pairs={{0,8},{8,0},{16,24},{24,16},{1,9},{9,1},{17,25},{25,17},{2,10},{10... | collective-permute-start | bytes 147464 | tf_op jit(solution)/shard_map/ppermute | solution.py:650
  21.4 11.8 %collective-permute-start.14 = (f32[9,1024]{1,0:T(8,128)}, f32[9,1024]{1,0:T(8,128)}, u32[]{:S(2)}, u32[]{:S(2)}) collective-permute-start(f32[9,1024]{1,0:T(8,128)} %pad_maximum_fusion.9), channel_id=1, source_target_pairs={{0,4},{4,0},{1,5},{5,1},{2,6},{6,2},{3,7},{7,3},{8,12},{12,8},{9,1... | collective-permute-start | bytes 110600 | tf_op jit(solution)/shard_map/ppermute | solution.py:572
  22.7 24.9 %collective-permute-start.5 = (bf16[32,6,192]{2,0,1:T(8,128)(2,1)}, bf16[32,6,192]{2,0,1:T(8,128)(2,1)}, u32[]{:S(2)}, u32[]{:S(2)}) collective-permute-start(bf16[32,6,192]{2,0,1:T(8,128)(2,1)} %convolution_convert_fusion), channel_id=1, source_target_pairs={{0,1},{1,0},{2,3},{3,2},{4,5},{5,4},{6,7},{7,6},{8,9},{9,8},{10,11... | collective-permute-start | bytes 221192 | tf_op jit(solution)/shard_map/ppermute | solution.py:569
  33.2 15.1 %collective-permute-start.4 = (bf16[32,6,192]{2,0,1:T(8,128)(2,1)}, bf16[32,6,192]{2,0,1:T(8,128)(2,1)S(1)}, u32[]{:S(2)}, u32[]{:S(2)}) collective-permute-start(bf16[32,6,192]{2,0,1:T(8,128)(2,1)} %convolution_convert_fusion), channel_id=1, source_target_pairs={{0,2},{1,3},{2,0},{3,1},{4,6},{5,7},{6,4},{7,5},{8,10},{9,11},{10,... | collective-permute-start | bytes 221192 | tf_op jit(solution)/shard_map/ppermute | solution.py:569
  39.0 10.7 %collective-permute-start.3 = (bf16[32,6,192]{2,0,1:T(8,128)(2,1)}, bf16[32,6,192]{2,0,1:T(8,128)(2,1)S(1)}, u32[]{:S(2)}, u32[]{:S(2)}) collective-permute-start(bf16[32,6,192]{2,0,1:T(8,128)(2,1)} %convolution_convert_fusion), channel_id=1, source_target_pairs={{0,3},{1,2},{2,1},{3,0},{4,7},{5,6},{6,5},{7,4},{8,11},{9,10},{10,... | collective-permute-start | bytes 221192 | tf_op jit(solution)/shard_map/ppermute | solution.py:569
  40.7 27.9 %collective-permute-start.7 = (bf16[384,768]{1,0:T(8,128)(2,1)S(1)}, bf16[384,768]{1,0:T(8,128)(2,1)S(1)}, u32[]{:S(2)}, u32[]{:S(2)}) collective-permute-start(bf16[384,768]{1,0:T(8,128)(2,1)S(1)} %fusion.7), channel_id=1, source_target_pairs={{0,2},{1,3},{2,0},{3,1},{4,6},{5,7},{6,4},{7,5},{8,10},{9,11},{10,... | collective-permute-start | bytes 1769480 | tf_op jit(solution)/shard_map/ppermute | solution.py:569
  43.9 29.8 %collective-permute-start.6 = (bf16[384,768]{1,0:T(8,128)(2,1)S(1)}, bf16[384,768]{1,0:T(8,128)(2,1)S(1)}, u32[]{:S(2)}, u32[]{:S(2)}) collective-permute-start(bf16[384,768]{1,0:T(8,128)(2,1)S(1)} %fusion.7), channel_id=1, source_target_pairs={{0,1},{1,0},{2,3},{3,2},{4,5},{5,4},{6,7},{7,6},{8,9},{9,8},{10,11... | collective-permute-start | bytes 1769480 | tf_op jit(solution)/shard_map/ppermute | solution.py:569
  47.7 15.1 %collective-permute-start.31 = (bf16[256,192]{1,0:T(8,128)(2,1)}, bf16[256,192]{1,0:T(8,128)(2,1)S(1)}, u32[]{:S(2)}, u32[]{:S(2)}) collective-permute-start(bf16[256,192]{1,0:T(8,128)(2,1)} %get-tuple-element.180), channel_id=1, source_target_pairs={{0,1},{1,0},{2,3},{3,2},{4,5},{5,4},{6,7},{7,6},{8,9},{9,8},{10,11... | collective-permute-start | bytes 294920 | tf_op jit(solution)/shard_map/ppermute | solution.py:569
  48.3 17.1 %collective-permute-start.29 = (bf16[256,192]{1,0:T(8,128)(2,1)}, bf16[256,192]{1,0:T(8,128)(2,1)S(1)}, u32[]{:S(2)}, u32[]{:S(2)}) collective-permute-start(bf16[256,192]{1,0:T(8,128)(2,1)} %get-tuple-element.181), channel_id=1, source_target_pairs={{0,3},{1,2},{2,1},{3,0},{4,7},{5,6},{6,5},{7,4},{8,11},{9,10},{10,... | collective-permute-start | bytes 294920 | tf_op jit(solution)/shard_map/ppermute | solution.py:569
  49.7 17.4 %collective-permute-start.30 = (bf16[256,192]{1,0:T(8,128)(2,1)}, bf16[256,192]{1,0:T(8,128)(2,1)S(1)}, u32[]{:S(2)}, u32[]{:S(2)}) collective-permute-start(bf16[256,192]{1,0:T(8,128)(2,1)} %get-tuple-element.182), channel_id=1, source_target_pairs={{0,2},{1,3},{2,0},{3,1},{4,6},{5,7},{6,4},{7,5},{8,10},{9,11},{10,... | collective-permute-start | bytes 294920 | tf_op jit(solution)/shard_map/ppermute | solution.py:569
  77.3 20.9 %collective-permute-start.33 = (bf16[256,768]{1,0:T(8,128)(2,1)S(1)}, bf16[256,768]{1,0:T(8,128)(2,1)S(1)}, u32[]{:S(2)}, u32[]{:S(2)}) collective-permute-start(bf16[256,768]{1,0:T(8,128)(2,1)S(1)} %pad_maximum_fusion.4.rest_5_.rest_10_.go_ref), channel_id=1, source_target_pairs={{0,2},{1,3},{2,0},{3,1},{4,6},{5,7},{6,4},{7,5},{8,10},{9,11},{10,... | collective-permute-start | bytes 1179656 | tf_op jit(solution)/shard_map/ppermute | solution.py:569
  80.7 19.6 %collective-permute-start.32 = (bf16[256,768]{1,0:T(8,128)(2,1)S(1)}, bf16[256,768]{1,0:T(8,128)(2,1)S(1)}, u32[]{:S(2)}, u32[]{:S(2)}) collective-permute-start(bf16[256,768]{1,0:T(8,128)(2,1)S(1)} %pad_maximum_fusion.4.rest_5_.rest_10_.go_ref), channel_id=1, source_target_pairs={{0,1},{1,0},{2,3},{3,2},{4,5},{5,4},{6,7},{7,6},{8,9},{9,8},{10,11... | collective-permute-start | bytes 1179656 | tf_op jit(solution)/shard_map/ppermute | solution.py:569
  96.6 16.0 %collective-permute-start.21 = (bf16[256,768]{1,0:T(8,128)(2,1)}, bf16[256,768]{1,0:T(8,128)(2,1)S(1)}, u32[]{:S(2)}, u32[]{:S(2)}) collective-permute-start(bf16[256,768]{1,0:T(8,128)(2,1)} %get-tuple-element.41.rest_0_), channel_id=1, source_target_pairs={{0,2},{1,3},{2,0},{3,1},{4,6},{5,7},{6,4},{7,5},{8,10},{9,11},{10,... | collective-permute-start | bytes 1179656 | tf_op jit(solution)/shard_map/ppermute | solution.py:569
  99.5 14.3 %collective-permute-start.20 = (bf16[256,768]{1,0:T(8,128)(2,1)}, bf16[256,768]{1,0:T(8,128)(2,1)S(1)}, u32[]{:S(2)}, u32[]{:S(2)}) collective-permute-start(bf16[256,768]{1,0:T(8,128)(2,1)} %get-tuple-element.41.rest_0_), channel_id=1, source_target_pairs={{0,1},{1,0},{2,3},{3,2},{4,5},{5,4},{6,7},{7,6},{8,9},{9,8},{10,11... | collective-permute-start | bytes 1179656 | tf_op jit(solution)/shard_map/ppermute | solution.py:569
  100.4 12.2 %collective-permute-start.34 = (bf16[128,768]{1,0:T(8,128)(2,1)S(1)}, bf16[128,768]{1,0:T(8,128)(2,1)S(1)}, u32[]{:S(2)}, u32[]{:S(2)}) collective-permute-start(bf16[128,768]{1,0:T(8,128)(2,1)S(1)} %slice.333), channel_id=1, source_target_pairs={{0,2},{1,3},{2,0},{3,1},{4,6},{5,7},{6,4},{7,5},{8,10},{9,11},{10,... | collective-permute-start | bytes 589832 | tf_op jit(solution)/shard_map/ppermute | solution.py:569
  100.9 12.9 %collective-permute-start.36 = (bf16[256,768]{1,0:T(8,128)(2,1)S(1)}, bf16[256,768]{1,0:T(8,128)(2,1)S(1)}, u32[]{:S(2)}, u32[]{:S(2)}) collective-permute-start(bf16[256,768]{1,0:T(8,128)(2,1)S(1)} %pad_maximum_fusion.4.rest_5_.rest_10_.go_ref), channel_id=1, source_target_pairs={{0,4},{4,0},{1,5},{5,1},{2,6},{6,2},{3,7},{7,3},{8,12},{12,8},{9,1... | collective-permute-start | bytes 1179656 | tf_op jit(solution)/shard_map/ppermute | solution.py:572
  113.8 26.1 %collective-permute-start.24 = (bf16[256,768]{1,0:T(8,128)(2,1)}, bf16[256,768]{1,0:T(8,128)(2,1)S(1)}, u32[]{:S(2)}, u32[]{:S(2)}) collective-permute-start(bf16[256,768]{1,0:T(8,128)(2,1)} %get-tuple-element.41.rest_0_), channel_id=1, source_target_pairs={{0,4},{4,0},{1,5},{5,1},{2,6},{6,2},{3,7},{7,3},{8,12},{12,8},{9,1... | collective-permute-start | bytes 1179656 | tf_op jit(solution)/shard_map/ppermute | solution.py:572
  117.5 22.5 %collective-permute-start.26 = (bf16[256,768]{1,0:T(8,128)(2,1)S(1)}, bf16[256,768]{1,0:T(8,128)(2,1)}, u32[]{:S(2)}, u32[]{:S(2)}) collective-permute-start(bf16[256,768]{1,0:T(8,128)(2,1)S(1)} %collective-permute-done.21.rest_2_), channel_id=1, source_target_pairs={{0,4},{4,0},{1,5},{5,1},{2,6},{6,2},{3,7},{7,3},{8,12},{12,8},{9,1... | collective-permute-start | bytes 1179656 | tf_op jit(solution)/shard_map/ppermute | solution.py:572
  117.5 22.5 %collective-permute-start.25 = (bf16[256,768]{1,0:T(8,128)(2,1)S(1)}, bf16[256,768]{1,0:T(8,128)(2,1)}, u32[]{:S(2)}, u32[]{:S(2)}) collective-permute-start(bf16[256,768]{1,0:T(8,128)(2,1)S(1)} %collective-permute-done.20.rest_1_), channel_id=1, source_target_pairs={{0,4},{4,0},{1,5},{5,1},{2,6},{6,2},{3,7},{7,3},{8,12},{12,8},{9,1... | collective-permute-start | bytes 1179656 | tf_op jit(solution)/shard_map/ppermute | solution.py:572
  121.7 18.3 %collective-permute-start.28 = (bf16[128,768]{1,0:T(8,128)(2,1)S(1)}, bf16[128,768]{1,0:T(8,128)(2,1)S(1)}, u32[]{:S(2)}, u32[]{:S(2)}) collective-permute-start(bf16[128,768]{1,0:T(8,128)(2,1)S(1)} %collective-permute-done.23.rest_4_), channel_id=1, source_target_pairs={{0,4},{4,0},{1,5},{5,1},{2,6},{6,2},{3,7},{7,3},{8,12},{12,8},{9,1... | collective-permute-start | bytes 589832 | tf_op jit(solution)/shard_map/ppermute | solution.py:572
  122.4 17.6 %collective-permute-start.27 = (bf16[128,768]{1,0:T(8,128)(2,1)S(1)}, bf16[128,768]{1,0:T(8,128)(2,1)}, u32[]{:S(2)}, u32[]{:S(2)}) collective-permute-start(bf16[128,768]{1,0:T(8,128)(2,1)S(1)} %collective-permute-done.22.rest_3_), channel_id=1, source_target_pairs={{0,4},{4,0},{1,5},{5,1},{2,6},{6,2},{3,7},{7,3},{8,12},{12,8},{9,1... | collective-permute-start | bytes 589832 | tf_op jit(solution)/shard_map/ppermute | solution.py:572
  179.9 223.0 %reduce-scatter.6.cloned.1.call-start = ((), (), s32[]{:S(2)}) async-start(), calls=%async_computation.4 | async-start | bytes 2949120 | tf_op jit(solution)/shard_map/reduce_scatter | solution.py:676
  180.7 236.0 %reduce-scatter.4.cloned.1.call-start = ((), (), s32[]{:S(2)}) async-start(), calls=%async_computation.3 | async-start | bytes 5898240 | tf_op jit(solution)/shard_map/reduce_scatter | solution.py:676
  221.6 10.5 %collective-permute-start.41 = (bf16[1024,768]{1,0:T(8,128)(2,1)}, bf16[1024,768]{1,0:T(8,128)(2,1)}, u32[]{:S(2)}, u32[]{:S(2)}) collective-permute-start(bf16[1024,768]{1,0:T(8,128)(2,1)} %get-tuple-element.53), channel_id=1, source_target_pairs={{0,4},{4,0},{1,5},{5,1},{2,6},{6,2},{3,7},{7,3},{8,12},{12,8},{9,1... | collective-permute-start | bytes 4718600 | tf_op jit(solution)/shard_map/ppermute | solution.py:572
  228.6 12.1 %collective-permute-start.49 = (bf16[256,768]{1,0:T(8,128)(2,1)S(1)}, bf16[256,768]{1,0:T(8,128)(2,1)S(1)}, u32[]{:S(2)}, u32[]{:S(2)}) collective-permute-start(bf16[256,768]{1,0:T(8,128)(2,1)S(1)} %get-tuple-element.152), channel_id=1, source_target_pairs={{0,1},{1,0},{2,3},{3,2},{4,5},{5,4},{6,7},{7,6},{8,9},{9,8},{10,11... | collective-permute-start | bytes 1179656 | tf_op jit(solution)/shard_map/ppermute | solution.py:569
  229.7 19.8 %collective-permute-start.51 = (bf16[256,768]{1,0:T(8,128)(2,1)S(1)}, bf16[256,768]{1,0:T(8,128)(2,1)S(1)}, u32[]{:S(2)}, u32[]{:S(2)}) collective-permute-start(bf16[256,768]{1,0:T(8,128)(2,1)S(1)} %get-tuple-element.153), channel_id=1, source_target_pairs={{0,3},{1,2},{2,1},{3,0},{4,7},{5,6},{6,5},{7,4},{8,11},{9,10},{10,... | collective-permute-start | bytes 1179656 | tf_op jit(solution)/shard_map/ppermute | solution.py:569
  231.8 19.0 %collective-permute-start.50 = (bf16[256,768]{1,0:T(8,128)(2,1)S(1)}, bf16[256,768]{1,0:T(8,128)(2,1)S(1)}, u32[]{:S(2)}, u32[]{:S(2)}) collective-permute-start(bf16[256,768]{1,0:T(8,128)(2,1)S(1)} %get-tuple-element.154), channel_id=1, source_target_pairs={{0,2},{1,3},{2,0},{3,1},{4,6},{5,7},{6,4},{7,5},{8,10},{9,11},{10,... | collective-permute-start | bytes 1179656 | tf_op jit(solution)/shard_map/ppermute | solution.py:569
  273.5 73.5 %collective-permute-start.62 = (f32[4,4,96,768]{3,2,1,0:T(8,128)}, f32[4,4,96,768]{3,2,1,0:T(8,128)}, u32[]{:S(2)}, u32[]{:S(2)}) collective-permute-start(f32[4,4,96,768]{3,2,1,0:T(8,128)} %get-tuple-element.65), channel_id=1, source_target_pairs={{0,4},{4,0},{1,5},{5,1},{2,6},{6,2},{3,7},{7,3},{8,12},{12,8},{9,1... | collective-permute-start | bytes 14155784 | tf_op jit(solution)/shard_map/ppermute | solution.py:572
  274.9 12.1 %collective-permute-start.42 = (bf16[256,768]{1,0:T(8,128)(2,1)S(1)}, bf16[256,768]{1,0:T(8,128)(2,1)S(1)}, u32[]{:S(2)}, u32[]{:S(2)}) collective-permute-start(bf16[256,768]{1,0:T(8,128)(2,1)S(1)} %get-tuple-element.155), channel_id=1, source_target_pairs={{0,1},{1,0},{2,3},{3,2},{4,5},{5,4},{6,7},{7,6},{8,9},{9,8},{10,11... | collective-permute-start | bytes 1179656 | tf_op jit(solution)/shard_map/ppermute | solution.py:569
  275.8 18.9 %collective-permute-start.44 = (bf16[256,768]{1,0:T(8,128)(2,1)S(1)}, bf16[256,768]{1,0:T(8,128)(2,1)S(1)}, u32[]{:S(2)}, u32[]{:S(2)}) collective-permute-start(bf16[256,768]{1,0:T(8,128)(2,1)S(1)} %get-tuple-element.156), channel_id=1, source_target_pairs={{0,3},{1,2},{2,1},{3,0},{4,7},{5,6},{6,5},{7,4},{8,11},{9,10},{10,... | collective-permute-start | bytes 1179656 | tf_op jit(solution)/shard_map/ppermute | solution.py:569
  276.7 19.4 %collective-permute-start.43 = (bf16[256,768]{1,0:T(8,128)(2,1)S(1)}, bf16[256,768]{1,0:T(8,128)(2,1)S(1)}, u32[]{:S(2)}, u32[]{:S(2)}) collective-permute-start(bf16[256,768]{1,0:T(8,128)(2,1)S(1)} %get-tuple-element.157), channel_id=1, source_target_pairs={{0,2},{1,3},{2,0},{3,1},{4,6},{5,7},{6,4},{7,5},{8,10},{9,11},{10,... | collective-permute-start | bytes 1179656 | tf_op jit(solution)/shard_map/ppermute | solution.py:569
  278.5 53.6 %collective-permute-start.69 = (f32[1,4,96,1536]{3,2,1,0:T(8,128)}, f32[1,4,96,1536]{3,2,1,0:T(8,128)}, u32[]{:S(2)}, u32[]{:S(2)}) collective-permute-start(f32[1,4,96,1536]{3,2,1,0:T(8,128)} %get-tuple-element.67), channel_id=1, source_target_pairs={{0,4},{4,0},{1,5},{5,1},{2,6},{6,2},{3,7},{7,3},{8,12},{12,8},{9,1... | collective-permute-start | bytes 7077896 | tf_op jit(solution)/shard_map/ppermute | solution.py:572
  313.9 9.7 %collective-permute-start.55 = (f32[6,32,192]{2,1,0:T(8,128)}, f32[6,32,192]{2,1,0:T(8,128)}, u32[]{:S(2)}, u32[]{:S(2)}) collective-permute-start(f32[6,32,192]{2,1,0:T(8,128)} %get-tuple-element.124), channel_id=1, source_target_pairs={{0,1},{1,0},{2,3},{3,2},{4,5},{5,4},{6,7},{7,6},{8,9},{9,8},{10,11... | collective-permute-start | bytes 442376 | tf_op jit(solution)/shard_map/ppermute | solution.py:569
  327.6 9.6 %collective-permute-start.60 = (bf16[6,32,192]{2,1,0:T(8,128)(2,1)S(1)}, bf16[6,32,192]{2,1,0:T(8,128)(2,1)S(1)}, u32[]{:S(2)}, u32[]{:S(2)}) collective-permute-start(bf16[6,32,192]{2,1,0:T(8,128)(2,1)S(1)} %get-tuple-element.123), channel_id=1, source_target_pairs={{0,24},{8,16},{16,8},{24,0},{1,25},{9,17},{17,9},{25,1},{2,26},{10... | collective-permute-start | bytes 221192 | tf_op jit(solution)/shard_map/ppermute | solution.py:650
  330.8 16.0 %collective-permute-start.59 = (bf16[6,32,192]{2,1,0:T(8,128)(2,1)S(1)}, bf16[6,32,192]{2,1,0:T(8,128)(2,1)S(1)}, u32[]{:S(2)}, u32[]{:S(2)}) collective-permute-start(bf16[6,32,192]{2,1,0:T(8,128)(2,1)S(1)} %get-tuple-element.123), channel_id=1, source_target_pairs={{0,16},{8,24},{16,0},{24,8},{1,17},{9,25},{17,1},{25,9},{2,18},{10... | collective-permute-start | bytes 221192 | tf_op jit(solution)/shard_map/ppermute | solution.py:650
  330.8 16.0 %collective-permute-start.58 = (bf16[6,32,192]{2,1,0:T(8,128)(2,1)S(1)}, bf16[6,32,192]{2,1,0:T(8,128)(2,1)S(1)}, u32[]{:S(2)}, u32[]{:S(2)}) collective-permute-start(bf16[6,32,192]{2,1,0:T(8,128)(2,1)S(1)} %get-tuple-element.123), channel_id=1, source_target_pairs={{0,8},{8,0},{16,24},{24,16},{1,9},{9,1},{17,25},{25,17},{2,10},{10... | collective-permute-start | bytes 221192 | tf_op jit(solution)/shard_map/ppermute | solution.py:650
  334.5 31.6 %collective-permute-start.70 = (bf16[96,1536]{1,0:T(8,128)(2,1)S(1)}, bf16[96,1536]{1,0:T(8,128)(2,1)S(1)}, u32[]{:S(2)}, u32[]{:S(2)}) collective-permute-start(bf16[96,1536]{1,0:T(8,128)(2,1)S(1)} %get-tuple-element.158), channel_id=1, source_target_pairs={{0,8},{8,0},{16,24},{24,16},{1,9},{9,1},{17,25},{25,17},{2,10},{10... | collective-permute-start | bytes 884744 | tf_op jit(solution)/shard_map/ppermute | solution.py:683
  337.3 33.7 %collective-permute-start.72 = (bf16[96,1536]{1,0:T(8,128)(2,1)S(1)}, bf16[96,1536]{1,0:T(8,128)(2,1)S(1)}, u32[]{:S(2)}, u32[]{:S(2)}) collective-permute-start(bf16[96,1536]{1,0:T(8,128)(2,1)S(1)} %get-tuple-element.159), channel_id=1, source_target_pairs={{0,24},{8,16},{16,8},{24,0},{1,25},{9,17},{17,9},{25,1},{2,26},{10... | collective-permute-start | bytes 884744 | tf_op jit(solution)/shard_map/ppermute | solution.py:683
  346.8 50.1 %collective-permute-start.71 = (bf16[96,1536]{1,0:T(8,128)(2,1)S(1)}, bf16[96,1536]{1,0:T(8,128)(2,1)S(1)}, u32[]{:S(2)}, u32[]{:S(2)}) collective-permute-start(bf16[96,1536]{1,0:T(8,128)(2,1)S(1)} %get-tuple-element.160), channel_id=1, source_target_pairs={{0,16},{8,24},{16,0},{24,8},{1,17},{9,25},{17,1},{25,9},{2,18},{10... | collective-permute-start | bytes 884744 | tf_op jit(solution)/shard_map/ppermute | solution.py:683
  346.9 51.0 %collective-permute-start.61 = (bf16[4,6,32,192]{3,2,1,0:T(8,128)(2,1)S(1)}, bf16[4,6,32,192]{3,2,1,0:T(8,128)(2,1)S(1)}, u32[]{:S(2)}, u32[]{:S(2)}) collective-permute-start(bf16[4,6,32,192]{3,2,1,0:T(8,128)(2,1)S(1)} %pad_maximum_fusion.5), channel_id=1, source_target_pairs={{0,4},{4,0},{1,5},{5,1},{2,6},{6,2},{3,7},{7,3},{8,12},{12,8},{9,1... | collective-permute-start | bytes 884744 | tf_op jit(solution)/shard_map/ppermute | solution.py:572
  350.4 48.7 %collective-permute-start.63 = (bf16[4,96,768]{2,1,0:T(8,128)(2,1)S(1)}, bf16[4,96,768]{2,1,0:T(8,128)(2,1)S(1)}, u32[]{:S(2)}, u32[]{:S(2)}) collective-permute-start(bf16[4,96,768]{2,1,0:T(8,128)(2,1)S(1)} %get-tuple-element.149), channel_id=1, source_target_pairs={{0,1},{1,0},{2,3},{3,2},{4,5},{5,4},{6,7},{7,6},{8,9},{9,8},{10,11... | collective-permute-start | bytes 1769480 | tf_op jit(solution)/shard_map/ppermute | solution.py:569
  366.2 32.9 %collective-permute-start.65 = (bf16[4,96,768]{2,1,0:T(8,128)(2,1)S(1)}, bf16[4,96,768]{2,1,0:T(8,128)(2,1)S(1)}, u32[]{:S(2)}, u32[]{:S(2)}) collective-permute-start(bf16[4,96,768]{2,1,0:T(8,128)(2,1)S(1)} %get-tuple-element.150), channel_id=1, source_target_pairs={{0,3},{1,2},{2,1},{3,0},{4,7},{5,6},{6,5},{7,4},{8,11},{9,10},{10,... | collective-permute-start | bytes 1769480 | tf_op jit(solution)/shard_map/ppermute | solution.py:569
  371.0 28.1 %collective-permute-start.64 = (bf16[4,96,768]{2,1,0:T(8,128)(2,1)S(1)}, bf16[4,96,768]{2,1,0:T(8,128)(2,1)S(1)}, u32[]{:S(2)}, u32[]{:S(2)}) collective-permute-start(bf16[4,96,768]{2,1,0:T(8,128)(2,1)S(1)} %get-tuple-element.151), channel_id=1, source_target_pairs={{0,2},{1,3},{2,0},{3,1},{4,6},{5,7},{6,4},{7,5},{8,10},{9,11},{10,... | collective-permute-start | bytes 1769480 | tf_op jit(solution)/shard_map/ppermute | solution.py:569
  399.5 9.6 %collective-permute-start.68 = (bf16[96,768]{1,0:T(8,128)(2,1)S(1)}, bf16[96,768]{1,0:T(8,128)(2,1)S(1)}, u32[]{:S(2)}, u32[]{:S(2)}) collective-permute-start(bf16[96,768]{1,0:T(8,128)(2,1)S(1)} %get-tuple-element.178), channel_id=1, source_target_pairs={{0,24},{8,16},{16,8},{24,0},{1,25},{9,17},{17,9},{25,1},{2,26},{10... | collective-permute-start | bytes 442376 | tf_op jit(solution)/shard_map/ppermute | solution.py:683
  402.2 12.5 %collective-permute-start.67 = (bf16[96,768]{1,0:T(8,128)(2,1)S(1)}, bf16[96,768]{1,0:T(8,128)(2,1)S(1)}, u32[]{:S(2)}, u32[]{:S(2)}) collective-permute-start(bf16[96,768]{1,0:T(8,128)(2,1)S(1)} %get-tuple-element.179), channel_id=1, source_target_pairs={{0,16},{8,24},{16,0},{24,8},{1,17},{9,25},{17,1},{25,9},{2,18},{10... | collective-permute-start | bytes 442376 | tf_op jit(solution)/shard_map/ppermute | solution.py:683
  (78 other events, 772.0 us)
Sparse Core Ops, SparseCore 0:
  180.0 48.5 reduce-scatter.7
  230.9 47.0 reduce-scatter.5
  280.4 109.3 reduce-scatter.3

commit v2 on v1

--- a/solution.py
+++ b/solution.py
@@ -14,6 +14,7 @@
 CAP = 384
 EPSILON = 1e-06
 NEG_FILL = -1e30
+DP, EXP, HID = "dp", "expert", "hidden"
 BF = jnp.bfloat16
 F32 = jnp.float32
 GELU_C = 0.7978845608028654
@@ -71,10 +72,10 @@
     step = pl.program_id(0)
     fetch_weights(w_in, w_ref, core_ref[0], sems)
     feat = ctx_ref.shape[2]
-    images = mod_ref.shape[0]
+    images = mod_ref.shape[1]
 
     def mod(k):
-        return dot(image_hot(img_ref[...], images), mod_ref[:, k * D:(k + 1) * D])
+        return dot(image_hot(img_ref[...], images), mod_ref[k])
 
     @pl.when(step == 0)
     def _():
@@ -133,7 +134,6 @@
         ],
         scratch_shapes=[pltpu.VMEM((parts, D, 4 * feat), BF), pltpu.SemaphoreType.DMA((len(weights),))],
         compiler_params=kernel_params(),
-        name="attn_fwd",
     )(x_rows, img_col, mod, seg_col, seg_row, core, *weights, *extras)
 
 
@@ -154,14 +154,14 @@
     step = pl.program_id(0)
     fetch_weights(w_in, w_ref, core_ref[0], sems)
     feat = ctx_ref.shape[2]
-    images = mod_ref.shape[0]
+    images = mod_ref.shape[1]
     scale = HEAD_DIM ** -0.5
 
     def hot():
         return image_hot(img_ref[...], images)
 
     def mod(k):
-        return dot(hot(), mod_ref[:, k * D:(k + 1) * D])
+        return dot(hot(), mod_ref[k])
 
     @pl.when(step == 0)
     def _():
@@ -290,7 +290,7 @@
     rows = x_rows.shape[0]
     parts = qkv.shape[0]
     feat = D // parts
-    images = mod.shape[0]
+    images = mod.shape[1]
     whole = fixed(rows, D)
     specs, shapes = row_specs(parts, pieces, 4 * feat, lambda m: m)
     return pl.pallas_call(
@@ -312,27 +312,81 @@
             pltpu.VMEM((parts, D, 4 * feat), BF), pltpu.SemaphoreType.DMA((len(weights),)),
         ],
         compiler_params=kernel_params(),
-        name="attn_bwd",
     )(gn2, mid, attn, go, x_rows, n1, qkv, ctx, img_col, mod, seg_col, seg_row, core, *weights)
 
 
 def finish_kernel(mid_ref, mlp_ref, go_ref, img_ref, gate_ref, out_ref, gmod_ref):
-    hot = image_hot(img_ref[...], gate_ref.shape[0])
+    hot = image_hot(img_ref[...], gate_ref.shape[1])
     mlp = mlp_ref[...]
-    out_ref[...] = (mid_ref[...] + dot(hot, gate_ref[...]) * mlp).astype(BF)
+    out_ref[...] = (mid_ref[...] + dot(hot, gate_ref[0]) * mlp).astype(BF)
     gmod_ref[...] = image_sum(hot, go_ref[...].astype(F32) * mlp)
 
 
-def finish(mid, mlp, go, img_col, gate):
+def gate_spec(mod):
+    return pl.BlockSpec((1,) + mod.shape[1:], lambda m: (5, 0, 0))
+
+
+def finish(mid, mlp, go, img_col, mod):
+    rows = mid.shape[0]
+    whole = fixed(rows, D)
     return pl.pallas_call(
         finish_kernel,
+        grid=(1,),
+        in_specs=[whole, whole, whole, fixed(rows, 1), gate_spec(mod)],
+        out_specs=[whole, fixed(*mod.shape[1:])],
         out_shape=[
             jax.ShapeDtypeStruct(mid.shape, BF),
-            jax.ShapeDtypeStruct(gate.shape, F32),
+            jax.ShapeDtypeStruct(mod.shape[1:], F32),
         ],
         compiler_params=kernel_params(),
-        name="finish",
-    )(mid, mlp, go, img_col, gate)
+    )(mid, mlp, go, img_col, mod)
+
+
+def tables_kernel(own_ref, far_ref, image_ref, ids_ref, row_ref, col_ref):
+    core, me = ids_ref[0], ids_ref[2]
+    tokens = own_ref.shape[1]
+    parts = 4
+    size = tokens // parts
+    segs = image_ref.shape[1] // parts
+    hots, gates, images, seg_rows = [], [], [], []
+    for j, ref in enumerate((own_ref, far_ref)):
+        tiles, pictures = [], []
+        for m in range(parts):
+            tile = ref[:, pl.ds(pl.multiple_of((me ^ m) * size, size), size)]
+            seg = tile[4:5]
+            image = jnp.zeros_like(seg)
+            for k in range(segs):
+                image = jnp.where(seg == float(k), image_ref[j, (me ^ m) * segs + k].astype(F32), image)
+            tiles.append(tile)
+            pictures.append(image)
+        table = jnp.concatenate(tiles, axis=1)
+        images.append(jnp.concatenate(pictures, axis=1))
+        seg_rows.append(table[4:5])
+        experts = (lax.broadcasted_iota(jnp.int32, (EXP_DEV, tokens), 0) + core * EXP_DEV).astype(F32)
+        first, second = table[0:1] == experts, table[1:2] == experts
+        hots.append(jnp.where(first | second, 1.0, 0.0))
+        gates.append(jnp.where(first, table[2:3], jnp.where(second, table[3:4], 0.0)))
+    hot = jnp.concatenate(hots, axis=0)
+    before = lax.broadcasted_iota(jnp.int32, (tokens, tokens), 0) <= lax.broadcasted_iota(jnp.int32, (tokens, tokens), 1)
+    slot = dot(hot.astype(BF), before.astype(BF))
+    pos = jnp.where(hot > 0.5, slot - 1.0, -1.0)
+    rest = jnp.concatenate(images + seg_rows + [jnp.zeros((4, tokens), F32)], axis=0)
+    rows = jnp.concatenate([pos] + gates + [rest], axis=0)
+    row_ref[...] = rows
+    col_ref[...] = rows.T
+
+
+def tables(own, far, images, ids):
+    tokens = own.shape[1]
+    return pl.pallas_call(
+        tables_kernel,
+        in_specs=[pl.BlockSpec(own.shape, lambda: (0, 0)), pl.BlockSpec(far.shape, lambda: (0, 0)), smem(), smem()],
+        out_shape=[
+            jax.ShapeDtypeStruct((24, tokens), F32),
+            jax.ShapeDtypeStruct((tokens, 24), F32),
+        ],
+        compiler_params=kernel_params(),
+    )(own, far, images, ids)
 
 
 def store_split(ref, values):
@@ -341,9 +395,9 @@
         ref[p, 0] = values[p * rows:(p + 1) * rows].astype(ref.dtype)
 
 
-def expert_one_kernel(pos_ref, gate_ref, img_ref, gm_ref, win_ref, *rest, tiles, first, kept):
-    pieces_in, rest = rest[:tiles], rest[tiles + 1 + kept:]
-    rows_ref, act_ref, slope_ref, gslot_ref, gw_ref, n2_ref, go_ref, sems = rest
+def expert_one_kernel(row_ref, win_ref, mod_ref, gate_far_ref, *rest, tiles, first, kept):
+    pieces_in, rest = rest[:tiles], rest[tiles + kept:]
+    rows_ref, act_ref, slope_ref, gslot_ref, gw_ref, n2_ref, go_ref, gm_ref, sems = rest
     local = first + pl.program_id(0)
     tokens = n2_ref.shape[1]
     images = gm_ref.shape[1]
@@ -354,17 +408,19 @@
         targets = []
         for i, (ref, j) in enumerate(((n2_ref, 0), (n2_ref, 1), (go_ref, 0), (go_ref, 1))):
             targets += laid_out(pieces_in[i * each:(i + 1) * each], ref.at[j])
-        fetch(pieces_in, targets, sems)
+        sources = list(pieces_in) + [mod_ref.at[5], gate_far_ref]
+        fetch(sources, targets + [gm_ref.at[0], gm_ref.at[1]], sems)
 
     def block(j, carry):
-        where_ = pos_ref[pl.ds(j * EXP_DEV + local, 1), :]
+        where_ = row_ref[pl.ds(j * EXP_DEV + local, 1), :].astype(jnp.int32)
         mask = lax.broadcasted_iota(jnp.int32, (CAP, tokens), 0) == where_
         pick = mask.astype(BF)
         rows = dot(pick, n2_ref[j]).astype(BF)
         slots = pl.ds(pl.multiple_of(j * CAP, CAP), CAP)
         rows_ref[0, slots, :] = rows
-        gate = jnp.sum(jnp.where(mask, gate_ref[pl.ds(j * EXP_DEV + local, 1), :], 0.0), axis=1, keepdims=True)
-        image = jnp.sum(jnp.where(mask, img_ref[pl.ds(j, 1), :], 0.0), axis=1, keepdims=True)
+        gates = row_ref[pl.ds(2 * EXP_DEV + j * EXP_DEV + local, 1), :]
+        gate = jnp.sum(jnp.where(mask, gates, 0.0), axis=1, keepdims=True)
+        image = jnp.sum(jnp.where(mask, row_ref[pl.ds(4 * EXP_DEV + j, 1), :], 0.0), axis=1, keepdims=True)
         hot = image_hot(image.astype(jnp.int32), images)
         grad = dot(hot, gm_ref[j]) * dot(pick, go_ref[j])
         gslot_ref[0, slots, :] = (gate * grad).astype(BF)
@@ -377,8 +433,8 @@
     store_split(gw_ref, dot(gslot_ref[0], act_ref[0], 0, 0))
 
 
-def expert_one(pos, gate, img, gate_mlp, w_in, tiles, after, pieces, first, kept):
-    tokens = pos.shape[1]
+def expert_one(rows, mod, gate_far, w_in, tiles, pieces, first, kept):
+    tokens = rows.shape[1]
     slots = 2 * CAP
     ff = w_in.shape[2]
     count = EXP_DEV // 2
@@ -386,14 +442,11 @@
     def shifted(*shape):
         return pl.BlockSpec((1,) + shape, lambda m: (m + first,) + (0,) * len(shape))
 
-    fixed_ins = 5
+    fixed_ins = 4
     return pl.pallas_call(
         functools.partial(expert_one_kernel, tiles=len(tiles), first=first, kept=len(kept)),
         grid=(count,),
-        in_specs=[
-            fixed(2 * EXP_DEV, tokens), fixed(2 * EXP_DEV, tokens), fixed(2, tokens),
-            fixed(*gate_mlp.shape), shifted(D, ff),
-        ] + [hbm()] * (len(tiles) + 1 + len(kept)),
+        in_specs=[fixed(*rows.shape), shifted(D, ff)] + [hbm()] * (2 + len(tiles) + len(kept)),
         out_specs=[
             shifted(slots, D), shifted(slots, ff), shifted(slots, ff), shifted(slots, D),
             pl.BlockSpec((pieces, 1, D // pieces, ff), lambda m: (0, m, 0, 0)),
@@ -406,52 +459,47 @@
             jax.ShapeDtypeStruct((pieces, count, D // pieces, ff), BF),
         ],
         scratch_shapes=[
-            pltpu.VMEM((2, tokens, D), BF), pltpu.VMEM((2, tokens, D), BF),
-            pltpu.SemaphoreType.DMA((len(tiles),)),
-        ],
-        input_output_aliases={fixed_ins + len(tiles) + 1 + i: i for i in range(len(kept))},
+            pltpu.VMEM((2, tokens, D), BF), pltpu.VMEM((2, tokens, D), BF), pltpu.VMEM((2,) + mod.shape[1:], BF),
+            pltpu.SemaphoreType.DMA((len(tiles) + 2,)),
+        ],
+        input_output_aliases={fixed_ins + len(tiles) + i: i for i in range(len(kept))},
         compiler_params=kernel_params(),
-        name="expert_one",
-    )(pos, gate, img, gate_mlp, w_in, *tiles, after, *kept)
+    )(rows, w_in, mod, gate_far, *tiles, *kept)
+
+
+def picked(col_ref, j, local):
+    lanes = lax.broadcasted_iota(jnp.int32, col_ref.shape, 1)
+    place = jnp.sum(jnp.where(lanes == j * EXP_DEV + local, col_ref[...], 0.0), axis=1, keepdims=True)
+    slots = lax.broadcasted_iota(jnp.int32, (col_ref.shape[0], CAP), 1)
+    return (slots == place.astype(jnp.int32)).astype(BF)
 
 
 def expert_two_kernel(
-    pos_ref, gate_ref, rows_ref, act_ref, slope_ref, gslot_ref, win_ref, wout_ref,
-    gw_ref, gn_ref, mix_ref, gn_far_ref, mix_far_ref,
-    gpre_ref, gn_acc, mix_acc,
+    col_ref, rows_ref, slope_ref, gslot_ref, win_ref, wout_ref,
+    gw_ref, gn_ref, gn_far_ref, gpre_ref, gn_acc,
 ):
     local = pl.program_id(0)
-    count = pl.num_programs(0)
-    tokens = pos_ref.shape[0]
-    lanes = lax.broadcasted_iota(jnp.int32, pos_ref.shape, 1)
 
     @pl.when(local == 0)
     def _():
-        for ref in (gn_ref, mix_ref, gn_acc, mix_acc):
-            ref[...] = jnp.zeros_like(ref)
-
-    for j, (gn, mix) in enumerate(((gn_ref, mix_ref), (gn_acc, mix_acc))):
+        gn_ref[...] = jnp.zeros_like(gn_ref)
+        gn_acc[...] = jnp.zeros_like(gn_acc)
+
+    for j, total in enumerate((gn_ref, gn_acc)):
         slots = slice(j * CAP, (j + 1) * CAP)
         grad_pre = (slope_ref[0, slots, :] * dot(gslot_ref[0, slots, :], wout_ref[0], 1, 1)).astype(BF)
         gpre_ref[slots, :] = grad_pre
         grad_in = dot(grad_pre, win_ref[0], 1, 1).astype(BF)
-        result = dot(act_ref[0, slots, :], wout_ref[0]).astype(BF)
-        here = lanes == j * count + local
-        where_ = jnp.sum(jnp.where(here, pos_ref[...], 0), axis=1, keepdims=True)
-        gate = jnp.sum(jnp.where(here, gate_ref[...], 0.0), axis=1, keepdims=True)
-        pick = (lax.broadcasted_iota(jnp.int32, (tokens, CAP), 1) == where_).astype(BF)
-        gn[...] += dot(pick, grad_in)
-        mix[...] += gate * dot(pick, result)
+        total[...] += dot(picked(col_ref, j, local), grad_in)
     store_split(gw_ref, dot(rows_ref[0], gpre_ref[...], 0, 0))
 
-    @pl.when(local == count - 1)
+    @pl.when(local == pl.num_programs(0) - 1)
     def _():
         gn_far_ref[...] = gn_acc[...].astype(BF)
-        mix_far_ref[...] = mix_acc[...].astype(BF)
-
-
-def expert_two(pos, gate, rows, act, slope, gslot, w_in, w_out, pieces):
-    tokens = pos.shape[0]
+
+
+def expert_two(cols, rows, slope, gslot, w_in, w_out, pieces):
+    tokens = cols.shape[0]
     slots = 2 * CAP
     ff = w_in.shape[2]
     whole = fixed(tokens, D)
@@ -459,32 +507,58 @@
         expert_two_kernel,
         grid=(EXP_DEV,),
         in_specs=[
-            fixed(tokens, 2 * EXP_DEV), fixed(tokens, 2 * EXP_DEV),
-            stepped(slots, D), stepped(slots, ff), stepped(slots, ff), stepped(slots, D),
+            fixed(*cols.shape), stepped(slots, D), stepped(slots, ff), stepped(slots, D),
             stepped(D, ff), stepped(ff, D),
         ],
-        out_specs=[
-            pl.BlockSpec((pieces, 1, D // pieces, ff), lambda m: (0, m, 0, 0)),
-            whole, whole, whole, whole,
-        ],
+        out_specs=[pl.BlockSpec((pieces, 1, D // pieces, ff), lambda m: (0, m, 0, 0)), whole, whole],
         out_shape=[
             jax.ShapeDtypeStruct((pieces, EXP_DEV, D // pieces, ff), BF),
             jax.ShapeDtypeStruct((tokens, D), F32),
-            jax.ShapeDtypeStruct((tokens, D), F32),
             jax.ShapeDtypeStruct((tokens, D), BF),
-            jax.ShapeDtypeStruct((tokens, D), BF),
-        ],
-        scratch_shapes=[
-            pltpu.VMEM((slots, ff), BF), pltpu.VMEM((tokens, D), F32), pltpu.VMEM((tokens, D), F32),
-        ],
+        ],
+        scratch_shapes=[pltpu.VMEM((slots, ff), BF), pltpu.VMEM((tokens, D), F32)],
         compiler_params=kernel_params(),
-        name="expert_two",
-    )(pos, gate, rows, act, slope, gslot, w_in, w_out)
+    )(cols, rows, slope, gslot, w_in, w_out)
+
+
+def expert_mix_kernel(col_ref, act_ref, wout_ref, mix_ref, mix_far_ref, mix_acc):
+    local = pl.program_id(0)
+    lanes = lax.broadcasted_iota(jnp.int32, col_ref.shape, 1)
+
+    @pl.when(local == 0)
+    def _():
+        mix_ref[...] = jnp.zeros_like(mix_ref)
+        mix_acc[...] = jnp.zeros_like(mix_acc)
+
+    for j, total in enumerate((mix_ref, mix_acc)):
+        result = dot(act_ref[0, j * CAP:(j + 1) * CAP, :], wout_ref[0]).astype(BF)
+        here = lanes == 2 * EXP_DEV + j * EXP_DEV + local
+        gate = jnp.sum(jnp.where(here, col_ref[...], 0.0), axis=1, keepdims=True)
+        total[...] += gate * dot(picked(col_ref, j, local), result)
+
+    @pl.when(local == pl.num_programs(0) - 1)
+    def _():
+        mix_far_ref[...] = mix_acc[...].astype(BF)
+
+
+def expert_mix(cols, act, w_out):
+    tokens = cols.shape[0]
+    ff = w_out.shape[1]
+    whole = fixed(tokens, D)
+    return pl.pallas_call(
+        expert_mix_kernel,
+        grid=(EXP_DEV,),
+        in_specs=[fixed(*cols.shape), stepped(2 * CAP, ff), stepped(ff, D)],
+        out_specs=[whole, whole],
+        out_shape=[jax.ShapeDtypeStruct((tokens, D), F32), jax.ShapeDtypeStruct((tokens, D), BF)],
+        scratch_shapes=[pltpu.VMEM((tokens, D), F32)],
+        compiler_params=kernel_params(),
+    )(cols, act, w_out)
 
 
 def shared_kernel(img_ref, gm_ref, win_ref, wout_ref, core_ref, *rest, tiles):
-    pieces_in, out_ref, gn_ref = rest[:tiles], rest[tiles], rest[tiles + 1]
-    gw_refs, rest = rest[tiles + 2:-6], rest[-6:]
+    pieces_in, out_ref, gn_ref = rest[:tiles], rest[tiles + 1], rest[tiles + 2]
+    gw_refs, rest = rest[tiles + 3:-6], rest[-6:]
     n2_ref, go_ref, act_ref, gs_ref, gpre_ref, sems = rest
     step = pl.program_id(0)
     ff = win_ref.shape[1]
@@ -500,7 +574,7 @@
     act = value.astype(BF)
     act_ref[here, :] = act
     out_ref[...] = dot(act, wout_ref[...])
-    gate = dot(image_hot(img_ref[...], gm_ref.shape[0]), gm_ref[...])
+    gate = dot(image_hot(img_ref[...], gm_ref.shape[1]), gm_ref[0])
     grad = (gate * go_ref[here, :].astype(F32)).astype(BF)
     gs_ref[here, :] = grad
     gpre = (slope * dot(grad, wout_ref[...], 1, 1)).astype(BF)
@@ -513,7 +587,7 @@
         store_rows(gw_refs, core_ref, dot(gs_ref[...], act_ref[...], 0, 0), slice(ff, 2 * ff))
 
 
-def shared_both(core, pieces, tiles, img_col, gate_mlp, w_in, w_out):
+def shared_both(core, pieces, tiles, img_col, mod, w_in, w_out, after):
     rows = tiles[0].shape[0]
     tokens = img_col.shape[0]
     steps = tokens // rows
@@ -525,8 +599,8 @@
         grid=(steps,),
         in_specs=[
             pl.BlockSpec((rows, 1), lambda m: (m, 0)),
-            fixed(*gate_mlp.shape), fixed(D, ff), fixed(ff, D), smem(),
-        ] + [hbm()] * len(tiles),
+            gate_spec(mod), fixed(D, ff), fixed(ff, D), smem(),
+        ] + [hbm()] * (len(tiles) + 1),
         out_specs=[moving, moving] + specs,
         out_shape=[
             jax.ShapeDtypeStruct((tokens, D), F32),
@@ -538,8 +612,7 @@
             pltpu.SemaphoreType.DMA((len(tiles),)),
         ],
         compiler_params=kernel_params(),
-        name="shared_both",
-    )(img_col, gate_mlp, w_in, w_out, core, *tiles)
+    )(img_col, mod, w_in, w_out, core, *tiles, after)
 
 
 def block(
@@ -549,10 +622,9 @@
     tokens, feat = patches.shape
     parts = D // feat
     rows = tokens // parts
-    image_count = cond.shape[0]
-    pieces = lax.axis_size("dp")
-    me = lax.axis_index("hidden")
-    core = lax.axis_index("expert")
+    pieces = lax.axis_size(DP)
+    me = lax.axis_index(HID)
+    core = lax.axis_index(EXP)
     bit_low = (me & 1) == 1
     bit_high = (me & 2) == 2
 
@@ -566,10 +638,10 @@
         ]
 
     def across(value, mask):
-        return lax.ppermute(value, "hidden", [(i, i ^ mask) for i in range(parts)])
+        return lax.ppermute(value, HID, [(i, i ^ mask) for i in range(parts)])
 
     def other_core(value):
-        return lax.ppermute(value, "expert", [(0, 1), (1, 0)])
+        return lax.ppermute(value, EXP, [(0, 1), (1, 0)])
 
     def exchanged(items):
         return [items[0]] + [across(items[m], m) for m in range(1, parts)]
@@ -585,9 +657,6 @@
     def blocks(value):
         return [value[i * rows:(i + 1) * rows] for i in range(parts)]
 
-    def to_rows(value):
-        return jnp.concatenate(turned(exchanged(turned(blocks(value)))), axis=1)
-
     def to_cols(value):
         cuts = [value[:, i * feat:(i + 1) * feat] for i in range(parts)]
         return jnp.concatenate(turned(exchanged(turned(cuts))), axis=0)
@@ -596,72 +665,58 @@
     half = lax.dynamic_slice_in_dim(packed, core * (D // 2), D // 2, axis=0)
     halves = passed_on(half)
     weights = [packed] + halves + [other_core(part) for part in halves]
-    flip = lax.axis_index("dp") if pieces == 4 else jnp.zeros((), jnp.int32)
-    core_id = jnp.stack([core, flip]).astype(jnp.int32)
-
-    x_rows = to_rows(patches)
+    flip = lax.axis_index(DP) if pieces == 4 else jnp.zeros((), jnp.int32)
+    core_id = jnp.stack([core, flip, me]).astype(jnp.int32)
+
+    def both_rows(left, right):
+        cuts = exchanged(turned(blocks(jnp.concatenate([left, right], axis=1))))
+        cuts = turned(cuts)
+        return [jnp.concatenate([cut[:, i * feat:(i + 1) * feat] for cut in cuts], axis=1) for i in range(2)]
+
+    x_rows, go_rows = both_rows(patches, grad_out)
     silu_cond = jax.nn.silu(cond.astype(F32)).astype(BF)
-    mod_own = jnp.einsum("id,dkc->ikc", silu_cond, w_ada, preferred_element_type=F32).astype(BF)
-    mod = jnp.concatenate(turned(gathered(mod_own)), axis=2).reshape(image_count, 6 * D)
-    gate_own = mod[:, 5 * D:]
-    gate_both = jnp.stack([gate_own, other_core(gate_own)])
-    go_rows = to_rows(grad_out)
+    mod_own = jnp.einsum("id,dkc->kic", silu_cond, w_ada, preferred_element_type=F32).astype(BF)
+    mod = jnp.concatenate(turned(gathered(mod_own)), axis=2)
     go_own = [go_rows] + passed_on(go_rows)
+    gate_far = other_core(mod[5])
     go_far = [other_core(tile) for tile in go_own]
 
-    seg_turned = jnp.concatenate(turned(jnp.split(seg_ids, parts, axis=0)), axis=0)
-    image_turned = jnp.concatenate(turned(jnp.split(seg_image, parts, axis=0)), axis=0)
-    seg_hot = seg_turned[:, :, None] == jnp.arange(seg_image.shape[1], dtype=jnp.int32)
-    tok_image = jnp.sum(jnp.where(seg_hot, image_turned[:, None, :], 0), axis=2).reshape(tokens)
-    routes_turned = jnp.concatenate(turned(blocks(routes)), axis=0).T
-    gates_turned = jnp.concatenate(turned(blocks(gates)), axis=0).T
-    expert_ids = jnp.arange(2 * EXP_DEV, dtype=jnp.int32)[:, None]
-    named = [routes_turned[k][None, :] == expert_ids for k in range(2)]
-    hot = named[0] | named[1]
-    slot = jnp.cumsum(hot.astype(jnp.int32), axis=1) - 1
-    pos_all = jnp.where(hot, slot, -1)
-    gate_all = jnp.where(named[0], gates_turned[0][None], jnp.where(named[1], gates_turned[1][None], 0.0))
-
-    def for_experts(table):
-        low, high = table[:EXP_DEV], table[EXP_DEV:]
-        mine = jnp.where(core == 0, low, high)
-        away = jnp.where(core == 0, high, low)
-        return mine, away
-
-    pos_mine, pos_away = for_experts(pos_all.astype(F32))
-    gate_mine, gate_away = for_experts(gate_all)
-    meta = other_core(jnp.concatenate([pos_away, gate_away, tok_image.astype(F32)[None]], axis=0))
-    pos = jnp.concatenate([pos_mine, meta[:EXP_DEV]], axis=0).astype(jnp.int32)
-    gate_rows = jnp.concatenate([gate_mine, meta[EXP_DEV:2 * EXP_DEV]], axis=0)
-    img_rows = jnp.stack([tok_image.astype(F32), meta[2 * EXP_DEV]])
-    img_col = tok_image[:, None]
-    img_own = img_col[:rows]
-    seg_row = seg_turned[:1]
-    seg_col = seg_row.reshape(rows, 1)
+    images_flat = seg_image.reshape(1, -1).astype(F32)
+    raw = jnp.concatenate(
+        [
+            routes.T.astype(F32), gates.T, seg_ids.reshape(1, tokens).astype(F32),
+            jnp.pad(images_flat, ((0, 0), (0, tokens - images_flat.shape[1]))),
+        ],
+        axis=0,
+    )
+    raw_far = other_core(raw)
+    image_ids = jnp.concatenate([images_flat, raw_far[5:, : images_flat.shape[1]]], axis=0).astype(jnp.int32)
+    table_rows, table_cols = tables(raw, raw_far, image_ids, core_id)
+    img_col = table_cols[:, 16:17].astype(jnp.int32)
+    seg_col = table_cols[:, 18:19]
+    seg_row = table_rows[18:19]
 
     ada_rows = D // (2 * pieces)
-    place = lax.axis_index("dp") * 2 + core
+    place = lax.axis_index(DP) * 2 + core
 
     def everyone(value):
         if pieces > 8 or pieces & (pieces - 1):
-            return lax.all_gather(value, ("dp", "expert"), axis=0, tiled=False)
+            return lax.all_gather(value, (DP, EXP), axis=0, tiled=False)
         own = [value]
         for m in range(1, pieces):
-            own.append(lax.ppermute(value, "dp", [(i, i ^ m) for i in range(pieces)]))
+            own.append(lax.ppermute(value, DP, [(i, i ^ m) for i in range(pieces)]))
         own = jnp.stack(own)
         return jnp.concatenate([own, other_core(own)], axis=0)
 
-    silu_mine = lax.dynamic_slice_in_dim(everyone(silu_cond), place * ada_rows, ada_rows, axis=2)
-    pos_cols, gate_cols = pos.T, gate_rows.T
     n1, qkv, ctx, attn, mid, n2 = attn_forward(
-        core_id, x_rows, img_own, mod, seg_col, seg_row, weights,
-        [pos, gate_rows, img_rows, pos_cols, gate_cols, gate_both, img_col, silu_mine], parts,
+        core_id, x_rows, img_col, mod, seg_col, seg_row, weights, [], parts,
     )
     n2_own = [n2] + passed_on(n2)
     n2_far = [other_core(tile) for tile in n2_own]
-
+    tiles = n2_own + n2_far + go_own + go_far
+    *kept, gw_out_low = expert_one(table_rows, mod, gate_far, w_expert_in, tiles, pieces, 0, [])
     shared_out, gn_shared, *gw_shared = shared_both(
-        core_id, pieces, n2_own + go_own, img_col, gate_own, w_shared_in, w_shared_out
+        core_id, pieces, n2_own + go_own, img_col, mod, w_shared_in, w_shared_out, gw_out_low
     )
 
     def core_half(parts_of):
@@ -673,31 +728,29 @@
         return parts_of[0] + other_core(parts_of[1])
 
     def over_dp(values):
-        return lax.psum_scatter(values, "dp", scatter_dimension=0, tiled=False).astype(F32)
+        return lax.psum_scatter(values, DP, scatter_dimension=0, tiled=False).astype(F32)
 
     def pieces_over_dp(values):
         if pieces != 4:
             return over_dp(values.astype(BF))
         total = values[0]
         for m in range(1, pieces):
-            moved = lax.ppermute(values[m].astype(BF), "dp", [(i, i ^ m) for i in range(pieces)])
+            moved = lax.ppermute(values[m].astype(BF), DP, [(i, i ^ m) for i in range(pieces)])
             total = total + moved.astype(F32)
         return total
 
     half_shared = core_half(gw_shared)[0]
     grad_shared = pieces_over_dp(half_shared)
 
-    tiles = n2_own + n2_far + go_own + go_far
-    *kept, gw_out_low = expert_one(pos, gate_rows, img_rows, gate_both, w_expert_in, tiles, gn_shared, pieces, 0, [])
     ge_out_low = over_dp(gw_out_low)
     *kept, gw_out_high = expert_one(
-        pos, gate_rows, img_rows, gate_both, w_expert_in, tiles, gn_shared, pieces, EXP_DEV // 2, kept
+        table_rows, mod, gate_far, w_expert_in, tiles, pieces, EXP_DEV // 2, kept
     )
     ge_out_high = over_dp(gw_out_high)
-    gw_in, gn_near, mix_near, gn_far, mix_far = expert_two(
-        pos_cols, gate_cols, *kept, w_expert_in, w_expert_out, pieces
-    )
+    slot_rows, act, slope, gslot = kept
+    gw_in, gn_near, gn_far = expert_two(table_cols, slot_rows, slope, gslot, w_expert_in, w_expert_out, pieces)
     grad_expert_in = over_dp(gw_in)
+    mix_near, mix_far = expert_mix(table_cols, act, w_expert_out)
 
     def row_total(near, far, extra):
         from_core = other_core(far).astype(F32)
@@ -712,9 +765,9 @@
     mlp = row_total(mix_near, mix_far, shared_out)
 
     gpatch, gmod_five, *gw_attn = attn_backward(
-        core_id, pieces, gn2, mid, attn, go_rows, x_rows, n1, qkv, ctx, img_own, mod, seg_col, seg_row, weights
+        core_id, pieces, gn2, mid, attn, go_rows, x_rows, n1, qkv, ctx, img_col, mod, seg_col, seg_row, weights
     )
-    out_rows, gmod_last = finish(mid, mlp, go_rows, img_own, gate_own)
+    out_rows, gmod_last = finish(mid, mlp, go_rows, img_col, mod)
     block_out = to_cols(out_rows)
     grad_patches = to_cols(gpatch)
 
@@ -723,6 +776,8 @@
     got = exchanged(cuts)
     grad_image = (got[0] + got[1] + got[2] + got[3]).astype(BF)
     image_all = everyone(grad_image)
+    silu_all = everyone(silu_cond)
+    silu_mine = lax.dynamic_slice_in_dim(silu_all, place * ada_rows, ada_rows, axis=2)
     grad_ada = jnp.einsum("gid,gkic->dkc", silu_mine, image_all, preferred_element_type=F32)
 
     attn_half = core_half(gw_attn)
@@ -746,31 +801,31 @@
 
 
 def solution(mesh):
-    rows = P(("dp", "expert"), None)
-    tiles = P(("dp", "expert"), "hidden")
+    rows = P((DP, EXP), None)
+    tiles = P((DP, EXP), HID)
     return jax.shard_map(
         block,
         mesh=mesh,
         in_specs=(
             tiles, rows, rows, rows, rows, rows, tiles,
-            P(None, None, "hidden"),
-            P(None, None, "hidden"),
-            P("hidden", None),
-            P(None, "hidden"),
-            P("hidden", None),
-            P("expert", None, "hidden"),
-            P("expert", "hidden", None),
+            P(None, None, HID),
+            P(None, None, HID),
+            P(HID, None),
+            P(None, HID),
+            P(HID, None),
+            P(EXP, None, HID),
+            P(EXP, HID, None),
         ),
         out_specs=(
             tiles,
             tiles,
-            P(("dp", "expert"), None, "hidden"),
-            P(("dp", "expert"), None, "hidden"),
-            P("hidden", ("dp", "expert")),
-            P(("dp", "expert"), "hidden"),
-            P("hidden", ("dp", "expert")),
-            P("expert", "dp", "hidden"),
-            P("expert", "hidden", "dp"),
+            P((DP, EXP), None, HID),
+            P((DP, EXP), None, HID),
+            P(HID, (DP, EXP)),
+            P((DP, EXP), HID),
+            P(HID, (DP, EXP)),
+            P(EXP, DP, HID),
+            P(EXP, HID, DP),
         ),
         check_vma=False,
     )

time: 434 us -> 411 us (0.947)
  waiting for transfers between devices: 144 us -> 111 us
  local copies, waits for them, and re-layouts: 23 us -> 28.1 us
  Pallas kernels: 132 us -> 137 us
    ppermute x73 -> x70, waiting for transfers between devices: 143 us -> 110 us  [the longest x36 55.7 us: across(): return lax.ppermute(value, HID, [(i, i ^ mask) for i in range(parts)])]
    another operation x10 -> x6, other arithmetic: 16.4 us -> 11.6 us
    pallas_call x2 -> x4, Pallas kernels: 43.6 us -> 48.2 us  [the longest x1 26.7 us: expert_two(): pl.pallas_call(expert_two_kernel, grid=(EXP_DEV,), in_specs=[fixed(*cols....]
    unnamed x122 -> x114, local copies, waits for them, and re-layouts: 12.3 us -> 16.9 us
    ppermute x73 -> x70, starting transfers between devices: 66.3 us -> 63.1 us  [the longest x36 43.2 us: across(): return lax.ppermute(value, HID, [(i, i ^ mask) for i in range(parts)])]
  transfers between devices with their start and end apart: 76 -> 73, of which waited for: 35 -> 30; matrix products, arithmetic and copies ran while one was open for 15% -> 16% of each run, Pallas kernels for 22% -> 24%
where the time goes in v2:
time: 411 us; the launch traced here: 403 us
  Pallas kernels  137 us (33%)
  waiting for transfers between devices  111 us (27%)
  starting transfers between devices  63.3 us (15%)
  other arithmetic  45.2 us (11%)
  local copies, waits for them, and re-layouts  28.1 us (7%)
  between operations  14.9 us (4%)
    ppermute x36, waiting for transfers between devices, across(): return lax.ppermute(value, HID, [(i, i ^ mask) for i in range(parts)])  55.7 us
    ppermute x36, starting transfers between devices, across(): return lax.ppermute(value, HID, [(i, i ^ mask) for i in range(parts)])  43.2 us
    pallas_call x2, Pallas kernels, expert_one(): pl.pallas_call(functools.partial(expert_one_kernel, tiles=len(tiles), fir...  39.6 us
    ppermute x6, waiting for transfers between devices, pieces_over_dp(): lax.ppermute(values[m].astype(BF), DP, [(i, i ^ m) for i in range(pieces)])  32 us
    pallas_call x1, Pallas kernels, expert_two(): pl.pallas_call(expert_two_kernel, grid=(EXP_DEV,), in_specs=[fixed(*cols....  26.7 us
    pallas_call x1, Pallas kernels, attn_backward(): pl.pallas_call(functools.partial(attn_bwd_kernel, shards=len(weights)), g...  21.4 us
    ppermute x6, waiting for transfers between devices, everyone(): own.append(lax.ppermute(value, DP, [(i, i ^ m) for i in range(pieces)]))  20 us
    pallas_call x1, Pallas kernels, shared_both(): pl.pallas_call(functools.partial(shared_kernel, tiles=len(tiles)), grid=(...  17.2 us
  transfers between devices with their start and end apart: 73, of which 30 were waited for; matrix products, arithmetic and copies ran while one was open for 16% of the time, Pallas kernels for 24%

profile of v2, /device:TPU:0, one launch (start us, length us, event | category | flops | bytes accessed | tf_op | source)
XLA Modules:
  0.0 402.9 jit_solution(2422716316485154594)
XLA Ops:
  11.2 3.0 collective-permute-start.8
  15.7 2.0 copy.36
  17.7 2.0 copy.37
  19.7 2.3 broadcast_select_fusion.15
  31.3 2.3 pad_maximum_fusion.rest_0_
  34.4 3.4 collective-permute-done.2
  51.3 2.0 shard_map.205
  53.4 4.9 %collective-permute-done.5 = bf16[6,32,192]{2,1,0:T(8,128)(2,1)S(1)} collective-permute-done((bf16[6,32,192]{2,1,0:T(8,128)(2,1)}, bf16[6,32,192]{2,1,0:T(8,128)(2,1)S(1)}, u32[]{:S(2)}, u32[]{:S(2)}) %collective-permute-start.5) | collective-permute-done | bytes 73760 | tf_op jit(solution)/shard_map/ppermute | solution.py:641
  58.8 2.6 fusion.44
  66.6 7.2 %collective-permute-done.25.rest_11_.rest_6_ = bf16[256,768]{1,0:T(8,128)(2,1)S(1)} collective-permute-done((bf16[256,768]{1,0:T(8,128)(2,1)S(1)}, bf16[256,768]{1,0:T(8,128)(2,1)S(1)}, u32[]{:S(2)}, u32[]{:S(2)}) %collective-permute-start.25) | collective-permute-done | bytes 393248 | tf_op jit(solution)/shard_map/ppermute | solution.py:641
  76.9 10.6 %shard_map.206 = (bf16[256,768]{1,0:T(8,128)(2,1)}, bf16[4,256,576]{2,1,0:T(8,128)(2,1)}, bf16[4,256,192]{2,1,0:T(8,128)(2,1)}, f32[256,768]{1,0:T(8,128)}, f32[...) custom-call(bf16[256,768]{1,0:T(8,128)(2,1)} %pad_maximum_fusion.3.x_ref, s32[1024,1]{1,0:T(8,128)} %get-tuple-element.159.img_ref, ...), custom_call_target="tpu_custom_call" | custom-call | tf_op jit(solution)/shard_map/pallas_call | solution.py:117
  87.5 1.8 collective-permute-start.17
  93.6 3.8 collective-permute-done.17.rest_2_
  102.6 3.8 collective-permute-done.19.rest_4_
  110.6 20.3 %shard_map.207 = (bf16[4,768,768]{2,1,0:T(8,128)(2,1)}, bf16[4,768,768]{2,1,0:T(8,128)(2,1)}, f32[4,768,768]{2,1,0:T(8,128)}, bf16[4,768,768]{2,1,0:T(8,128)(2,1)}, bf16[4,2,192,768]{3,2,1,0:T(8,128)(2,1)}) custom-call(f32[24,1024]{1,0:T(8,128)} %get-tuple-element.43.row_ref, bf16[4,768,768]{2,1,0:T(8,128)(2,1)} %win_ref.7, ...), custom_call_target="tpu_custom_call" | custom-call | tf_op jit(solution)/shard_map/pallas_call | solution.py:446
  131.0 19.2 %shard_map.208 = (bf16[4,768,768]{2,1,0:T(8,128)(2,1)}, bf16[4,768,768]{2,1,0:T(8,128)(2,1)}, f32[4,768,768]{2,1,0:T(8,128)}, bf16[4,768,768]{2,1,0:T(8,128)(2,1)}, bf16[4,2,192,768]{3,2,1,0:T(8,128)(2,1)}) custom-call(f32[24,1024]{1,0:T(8,128)} %get-tuple-element.43.row_ref, ...), custom_call_target="tpu_custom_call", output_to_operand_aliasing={{0}: (24, {}), {1}: (25, {}), {2}: (26, {}), {3}: (27, {})} | custom-call | tf_op jit(solution)/shard_map/pallas_call | solution.py:446
  151.0 26.7 %shard_map.212 = (bf16[4,4,192,768]{3,2,1,0:T(8,128)(2,1)}, f32[1024,768]{1,0:T(8,128)}, bf16[1024,768]{1,0:T(8,128)(2,1)}) custom-call(f32[1024,24]{1,0:T(8,128)} %get-tuple-element.42.col_ref, bf16[4,768,768]{2,1,0:T(8,128)(2,1)} %get-tuple-element.56.rows_ref, f32[4,768,768]{2,1,0:T(8,128)} %get-tuple-element.57.slope_ref, ...), custom_call_target="tpu_custom_call" | custom-call | tf_op jit(solution)/shard_map/pallas_call | solution.py:506
  177.9 16.7 %shard_map.209 = (f32[1024,768]{1,0:T(8,128)}, bf16[1024,768]{1,0:T(8,128)(2,1)}) custom-call(f32[1024,24]{1,0:T(8,128)} %get-tuple-element.42.col_ref, bf16[4,768,768]{2,1,0:T(8,128)(2,1)} %get-tuple-element.50.act_ref, bf16[4,768,768]{2,1,0:T(8,128)(2,1)} %wout_ref.5), custom_call_target="tpu_custom_call" | custom-call | tf_op jit(solution)/shard_map/pallas_call | solution.py:548
  195.1 3.6 collective-permute-start.50
  201.0 2.6 collective-permute-done.49
  205.6 17.2 %shard_map.210 = (f32[1024,768]{1,0:T(8,128)}, f32[1024,768]{1,0:T(8,128)}, f32[1,4,96,1536]{3,2,1,0:T(8,128)}, f32[1,4,96,1536]{3,2,1,0:T(8,128)}) custom-call(s32[1024,1]{1,0:T(8,128)} %get-tuple-element.159.img_ref, bf16[6,32,768]{2,1,0:T(8,128)(2,1)} %pad_maximum_fusion.6.mod_ref.gm_ref.gate_ref, bf16[768,768]{1,0:T(8,128)(2,1)} %win_ref.6, ...), custom_call_target="tpu_custom_call" | custom-call | tf_op jit(solution)/shard_map/pallas_call | solution.py:597
  222.9 3.1 fusion.37
  226.9 1.8 collective-permute-start.44
  229.7 2.1 fusion.38
  233.4 4.7 %collective-permute-done.42 = bf16[256,768]{1,0:T(8,128)(2,1)S(1)} collective-permute-done((bf16[256,768]{1,0:T(8,128)(2,1)S(1)}, bf16[256,768]{1,0:T(8,128)(2,1)S(1)}, u32[]{:S(2)}, u32[]{:S(2)}) %collective-permute-start.42) | collective-permute-done | bytes 393248 | tf_op jit(solution)/shard_map/ppermute | solution.py:641
  239.3 7.8 %collective-permute-done.44 = bf16[256,768]{1,0:T(8,128)(2,1)S(1)} collective-permute-done((bf16[256,768]{1,0:T(8,128)(2,1)S(1)}, bf16[256,768]{1,0:T(8,128)(2,1)S(1)}, u32[]{:S(2)}, u32[]{:S(2)}) %collective-permute-start.44) | collective-permute-done | bytes 393248 | tf_op jit(solution)/shard_map/ppermute | solution.py:641
  249.2 21.4 %shard_map.213 = (bf16[256,768]{1,0:T(8,128)(2,1)}, f32[5,32,768]{2,1,0:T(8,128)}, f32[4,4,96,768]{3,2,1,0:T(8,128)}, f32[4,4,96,768]{3,2,1,0:T(8,128)}) custom-call(f32[256,768]{1,0:T(8,128)} %fusion.5.gn2_ref, f32[256,768]{1,0:T(8,128)} %get-tuple-element.44.mid_ref, f32[256,768]{1,0:T(8,128)} %get-tuple-element.62.attn_ref, bf16[256,768]{1,0:T(8,128)(2,1)} %copy-done.2, ...), custom_call_target="tpu_custom_call" | custom-call | tf_op jit(solution)/shard_map/pallas_call | solution.py:296
  273.4 2.3 fusion.7.mlp_ref
  275.7 2.7 shard_map.211
  293.4 2.4 collective-permute-done.45
  299.5 5.8 %collective-permute-done.53 = f32[6,32,192]{2,1,0:T(8,128)S(1)} collective-permute-done((f32[6,32,192]{2,1,0:T(8,128)}, f32[6,32,192]{2,1,0:T(8,128)S(1)}, u32[]{:S(2)}, u32[]{:S(2)}) %collective-permute-start.53) | collective-permute-done | bytes 147488 | tf_op jit(solution)/shard_map/ppermute | solution.py:641
  306.1 2.1 collective-permute-start.57
  308.2 2.3 collective-permute-start.55
  311.5 4.2 %collective-permute-done.57 = bf16[6,32,192]{2,1,0:T(8,128)(2,1)S(1)} collective-permute-done((bf16[6,32,192]{2,1,0:T(8,128)(2,1)S(1)}, bf16[6,32,192]{2,1,0:T(8,128)(2,1)S(1)}, u32[]{:S(2)}, u32[]{:S(2)}) %collective-permute-start.57) | collective-permute-done | bytes 73760 | tf_op jit(solution)/shard_map/ppermute | solution.py:707
  315.6 11.7 %collective-permute-done.56 = bf16[6,32,192]{2,1,0:T(8,128)(2,1)S(1)} collective-permute-done((bf16[6,32,192]{2,1,0:T(8,128)(2,1)S(1)}, bf16[6,32,192]{2,1,0:T(8,128)(2,1)S(1)}, u32[]{:S(2)}, u32[]{:S(2)}) %collective-permute-start.56) | collective-permute-done | bytes 73760 | tf_op jit(solution)/shard_map/ppermute | solution.py:707
  329.5 2.3 fusion.29
  332.6 2.8 collective-permute-start.68
  335.5 2.1 convolution_bitcast_fusion
  337.6 3.1 fusion.32
  343.5 3.1 collective-permute-done.67
  346.6 2.5 collective-permute-start.61
  349.0 6.2 %collective-permute-done.69 = bf16[96,1536]{1,0:T(8,128)(2,1)S(1)} collective-permute-done((bf16[96,1536]{1,0:T(8,128)(2,1)S(1)}, bf16[96,1536]{1,0:T(8,128)(2,1)S(1)}, u32[]{:S(2)}, u32[]{:S(2)}) %collective-permute-start.69) | collective-permute-done | bytes 294944 | tf_op jit(solution)/shard_map/ppermute | solution.py:738
  355.2 13.3 %collective-permute-done.68 = bf16[96,1536]{1,0:T(8,128)(2,1)S(1)} collective-permute-done((bf16[96,1536]{1,0:T(8,128)(2,1)S(1)}, bf16[96,1536]{1,0:T(8,128)(2,1)S(1)}, u32[]{:S(2)}, u32[]{:S(2)}) %collective-permute-start.68) | collective-permute-done | bytes 294944 | tf_op jit(solution)/shard_map/ppermute | solution.py:738
  369.5 5.6 %collective-permute-done.61 = bf16[4,96,768]{2,1,0:T(8,128)(2,1)S(1)} collective-permute-done((bf16[4,96,768]{2,1,0:T(8,128)(2,1)S(1)}, bf16[4,96,768]{2,1,0:T(8,128)(2,1)S(1)}, u32[]{:S(2)}, u32[]{:S(2)}) %collective-permute-start.61) | collective-permute-done | bytes 589856 | tf_op jit(solution)/shard_map/ppermute | solution.py:641
  378.9 2.8 convert_bitcast_fusion
  382.6 2.5 collective-permute-done.65
  385.1 6.0 %collective-permute-done.64 = bf16[96,768]{1,0:T(8,128)(2,1)S(1)} collective-permute-done((bf16[96,768]{1,0:T(8,128)(2,1)S(1)}, bf16[96,768]{1,0:T(8,128)(2,1)S(1)}, u32[]{:S(2)}, u32[]{:S(2)}) %collective-permute-start.64) | collective-permute-done | bytes 147488 | tf_op jit(solution)/shard_map/ppermute | solution.py:738
  393.1 2.9 bitcast_convert_fusion
  (291 shorter events, 100.3 us)
Async XLA Ops:
  7.2 371.7 %reduce-scatter.8.cloned.1.call-start = ((), (), s32[]{:S(2)}) async-start(), calls=%async_computation.5 | async-start | bytes 2949120 | tf_op jit(solution)/shard_map/reduce_scatter | solution.py:731
  11.2 33.6 %collective-permute-start.8 = (bf16[384,768]{1,0:T(8,128)(2,1)}, bf16[384,768]{1,0:T(8,128)(2,1)S(1)}, u32[]{:S(2)}, u32[]{:S(2)}) collective-permute-start(bf16[384,768]{1,0:T(8,128)(2,1)} %fusion.8), channel_id=1, source_target_pairs={{0,2},{1,3},{2,0},{3,1},{4,6},{5,7},{6,4},{7,5},{8,10},{9,11},{10,... | collective-permute-start | bytes 1769480 | tf_op jit(solution)/shard_map/ppermute | solution.py:641
  14.2 31.7 %collective-permute-start.7 = (bf16[384,768]{1,0:T(8,128)(2,1)}, bf16[384,768]{1,0:T(8,128)(2,1)}, u32[]{:S(2)}, u32[]{:S(2)}) collective-permute-start(bf16[384,768]{1,0:T(8,128)(2,1)} %fusion.8), channel_id=1, source_target_pairs={{0,1},{1,0},{2,3},{3,2},{4,5},{5,4},{6,7},{7,6},{8,9},{9,8},{10,11... | collective-permute-start | bytes 1769480 | tf_op jit(solution)/shard_map/ppermute | solution.py:641
  22.0 12.4 %collective-permute-start = (bf16[256,384]{1,0:T(8,128)(2,1)}, bf16[256,384]{1,0:T(8,128)(2,1)}, u32[]{:S(2)}, u32[]{:S(2)}) collective-permute-start(bf16[256,384]{1,0:T(8,128)(2,1)} %get-tuple-element.122), channel_id=1, source_target_pairs={{0,3},{1,2},{2,1},{3,0},{4,7},{5,6},{6,5},{7,4},{8,11},{9,10},{10,... | collective-permute-start | bytes 589832 | tf_op jit(solution)/shard_map/ppermute | solution.py:641
  23.5 14.3 %collective-permute-start.2 = (bf16[256,384]{1,0:T(8,128)(2,1)}, bf16[256,384]{1,0:T(8,128)(2,1)}, u32[]{:S(2)}, u32[]{:S(2)}) collective-permute-start(bf16[256,384]{1,0:T(8,128)(2,1)} %get-tuple-element.143), channel_id=1, source_target_pairs={{0,1},{1,0},{2,3},{3,2},{4,5},{5,4},{6,7},{7,6},{8,9},{9,8},{10,11... | collective-permute-start | bytes 589832 | tf_op jit(solution)/shard_map/ppermute | solution.py:641
  24.8 14.4 %collective-permute-start.1 = (bf16[256,384]{1,0:T(8,128)(2,1)}, bf16[256,384]{1,0:T(8,128)(2,1)}, u32[]{:S(2)}, u32[]{:S(2)}) collective-permute-start(bf16[256,384]{1,0:T(8,128)(2,1)} %get-tuple-element.144), channel_id=1, source_target_pairs={{0,2},{1,3},{2,0},{3,1},{4,6},{5,7},{6,4},{7,5},{8,10},{9,11},{10,... | collective-permute-start | bytes 589832 | tf_op jit(solution)/shard_map/ppermute | solution.py:641
  34.4 8.9 %collective-permute-start.3 = (f32[6,1024]{1,0:T(8,128)S(1)}, f32[6,1024]{1,0:T(8,128)S(1)}, u32[]{:S(2)}, u32[]{:S(2)}) collective-permute-start(f32[6,1024]{1,0:T(8,128)S(1)} %select_maximum_fusion.own_ref), channel_id=1, source_target_pairs={{0,4},{4,0},{1,5},{5,1},{2,6},{6,2},{3,7},{7,3},{8,12},{12,8},{9,1... | collective-permute-start | bytes 73736 | tf_op jit(solution)/shard_map/ppermute | solution.py:644
  37.7 11.5 %collective-permute-start.6 = (bf16[6,32,192]{2,1,0:T(8,128)(2,1)}, bf16[6,32,192]{2,1,0:T(8,128)(2,1)S(1)}, u32[]{:S(2)}, u32[]{:S(2)}) collective-permute-start(bf16[6,32,192]{2,1,0:T(8,128)(2,1)} %fusion.3), channel_id=1, source_target_pairs={{0,1},{1,0},{2,3},{3,2},{4,5},{5,4},{6,7},{7,6},{8,9},{9,8},{10,11... | collective-permute-start | bytes 221192 | tf_op jit(solution)/shard_map/ppermute | solution.py:641
  42.1 20.8 %collective-permute-start.26 = (bf16[256,768]{1,0:T(8,128)(2,1)S(1)}, bf16[256,768]{1,0:T(8,128)(2,1)S(1)}, u32[]{:S(2)}, u32[]{:S(2)}) collective-permute-start(bf16[256,768]{1,0:T(8,128)(2,1)S(1)} %pad_maximum_fusion.4.rest_10_.rest_5_.go_ref), channel_id=1, source_target_pairs={{0,2},{1,3},{2,0},{3,1},{4,6},{5,7},{6,4},{7,5},{8,10},{9,11},{10,... | collective-permute-start | bytes 1179656 | tf_op jit(solution)/shard_map/ppermute | solution.py:641
  43.2 15.1 %collective-permute-start.5 = (bf16[6,32,192]{2,1,0:T(8,128)(2,1)}, bf16[6,32,192]{2,1,0:T(8,128)(2,1)S(1)}, u32[]{:S(2)}, u32[]{:S(2)}) collective-permute-start(bf16[6,32,192]{2,1,0:T(8,128)(2,1)} %fusion.3), channel_id=1, source_target_pairs={{0,2},{1,3},{2,0},{3,1},{4,6},{5,7},{6,4},{7,5},{8,10},{9,11},{10,... | collective-permute-start | bytes 221192 | tf_op jit(solution)/shard_map/ppermute | solution.py:641
  44.8 13.6 %collective-permute-start.4 = (bf16[6,32,192]{2,1,0:T(8,128)(2,1)}, bf16[6,32,192]{2,1,0:T(8,128)(2,1)S(1)}, u32[]{:S(2)}, u32[]{:S(2)}) collective-permute-start(bf16[6,32,192]{2,1,0:T(8,128)(2,1)} %fusion.3), channel_id=1, source_target_pairs={{0,3},{1,2},{2,1},{3,0},{4,7},{5,6},{6,5},{7,4},{8,11},{9,10},{10,... | collective-permute-start | bytes 221192 | tf_op jit(solution)/shard_map/ppermute | solution.py:641
  45.8 17.5 %collective-permute-start.10 = (bf16[192,768]{1,0:T(8,128)(2,1)}, bf16[192,768]{1,0:T(8,128)(2,1)S(1)}, u32[]{:S(2)}, u32[]{:S(2)}) collective-permute-start(bf16[192,768]{1,0:T(8,128)(2,1)} %slice.267), channel_id=1, source_target_pairs={{0,1},{1,0},{2,3},{3,2},{4,5},{5,4},{6,7},{7,6},{8,9},{9,8},{10,11... | collective-permute-start | bytes 884744 | tf_op jit(solution)/shard_map/ppermute | solution.py:641
  49.2 14.1 %collective-permute-start.9 = (bf16[192,768]{1,0:T(8,128)(2,1)}, bf16[192,768]{1,0:T(8,128)(2,1)}, u32[]{:S(2)}, u32[]{:S(2)}) collective-permute-start(bf16[192,768]{1,0:T(8,128)(2,1)} %slice.266), channel_id=1, source_target_pairs={{0,2},{1,3},{2,0},{3,1},{4,6},{5,7},{6,4},{7,5},{8,10},{9,11},{10,... | collective-permute-start | bytes 884744 | tf_op jit(solution)/shard_map/ppermute | solution.py:641
  58.3 17.0 %collective-permute-start.12 = (bf16[384,768]{1,0:T(8,128)(2,1)S(1)}, bf16[384,768]{1,0:T(8,128)(2,1)S(1)}, u32[]{:S(2)}, u32[]{:S(2)}) collective-permute-start(bf16[384,768]{1,0:T(8,128)(2,1)S(1)} %collective-permute-done.8.rest_2_), channel_id=1, source_target_pairs={{0,4},{4,0},{1,5},{5,1},{2,6},{6,2},{3,7},{7,3},{8,12},{12,8},{9,1... | collective-permute-start | bytes 1769480 | tf_op jit(solution)/shard_map/ppermute | solution.py:644
  58.3 17.1 %collective-permute-start.11 = (bf16[384,768]{1,0:T(8,128)(2,1)}, bf16[384,768]{1,0:T(8,128)(2,1)S(1)}, u32[]{:S(2)}, u32[]{:S(2)}) collective-permute-start(bf16[384,768]{1,0:T(8,128)(2,1)} %collective-permute-done.7.rest_1_), channel_id=1, source_target_pairs={{0,4},{4,0},{1,5},{5,1},{2,6},{6,2},{3,7},{7,3},{8,12},{12,8},{9,1... | collective-permute-start | bytes 1769480 | tf_op jit(solution)/shard_map/ppermute | solution.py:644
  62.8 11.0 %collective-permute-start.25 = (bf16[256,768]{1,0:T(8,128)(2,1)S(1)}, bf16[256,768]{1,0:T(8,128)(2,1)S(1)}, u32[]{:S(2)}, u32[]{:S(2)}) collective-permute-start(bf16[256,768]{1,0:T(8,128)(2,1)S(1)} %pad_maximum_fusion.4.rest_10_.rest_5_.go_ref), channel_id=1, source_target_pairs={{0,1},{1,0},{2,3},{3,2},{4,5},{5,4},{6,7},{7,6},{8,9},{9,8},{10,11... | collective-permute-start | bytes 1179656 | tf_op jit(solution)/shard_map/ppermute | solution.py:641
  63.4 11.7 %collective-permute-start.14 = (bf16[192,768]{1,0:T(8,128)(2,1)S(1)}, bf16[192,768]{1,0:T(8,128)(2,1)}, u32[]{:S(2)}, u32[]{:S(2)}) collective-permute-start(bf16[192,768]{1,0:T(8,128)(2,1)S(1)} %collective-permute-done.10.rest_4_), channel_id=1, source_target_pairs={{0,4},{4,0},{1,5},{5,1},{2,6},{6,2},{3,7},{7,3},{8,12},{12,8},{9,1... | collective-permute-start | bytes 884744 | tf_op jit(solution)/shard_map/ppermute | solution.py:644
  63.4 12.0 %collective-permute-start.13 = (bf16[192,768]{1,0:T(8,128)(2,1)}, bf16[192,768]{1,0:T(8,128)(2,1)S(1)}, u32[]{:S(2)}, u32[]{:S(2)}) collective-permute-start(bf16[192,768]{1,0:T(8,128)(2,1)} %collective-permute-done.9.rest_3_), channel_id=1, source_target_pairs={{0,4},{4,0},{1,5},{5,1},{2,6},{6,2},{3,7},{7,3},{8,12},{12,8},{9,1... | collective-permute-start | bytes 884744 | tf_op jit(solution)/shard_map/ppermute | solution.py:644
  73.8 19.2 %collective-permute-start.28 = (bf16[128,768]{1,0:T(8,128)(2,1)S(1)}, bf16[128,768]{1,0:T(8,128)(2,1)S(1)}, u32[]{:S(2)}, u32[]{:S(2)}) collective-permute-start(bf16[128,768]{1,0:T(8,128)(2,1)S(1)} %slice.276), channel_id=1, source_target_pairs={{0,1},{1,0},{2,3},{3,2},{4,5},{5,4},{6,7},{7,6},{8,9},{9,8},{10,11... | collective-permute-start | bytes 589832 | tf_op jit(solution)/shard_map/ppermute | solution.py:641
  75.1 18.3 %collective-permute-start.27 = (bf16[128,768]{1,0:T(8,128)(2,1)}, bf16[128,768]{1,0:T(8,128)(2,1)S(1)}, u32[]{:S(2)}, u32[]{:S(2)}) collective-permute-start(bf16[128,768]{1,0:T(8,128)(2,1)} %slice.275), channel_id=1, source_target_pairs={{0,2},{1,3},{2,0},{3,1},{4,6},{5,7},{6,4},{7,5},{8,10},{9,11},{10,... | collective-permute-start | bytes 589832 | tf_op jit(solution)/shard_map/ppermute | solution.py:641
  87.5 10.0 %collective-permute-start.17 = (bf16[256,768]{1,0:T(8,128)(2,1)}, bf16[256,768]{1,0:T(8,128)(2,1)S(1)}, u32[]{:S(2)}, u32[]{:S(2)}) collective-permute-start(bf16[256,768]{1,0:T(8,128)(2,1)} %get-tuple-element.45.rest_0_), channel_id=1, source_target_pairs={{0,2},{1,3},{2,0},{3,1},{4,6},{5,7},{6,4},{7,5},{8,10},{9,11},{10,... | collective-permute-start | bytes 1179656 | tf_op jit(solution)/shard_map/ppermute | solution.py:641
  89.3 9.5 %collective-permute-start.16 = (bf16[256,768]{1,0:T(8,128)(2,1)}, bf16[256,768]{1,0:T(8,128)(2,1)S(1)}, u32[]{:S(2)}, u32[]{:S(2)}) collective-permute-start(bf16[256,768]{1,0:T(8,128)(2,1)} %get-tuple-element.45.rest_0_), channel_id=1, source_target_pairs={{0,1},{1,0},{2,3},{3,2},{4,5},{5,4},{6,7},{7,6},{8,9},{9,8},{10,11... | collective-permute-start | bytes 1179656 | tf_op jit(solution)/shard_map/ppermute | solution.py:641
  98.9 8.7 %collective-permute-start.20 = (bf16[256,768]{1,0:T(8,128)(2,1)}, bf16[256,768]{1,0:T(8,128)(2,1)S(1)}, u32[]{:S(2)}, u32[]{:S(2)}) collective-permute-start(bf16[256,768]{1,0:T(8,128)(2,1)} %get-tuple-element.45.rest_0_), channel_id=1, source_target_pairs={{0,4},{4,0},{1,5},{5,1},{2,6},{6,2},{3,7},{7,3},{8,12},{12,8},{9,1... | collective-permute-start | bytes 1179656 | tf_op jit(solution)/shard_map/ppermute | solution.py:644
  150.2 228.7 %reduce-scatter.6.cloned.1.call-start = ((), (), s32[]{:S(2)}) async-start(), calls=%async_computation.4 | async-start | bytes 2949120 | tf_op jit(solution)/shard_map/reduce_scatter | solution.py:731
  151.0 242.1 %reduce-scatter.4.cloned.1.call-start = ((), (), s32[]{:S(2)}) async-start(), calls=%async_computation.3 | async-start | bytes 5898240 | tf_op jit(solution)/shard_map/reduce_scatter | solution.py:731
  177.8 45.1 %collective-permute-start.41 = (bf16[1024,768]{1,0:T(8,128)(2,1)}, bf16[1024,768]{1,0:T(8,128)(2,1)}, u32[]{:S(2)}, u32[]{:S(2)}) collective-permute-start(bf16[1024,768]{1,0:T(8,128)(2,1)} %get-tuple-element.61), channel_id=1, source_target_pairs={{0,4},{4,0},{1,5},{5,1},{2,6},{6,2},{3,7},{7,3},{8,12},{12,8},{9,1... | collective-permute-start | bytes 4718600 | tf_op jit(solution)/shard_map/ppermute | solution.py:644
  194.6 35.0 %collective-permute-start.34 = (bf16[1024,768]{1,0:T(8,128)(2,1)}, bf16[1024,768]{1,0:T(8,128)(2,1)}, u32[]{:S(2)}, u32[]{:S(2)}) collective-permute-start(bf16[1024,768]{1,0:T(8,128)(2,1)} %get-tuple-element.54), channel_id=1, source_target_pairs={{0,4},{4,0},{1,5},{5,1},{2,6},{6,2},{3,7},{7,3},{8,12},{12,8},{9,1... | collective-permute-start | bytes 4718600 | tf_op jit(solution)/shard_map/ppermute | solution.py:644
  204.4 66.9 %collective-permute-start.51 = (bf16[4,32,768]{2,1,0:T(8,128)(2,1)}, bf16[4,32,768]{2,1,0:T(8,128)(2,1)}, u32[]{:S(2)}, u32[]{:S(2)}) collective-permute-start(bf16[4,32,768]{2,1,0:T(8,128)(2,1)} %pad_maximum_fusion.9), channel_id=1, source_target_pairs={{0,4},{4,0},{1,5},{5,1},{2,6},{6,2},{3,7},{7,3},{8,12},{12,8},{9,1... | collective-permute-start | bytes 589832 | tf_op jit(solution)/shard_map/ppermute | solution.py:644
  226.1 12.1 %collective-permute-start.42 = (bf16[256,768]{1,0:T(8,128)(2,1)S(1)}, bf16[256,768]{1,0:T(8,128)(2,1)S(1)}, u32[]{:S(2)}, u32[]{:S(2)}) collective-permute-start(bf16[256,768]{1,0:T(8,128)(2,1)S(1)} %get-tuple-element.130), channel_id=1, source_target_pairs={{0,1},{1,0},{2,3},{3,2},{4,5},{5,4},{6,7},{7,6},{8,9},{9,8},{10,11... | collective-permute-start | bytes 1179656 | tf_op jit(solution)/shard_map/ppermute | solution.py:641
  226.9 20.2 %collective-permute-start.44 = (bf16[256,768]{1,0:T(8,128)(2,1)S(1)}, bf16[256,768]{1,0:T(8,128)(2,1)S(1)}, u32[]{:S(2)}, u32[]{:S(2)}) collective-permute-start(bf16[256,768]{1,0:T(8,128)(2,1)S(1)} %get-tuple-element.131), channel_id=1, source_target_pairs={{0,3},{1,2},{2,1},{3,0},{4,7},{5,6},{6,5},{7,4},{8,11},{9,10},{10,... | collective-permute-start | bytes 1179656 | tf_op jit(solution)/shard_map/ppermute | solution.py:641
  228.7 19.4 %collective-permute-start.43 = (bf16[256,768]{1,0:T(8,128)(2,1)S(1)}, bf16[256,768]{1,0:T(8,128)(2,1)S(1)}, u32[]{:S(2)}, u32[]{:S(2)}) collective-permute-start(bf16[256,768]{1,0:T(8,128)(2,1)S(1)} %get-tuple-element.132), channel_id=1, source_target_pairs={{0,2},{1,3},{2,0},{3,1},{4,6},{5,7},{6,4},{7,5},{8,10},{9,11},{10,... | collective-permute-start | bytes 1179656 | tf_op jit(solution)/shard_map/ppermute | solution.py:641
  232.6 40.7 %collective-permute-start.35 = (bf16[256,768]{1,0:T(8,128)(2,1)}, bf16[256,768]{1,0:T(8,128)(2,1)}, u32[]{:S(2)}, u32[]{:S(2)}) collective-permute-start(bf16[256,768]{1,0:T(8,128)(2,1)} %get-tuple-element.133), channel_id=1, source_target_pairs={{0,1},{1,0},{2,3},{3,2},{4,5},{5,4},{6,7},{7,6},{8,9},{9,8},{10,11... | collective-permute-start | bytes 1179656 | tf_op jit(solution)/shard_map/ppermute | solution.py:641
  238.2 35.2 %collective-permute-start.37 = (bf16[256,768]{1,0:T(8,128)(2,1)S(1)}, bf16[256,768]{1,0:T(8,128)(2,1)}, u32[]{:S(2)}, u32[]{:S(2)}) collective-permute-start(bf16[256,768]{1,0:T(8,128)(2,1)S(1)} %get-tuple-element.134), channel_id=1, source_target_pairs={{0,3},{1,2},{2,1},{3,0},{4,7},{5,6},{6,5},{7,4},{8,11},{9,10},{10,... | collective-permute-start | bytes 1179656 | tf_op jit(solution)/shard_map/ppermute | solution.py:641
  247.2 26.2 %collective-permute-start.36 = (bf16[256,768]{1,0:T(8,128)(2,1)S(1)}, bf16[256,768]{1,0:T(8,128)(2,1)}, u32[]{:S(2)}, u32[]{:S(2)}) collective-permute-start(bf16[256,768]{1,0:T(8,128)(2,1)S(1)} %get-tuple-element.135), channel_id=1, source_target_pairs={{0,2},{1,3},{2,0},{3,1},{4,6},{5,7},{6,4},{7,5},{8,10},{9,11},{10,... | collective-permute-start | bytes 1179656 | tf_op jit(solution)/shard_map/ppermute | solution.py:641
  270.5 67.0 %collective-permute-start.59 = (f32[4,4,96,768]{3,2,1,0:T(8,128)}, f32[4,4,96,768]{3,2,1,0:T(8,128)}, u32[]{:S(2)}, u32[]{:S(2)}) collective-permute-start(f32[4,4,96,768]{3,2,1,0:T(8,128)} %get-tuple-element.70), channel_id=1, source_target_pairs={{0,4},{4,0},{1,5},{5,1},{2,6},{6,2},{3,7},{7,3},{8,12},{12,8},{9,1... | collective-permute-start | bytes 14155784 | tf_op jit(solution)/shard_map/ppermute | solution.py:644
  272.9 56.6 %collective-permute-start.66 = (f32[1,4,96,1536]{3,2,1,0:T(8,128)}, f32[1,4,96,1536]{3,2,1,0:T(8,128)}, u32[]{:S(2)}, u32[]{:S(2)}) collective-permute-start(f32[1,4,96,1536]{3,2,1,0:T(8,128)} %get-tuple-element.72), channel_id=1, source_target_pairs={{0,4},{4,0},{1,5},{5,1},{2,6},{6,2},{3,7},{7,3},{8,12},{12,8},{9,1... | collective-permute-start | bytes 7077896 | tf_op jit(solution)/shard_map/ppermute | solution.py:644
  295.8 9.5 %collective-permute-start.53 = (f32[6,32,192]{2,1,0:T(8,128)}, f32[6,32,192]{2,1,0:T(8,128)S(1)}, u32[]{:S(2)}, u32[]{:S(2)}) collective-permute-start(f32[6,32,192]{2,1,0:T(8,128)} %get-tuple-element.141), channel_id=1, source_target_pairs={{0,2},{1,3},{2,0},{3,1},{4,6},{5,7},{6,4},{7,5},{8,10},{9,11},{10,... | collective-permute-start | bytes 442376 | tf_op jit(solution)/shard_map/ppermute | solution.py:641
  306.1 9.6 %collective-permute-start.57 = (bf16[6,32,192]{2,1,0:T(8,128)(2,1)S(1)}, bf16[6,32,192]{2,1,0:T(8,128)(2,1)S(1)}, u32[]{:S(2)}, u32[]{:S(2)}) collective-permute-start(bf16[6,32,192]{2,1,0:T(8,128)(2,1)S(1)} %get-tuple-element.102), channel_id=1, source_target_pairs={{0,24},{8,16},{16,8},{24,0},{1,25},{9,17},{17,9},{25,1},{2,26},{10... | collective-permute-start | bytes 221192 | tf_op jit(solution)/shard_map/ppermute | solution.py:707
  308.1 19.2 %collective-permute-start.56 = (bf16[6,32,192]{2,1,0:T(8,128)(2,1)S(1)}, bf16[6,32,192]{2,1,0:T(8,128)(2,1)S(1)}, u32[]{:S(2)}, u32[]{:S(2)}) collective-permute-start(bf16[6,32,192]{2,1,0:T(8,128)(2,1)S(1)} %get-tuple-element.102), channel_id=1, source_target_pairs={{0,16},{8,24},{16,0},{24,8},{1,17},{9,25},{17,1},{25,9},{2,18},{10... | collective-permute-start | bytes 221192 | tf_op jit(solution)/shard_map/ppermute | solution.py:707
  308.2 19.1 %collective-permute-start.55 = (bf16[6,32,192]{2,1,0:T(8,128)(2,1)S(1)}, bf16[6,32,192]{2,1,0:T(8,128)(2,1)S(1)}, u32[]{:S(2)}, u32[]{:S(2)}) collective-permute-start(bf16[6,32,192]{2,1,0:T(8,128)(2,1)S(1)} %get-tuple-element.102), channel_id=1, source_target_pairs={{0,8},{8,0},{16,24},{24,16},{1,9},{9,1},{17,25},{25,17},{2,10},{10... | collective-permute-start | bytes 221192 | tf_op jit(solution)/shard_map/ppermute | solution.py:707
  331.9 14.7 %collective-permute-start.67 = (bf16[96,1536]{1,0:T(8,128)(2,1)S(1)}, bf16[96,1536]{1,0:T(8,128)(2,1)S(1)}, u32[]{:S(2)}, u32[]{:S(2)}) collective-permute-start(bf16[96,1536]{1,0:T(8,128)(2,1)S(1)} %get-tuple-element.138), channel_id=1, source_target_pairs={{0,8},{8,0},{16,24},{24,16},{1,9},{9,1},{17,25},{25,17},{2,10},{10... | collective-permute-start | bytes 884744 | tf_op jit(solution)/shard_map/ppermute | solution.py:738
  331.9 23.3 %collective-permute-start.69 = (bf16[96,1536]{1,0:T(8,128)(2,1)S(1)}, bf16[96,1536]{1,0:T(8,128)(2,1)S(1)}, u32[]{:S(2)}, u32[]{:S(2)}) collective-permute-start(bf16[96,1536]{1,0:T(8,128)(2,1)S(1)} %get-tuple-element.139), channel_id=1, source_target_pairs={{0,24},{8,16},{16,8},{24,0},{1,25},{9,17},{17,9},{25,1},{2,26},{10... | collective-permute-start | bytes 884744 | tf_op jit(solution)/shard_map/ppermute | solution.py:738
  332.6 35.9 %collective-permute-start.68 = (bf16[96,1536]{1,0:T(8,128)(2,1)S(1)}, bf16[96,1536]{1,0:T(8,128)(2,1)S(1)}, u32[]{:S(2)}, u32[]{:S(2)}) collective-permute-start(bf16[96,1536]{1,0:T(8,128)(2,1)S(1)} %get-tuple-element.140), channel_id=1, source_target_pairs={{0,16},{8,24},{16,0},{24,8},{1,17},{9,25},{17,1},{25,9},{2,18},{10... | collective-permute-start | bytes 884744 | tf_op jit(solution)/shard_map/ppermute | solution.py:738
  340.8 28.6 %collective-permute-start.60 = (bf16[4,96,768]{2,1,0:T(8,128)(2,1)S(1)}, bf16[4,96,768]{2,1,0:T(8,128)(2,1)S(1)}, u32[]{:S(2)}, u32[]{:S(2)}) collective-permute-start(bf16[4,96,768]{2,1,0:T(8,128)(2,1)S(1)} %get-tuple-element.127), channel_id=1, source_target_pairs={{0,1},{1,0},{2,3},{3,2},{4,5},{5,4},{6,7},{7,6},{8,9},{9,8},{10,11... | collective-permute-start | bytes 1769480 | tf_op jit(solution)/shard_map/ppermute | solution.py:641
  341.9 27.6 %collective-permute-start.62 = (bf16[4,96,768]{2,1,0:T(8,128)(2,1)S(1)}, bf16[4,96,768]{2,1,0:T(8,128)(2,1)S(1)}, u32[]{:S(2)}, u32[]{:S(2)}) collective-permute-start(bf16[4,96,768]{2,1,0:T(8,128)(2,1)S(1)} %get-tuple-element.128), channel_id=1, source_target_pairs={{0,3},{1,2},{2,1},{3,0},{4,7},{5,6},{6,5},{7,4},{8,11},{9,10},{10,... | collective-permute-start | bytes 1769480 | tf_op jit(solution)/shard_map/ppermute | solution.py:641
  346.6 28.5 %collective-permute-start.61 = (bf16[4,96,768]{2,1,0:T(8,128)(2,1)S(1)}, bf16[4,96,768]{2,1,0:T(8,128)(2,1)S(1)}, u32[]{:S(2)}, u32[]{:S(2)}) collective-permute-start(bf16[4,96,768]{2,1,0:T(8,128)(2,1)S(1)} %get-tuple-element.129), channel_id=1, source_target_pairs={{0,2},{1,3},{2,0},{3,1},{4,6},{5,7},{6,4},{7,5},{8,10},{9,11},{10,... | collective-permute-start | bytes 1769480 | tf_op jit(solution)/shard_map/ppermute | solution.py:641
  375.7 9.4 %collective-permute-start.65 = (bf16[96,768]{1,0:T(8,128)(2,1)S(1)}, bf16[96,768]{1,0:T(8,128)(2,1)S(1)}, u32[]{:S(2)}, u32[]{:S(2)}) collective-permute-start(bf16[96,768]{1,0:T(8,128)(2,1)S(1)} %get-tuple-element.156), channel_id=1, source_target_pairs={{0,24},{8,16},{16,8},{24,0},{1,25},{9,17},{17,9},{25,1},{2,26},{10... | collective-permute-start | bytes 442376 | tf_op jit(solution)/shard_map/ppermute | solution.py:738
  377.3 13.8 %collective-permute-start.64 = (bf16[96,768]{1,0:T(8,128)(2,1)S(1)}, bf16[96,768]{1,0:T(8,128)(2,1)S(1)}, u32[]{:S(2)}, u32[]{:S(2)}) collective-permute-start(bf16[96,768]{1,0:T(8,128)(2,1)S(1)} %get-tuple-element.157), channel_id=1, source_target_pairs={{0,16},{8,24},{16,0},{24,8},{1,17},{9,25},{17,1},{25,9},{2,18},{10... | collective-permute-start | bytes 442376 | tf_op jit(solution)/shard_map/ppermute | solution.py:738
  (75 other events, 632.5 us)
Sparse Core Ops, SparseCore 0:
  150.3 47.9 reduce-scatter.7
  201.2 47.0 reduce-scatter.5
  250.7 96.1 reduce-scatter.3

commit v3 on v2

--- a/solution.py
+++ b/solution.py
@@ -217,10 +217,10 @@
         low = values[2 * p * rows:(2 * p + 1) * rows]
         high = values[(2 * p + 1) * rows:(2 * p + 2) * rows]
         mine[0, p ^ core_ref[1], :, cols] = jnp.where(core_ref[0] == 0, low, high)
-        theirs[0, p ^ core_ref[1], :, cols] = jnp.where(core_ref[0] == 0, high, low)
-
-
-def row_specs(parts, pieces, width, index):
+        theirs[0, p ^ core_ref[1], :, cols] = jnp.where(core_ref[0] == 0, high, low).astype(theirs.dtype)
+
+
+def row_specs(parts, pieces, width, index, away):
     rows = D // (2 * pieces)
     if rows % 8:
         shape = (D, width)
@@ -229,7 +229,7 @@
         shape = (pieces, rows, width)
         count = 2
     spec = pl.BlockSpec((1,) + shape, lambda m: (index(m),) + (0,) * len(shape))
-    return [spec] * count, [jax.ShapeDtypeStruct((parts,) + shape, F32)] * count
+    return [spec] * count, [jax.ShapeDtypeStruct((parts,) + shape, kind) for kind in (F32, away)[:count]]
 
 
 def smem():
@@ -292,7 +292,7 @@
     feat = D // parts
     images = mod.shape[1]
     whole = fixed(rows, D)
-    specs, shapes = row_specs(parts, pieces, 4 * feat, lambda m: m)
+    specs, shapes = row_specs(parts, pieces, 4 * feat, lambda m: m, BF)
     return pl.pallas_call(
         functools.partial(attn_bwd_kernel, shards=len(weights)),
         grid=(parts,),
@@ -593,7 +593,7 @@
     steps = tokens // rows
     ff = w_in.shape[1]
     moving = pl.BlockSpec((rows, D), lambda m: (m, 0))
-    specs, shapes = row_specs(1, pieces, 2 * ff, lambda m: 0)
+    specs, shapes = row_specs(1, pieces, 2 * ff, lambda m: 0, F32)
     return pl.pallas_call(
         functools.partial(shared_kernel, tiles=len(tiles)),
         grid=(steps,),
@@ -699,14 +699,23 @@
     ada_rows = D // (2 * pieces)
     place = lax.axis_index(DP) * 2 + core
 
-    def everyone(value):
-        if pieces > 8 or pieces & (pieces - 1):
-            return lax.all_gather(value, (DP, EXP), axis=0, tiled=False)
-        own = [value]
-        for m in range(1, pieces):
-            own.append(lax.ppermute(value, DP, [(i, i ^ m) for i in range(pieces)]))
+    def images_and_silu(grads, silu):
+        if pieces != 4:
+            images = lax.all_gather(grads, (DP, EXP), axis=0, tiled=False)
+            silu = lax.all_gather(silu, (DP, EXP), axis=0, tiled=False)
+            return images, lax.dynamic_slice_in_dim(silu, place * ada_rows, ada_rows, axis=2)
+        count, feat_own = grads.shape[1:]
+        wide = 2 * ada_rows
+        own = []
+        for m in range(pieces):
+            cols = lax.dynamic_slice_in_dim(silu, (flip ^ m) * wide, wide, axis=1)
+            part = jnp.concatenate([grads.reshape(6 * count, feat_own), cols], axis=0)
+            own.append(lax.ppermute(part, DP, [(i, i ^ m) for i in range(pieces)]) if m else part)
         own = jnp.stack(own)
-        return jnp.concatenate([own, other_core(own)], axis=0)
+        every = jnp.concatenate([own, other_core(own)], axis=0)
+        cols = every[:, 6 * count:]
+        cols = jnp.where(core == 0, cols[..., :ada_rows], cols[..., ada_rows:])
+        return every[:, :6 * count].reshape(2 * pieces, 6, count, feat_own), cols
 
     n1, qkv, ctx, attn, mid, n2 = attn_forward(
         core_id, x_rows, img_col, mod, seg_col, seg_row, weights, [], parts,
@@ -725,7 +734,7 @@
             cut = values.reshape(values.shape[0], pieces, 2, D // (2 * pieces), values.shape[2])
             low, high = cut[:, :, 0], cut[:, :, 1]
             parts_of = jnp.where(core == 0, low, high), jnp.where(core == 0, high, low)
-        return parts_of[0] + other_core(parts_of[1])
+        return parts_of[0], other_core(parts_of[1])
 
     def over_dp(values):
         return lax.psum_scatter(values, DP, scatter_dimension=0, tiled=False).astype(F32)
@@ -739,7 +748,8 @@
             total = total + moved.astype(F32)
         return total
 
-    half_shared = core_half(gw_shared)[0]
+    mine, theirs = core_half(gw_shared)
+    half_shared = mine[0] + theirs[0]
     grad_shared = pieces_over_dp(half_shared)
 
     ge_out_low = over_dp(gw_out_low)
@@ -775,12 +785,11 @@
     cuts = turned([gmod[:, :, i * feat:(i + 1) * feat] for i in range(parts)])
     got = exchanged(cuts)
     grad_image = (got[0] + got[1] + got[2] + got[3]).astype(BF)
-    image_all = everyone(grad_image)
-    silu_all = everyone(silu_cond)
-    silu_mine = lax.dynamic_slice_in_dim(silu_all, place * ada_rows, ada_rows, axis=2)
+    image_all, silu_mine = images_and_silu(grad_image, silu_cond)
     grad_ada = jnp.einsum("gid,gkic->dkc", silu_mine, image_all, preferred_element_type=F32)
 
-    attn_half = core_half(gw_attn)
+    mine, theirs = core_half(gw_attn)
+    attn_half = mine + theirs.astype(F32)
     attn_sum = attn_half[0]
     for m in range(1, parts):
         moved = across(attn_half[m].astype(BF), m)

time: 411 us -> 408 us (level)
  starting transfers between devices: 63.3 us -> 71.7 us
  waiting for transfers between devices: 111 us -> 104 us
  local copies, waits for them, and re-layouts: 28.1 us -> 23.8 us
    ppermute x6, starting transfers between devices: 7.1 us -> 20.6 us  [pieces_over_dp(): lax.ppermute(values[m].astype(BF), DP, [(i, i ^ m) for i in range(pieces)])]
    ppermute x36, waiting for transfers between devices: 55.7 us -> 51 us  [across(): return lax.ppermute(value, HID, [(i, i ^ mask) for i in range(parts)])]
    ppermute x6 -> x3, waiting for transfers between devices: 20 us -> 15.5 us  [images_and_silu(): lax.ppermute(part, DP, [(i, i ^ m) for i in range(pieces)])]
    ppermute x6 -> x3, starting transfers between devices: 8.77 us -> 4.45 us  [images_and_silu(): lax.ppermute(part, DP, [(i, i ^ m) for i in range(pieces)])]
    unnamed x114 -> x107, local copies, waits for them, and re-layouts: 16.9 us -> 13.9 us
  transfers between devices with their start and end apart: 73 -> 69, of which waited for: 30 -> 21; matrix products, arithmetic and copies ran while one was open for 16% -> 15% of each run, Pallas kernels for 24% -> 24%
where the time goes in v3:
time: 408 us; the launch traced here: 400 us
  Pallas kernels  136 us (33%)
  waiting for transfers between devices  104 us (25%)
  starting transfers between devices  71.7 us (18%)
  other arithmetic  45.4 us (11%)
  local copies, waits for them, and re-layouts  23.8 us (6%)
  between operations  14.8 us (4%)
    ppermute x36, waiting for transfers between devices, across(): return lax.ppermute(value, HID, [(i, i ^ mask) for i in range(parts)])  51 us
    ppermute x36, starting transfers between devices, across(): return lax.ppermute(value, HID, [(i, i ^ mask) for i in range(parts)])  43.3 us
    pallas_call x2, Pallas kernels, expert_one(): pl.pallas_call(functools.partial(expert_one_kernel, tiles=len(tiles), fir...  39.5 us
    ppermute x6, waiting for transfers between devices, pieces_over_dp(): lax.ppermute(values[m].astype(BF), DP, [(i, i ^ m) for i in range(pieces)])  35.3 us
    pallas_call x1, Pallas kernels, expert_two(): pl.pallas_call(expert_two_kernel, grid=(EXP_DEV,), in_specs=[fixed(*cols....  26.6 us
    pallas_call x1, Pallas kernels, attn_backward(): pl.pallas_call(functools.partial(attn_bwd_kernel, shards=len(weights)), g...  21.2 us
    ppermute x6, starting transfers between devices, pieces_over_dp(): lax.ppermute(values[m].astype(BF), DP, [(i, i ^ m) for i in range(pieces)])  20.6 us
    pallas_call x1, Pallas kernels, expert_mix(): pl.pallas_call(expert_mix_kernel, grid=(EXP_DEV,), in_specs=[fixed(*cols....  17 us
  transfers between devices with their start and end apart: 69, of which 21 were waited for; matrix products, arithmetic and copies ran while one was open for 15% of the time, Pallas kernels for 24%

profile of v3, /device:TPU:0, one launch (start us, length us, event | category | flops | bytes accessed | tf_op | source)
XLA Modules:
  0.0 399.7 jit_solution(8549491178375211164)
XLA Ops:
  11.2 3.0 collective-permute-start.7
  15.7 2.0 copy.36
  17.7 2.0 copy.35
  19.7 2.3 broadcast_select_fusion.15
  27.2 2.1 fusion.3
  30.1 2.2 pad_maximum_fusion.rest_0_
  32.3 2.1 collective-permute-done
  34.4 3.3 collective-permute-done.1
  51.3 2.0 shard_map.205
  53.4 2.7 collective-permute-done.6
  56.1 2.5 fusion.45
  63.6 7.9 %collective-permute-done.26.rest_12_.rest_7_ = bf16[256,768]{1,0:T(8,128)(2,1)S(1)} collective-permute-done((bf16[256,768]{1,0:T(8,128)(2,1)S(1)}, bf16[256,768]{1,0:T(8,128)(2,1)S(1)}, u32[]{:S(2)}, u32[]{:S(2)}) %collective-permute-start.26) | collective-permute-done | bytes 393248 | tf_op jit(solution)/shard_map/ppermute | solution.py:641
  75.7 10.6 %shard_map.206 = (bf16[256,768]{1,0:T(8,128)(2,1)}, bf16[4,256,576]{2,1,0:T(8,128)(2,1)}, bf16[4,256,192]{2,1,0:T(8,128)(2,1)}, f32[256,768]{1,0:T(8,128)}, f32[...) custom-call(bf16[256,768]{1,0:T(8,128)(2,1)} %pad_maximum_fusion.4.x_ref, s32[1024,1]{1,0:T(8,128)} %get-tuple-element.155.img_ref, ...), custom_call_target="tpu_custom_call" | custom-call | tf_op jit(solution)/shard_map/pallas_call | solution.py:117
  91.4 5.4 %collective-permute-done.16.rest_1_ = bf16[256,768]{1,0:T(8,128)(2,1)S(1)} collective-permute-done((bf16[256,768]{1,0:T(8,128)(2,1)}, bf16[256,768]{1,0:T(8,128)(2,1)S(1)}, u32[]{:S(2)}, u32[]{:S(2)}) %collective-permute-start.16) | collective-permute-done | bytes 393248 | tf_op jit(solution)/shard_map/ppermute | solution.py:641
  101.5 3.3 collective-permute-done.18.rest_3_
  104.8 2.5 collective-permute-done.19.rest_4_
  109.0 20.3 %shard_map.207 = (bf16[4,768,768]{2,1,0:T(8,128)(2,1)}, bf16[4,768,768]{2,1,0:T(8,128)(2,1)}, f32[4,768,768]{2,1,0:T(8,128)}, bf16[4,768,768]{2,1,0:T(8,128)(2,1)}, bf16[4,2,192,768]{3,2,1,0:T(8,128)(2,1)}) custom-call(f32[24,1024]{1,0:T(8,128)} %get-tuple-element.43.row_ref, bf16[4,768,768]{2,1,0:T(8,128)(2,1)} %win_ref.7, ...), custom_call_target="tpu_custom_call" | custom-call | tf_op jit(solution)/shard_map/pallas_call | solution.py:446
  129.3 19.2 %shard_map.208 = (bf16[4,768,768]{2,1,0:T(8,128)(2,1)}, bf16[4,768,768]{2,1,0:T(8,128)(2,1)}, f32[4,768,768]{2,1,0:T(8,128)}, bf16[4,768,768]{2,1,0:T(8,128)(2,1)}, bf16[4,2,192,768]{3,2,1,0:T(8,128)(2,1)}) custom-call(f32[24,1024]{1,0:T(8,128)} %get-tuple-element.43.row_ref, ...), custom_call_target="tpu_custom_call", output_to_operand_aliasing={{0}: (24, {}), {1}: (25, {}), {2}: (26, {}), {3}: (27, {})} | custom-call | tf_op jit(solution)/shard_map/pallas_call | solution.py:446
  149.3 17.0 %shard_map.209 = (f32[1024,768]{1,0:T(8,128)}, bf16[1024,768]{1,0:T(8,128)(2,1)}) custom-call(f32[1024,24]{1,0:T(8,128)} %get-tuple-element.42.col_ref, bf16[4,768,768]{2,1,0:T(8,128)(2,1)} %get-tuple-element.50.act_ref, bf16[4,768,768]{2,1,0:T(8,128)(2,1)} %wout_ref.5), custom_call_target="tpu_custom_call" | custom-call | tf_op jit(solution)/shard_map/pallas_call | solution.py:548
  166.4 26.6 %shard_map.212 = (bf16[4,4,192,768]{3,2,1,0:T(8,128)(2,1)}, f32[1024,768]{1,0:T(8,128)}, bf16[1024,768]{1,0:T(8,128)(2,1)}) custom-call(f32[1024,24]{1,0:T(8,128)} %get-tuple-element.42.col_ref, bf16[4,768,768]{2,1,0:T(8,128)(2,1)} %get-tuple-element.56.rows_ref, f32[4,768,768]{2,1,0:T(8,128)} %get-tuple-element.57.slope_ref, ...), custom_call_target="tpu_custom_call" | custom-call | tf_op jit(solution)/shard_map/pallas_call | solution.py:506
  193.6 16.6 %shard_map.210 = (f32[1024,768]{1,0:T(8,128)}, f32[1024,768]{1,0:T(8,128)}, f32[1,4,96,1536]{3,2,1,0:T(8,128)}, f32[1,4,96,1536]{3,2,1,0:T(8,128)}) custom-call(s32[1024,1]{1,0:T(8,128)} %get-tuple-element.155.img_ref, bf16[6,32,768]{2,1,0:T(8,128)(2,1)} %pad_maximum_fusion.6.mod_ref.gm_ref.gate_ref, bf16[768,768]{1,0:T(8,128)(2,1)} %win_ref.6, ...), custom_call_target="tpu_custom_call" | custom-call | tf_op jit(solution)/shard_map/pallas_call | solution.py:597
  210.3 1.9 copy-done.10
  212.2 3.1 fusion.39
  219.0 2.1 fusion.38
  223.6 4.8 %collective-permute-done.37 = bf16[256,768]{1,0:T(8,128)(2,1)S(1)} collective-permute-done((bf16[256,768]{1,0:T(8,128)(2,1)S(1)}, bf16[256,768]{1,0:T(8,128)(2,1)S(1)}, u32[]{:S(2)}, u32[]{:S(2)}) %collective-permute-start.37) | collective-permute-done | bytes 393248 | tf_op jit(solution)/shard_map/ppermute | solution.py:641
  228.9 7.9 %collective-permute-done.36 = bf16[256,768]{1,0:T(8,128)(2,1)S(1)} collective-permute-done((bf16[256,768]{1,0:T(8,128)(2,1)S(1)}, bf16[256,768]{1,0:T(8,128)(2,1)S(1)}, u32[]{:S(2)}, u32[]{:S(2)}) %collective-permute-start.36) | collective-permute-done | bytes 393248 | tf_op jit(solution)/shard_map/ppermute | solution.py:641
  239.3 2.7 shard_map.211
  242.0 2.0 broadcast_select_fusion.46
  246.1 7.7 %collective-permute-done.43 = bf16[256,768]{1,0:T(8,128)(2,1)} collective-permute-done((bf16[256,768]{1,0:T(8,128)(2,1)}, bf16[256,768]{1,0:T(8,128)(2,1)}, u32[]{:S(2)}, u32[]{:S(2)}) %collective-permute-start.43) | collective-permute-done | bytes 393248 | tf_op jit(solution)/shard_map/ppermute | solution.py:641
  255.2 2.3 fusion.5.gn2_ref
  257.5 21.2 %shard_map.213 = (bf16[256,768]{1,0:T(8,128)(2,1)}, f32[5,32,768]{2,1,0:T(8,128)}, f32[4,4,96,768]{3,2,1,0:T(8,128)}, bf16[4,4,96,768]{3,2,1,0:T(8,128)(2,1)}) custom-call(f32[256,768]{1,0:T(8,128)} %fusion.5.gn2_ref, f32[256,768]{1,0:T(8,128)} %get-tuple-element.44.mid_ref, f32[256,768]{1,0:T(8,128)} %get-tuple-element.62.attn_ref, ...), custom_call_target="tpu_custom_call" | custom-call | tf_op jit(solution)/shard_map/pallas_call | solution.py:296
  280.7 2.0 broadcast_select_fusion.58
  283.6 1.8 collective-permute-start.46
  288.2 1.8 collective-permute-start.49
  290.0 2.0 collective-permute-start.48
  301.3 2.6 collective-permute-start.52
  304.1 8.3 %collective-permute-done.51 = bf16[224,192]{1,0:T(8,128)(2,1)S(1)} collective-permute-done((bf16[224,192]{1,0:T(8,128)(2,1)S(1)}, bf16[224,192]{1,0:T(8,128)(2,1)S(1)}, u32[]{:S(2)}, u32[]{:S(2)}) %collective-permute-start.51) | collective-permute-done | bytes 86048 | tf_op jit(solution)/shard_map/ppermute | solution.py:713
  312.5 7.1 %collective-permute-done.52 = bf16[224,192]{1,0:T(8,128)(2,1)S(1)} collective-permute-done((bf16[224,192]{1,0:T(8,128)(2,1)S(1)}, bf16[224,192]{1,0:T(8,128)(2,1)S(1)}, u32[]{:S(2)}, u32[]{:S(2)}) %collective-permute-start.52) | collective-permute-done | bytes 86048 | tf_op jit(solution)/shard_map/ppermute | solution.py:713
  319.9 2.4 fusion.31
  322.3 4.2 %collective-permute-start.65 = (bf16[96,1536]{1,0:T(8,128)(2,1)S(1)}, bf16[96,1536]{1,0:T(8,128)(2,1)S(1)}, u32[]{:S(2)}, u32[]{:S(2)}) collective-permute-start(bf16[96,1536]{1,0:T(8,128)(2,1)S(1)} %get-tuple-element.135), channel_id=1, source_target_pairs={{0,24},{8,16},{16,8},{24,0},{1,25},{9,17},{17,9},{25,1},{2,26},{10... | collective-permute-start | bytes 884744 | tf_op jit(solution)/shard_map/ppermute | solution.py:747
  326.6 6.7 %collective-permute-start.64 = (bf16[96,1536]{1,0:T(8,128)(2,1)S(1)}, bf16[96,1536]{1,0:T(8,128)(2,1)S(1)}, u32[]{:S(2)}, u32[]{:S(2)}) collective-permute-start(bf16[96,1536]{1,0:T(8,128)(2,1)S(1)} %get-tuple-element.136), channel_id=1, source_target_pairs={{0,16},{8,24},{16,0},{24,8},{1,17},{9,25},{17,1},{25,9},{2,18},{10... | collective-permute-start | bytes 884744 | tf_op jit(solution)/shard_map/ppermute | solution.py:747
  336.0 2.6 collective-permute-start.58
  338.6 2.1 collective-permute-done.65
  341.6 26.6 %collective-permute-done.64 = bf16[96,1536]{1,0:T(8,128)(2,1)S(1)} collective-permute-done((bf16[96,1536]{1,0:T(8,128)(2,1)S(1)}, bf16[96,1536]{1,0:T(8,128)(2,1)S(1)}, u32[]{:S(2)}, u32[]{:S(2)}) %collective-permute-start.64) | collective-permute-done | bytes 294944 | tf_op jit(solution)/shard_map/ppermute | solution.py:747
  371.0 7.7 %collective-permute-start.60 = (bf16[96,768]{1,0:T(8,128)(2,1)S(1)}, bf16[96,768]{1,0:T(8,128)(2,1)S(1)}, u32[]{:S(2)}, u32[]{:S(2)}) collective-permute-start(bf16[96,768]{1,0:T(8,128)(2,1)S(1)} %get-tuple-element.153), channel_id=1, source_target_pairs={{0,16},{8,24},{16,0},{24,8},{1,17},{9,25},{17,1},{25,9},{2,18},{10... | collective-permute-start | bytes 442376 | tf_op jit(solution)/shard_map/ppermute | solution.py:747
  378.7 2.8 convert_bitcast_fusion
  381.5 6.6 %collective-permute-done.60 = bf16[96,768]{1,0:T(8,128)(2,1)S(1)} collective-permute-done((bf16[96,768]{1,0:T(8,128)(2,1)S(1)}, bf16[96,768]{1,0:T(8,128)(2,1)S(1)}, u32[]{:S(2)}, u32[]{:S(2)}) %collective-permute-start.60) | collective-permute-done | bytes 147488 | tf_op jit(solution)/shard_map/ppermute | solution.py:747
  390.0 2.9 bitcast_convert_fusion
  (278 shorter events, 83.5 us)
Async XLA Ops:
  7.2 371.5 %reduce-scatter.8.cloned.1.call-start = ((), (), s32[]{:S(2)}) async-start(), calls=%async_computation.5 | async-start | bytes 2949120 | tf_op jit(solution)/shard_map/reduce_scatter | solution.py:740
  11.2 33.5 %collective-permute-start.7 = (bf16[384,768]{1,0:T(8,128)(2,1)}, bf16[384,768]{1,0:T(8,128)(2,1)S(1)}, u32[]{:S(2)}, u32[]{:S(2)}) collective-permute-start(bf16[384,768]{1,0:T(8,128)(2,1)} %fusion.8), channel_id=1, source_target_pairs={{0,1},{1,0},{2,3},{3,2},{4,5},{5,4},{6,7},{7,6},{8,9},{9,8},{10,11... | collective-permute-start | bytes 1769480 | tf_op jit(solution)/shard_map/ppermute | solution.py:641
  14.1 31.7 %collective-permute-start.8 = (bf16[384,768]{1,0:T(8,128)(2,1)}, bf16[384,768]{1,0:T(8,128)(2,1)}, u32[]{:S(2)}, u32[]{:S(2)}) collective-permute-start(bf16[384,768]{1,0:T(8,128)(2,1)} %fusion.8), channel_id=1, source_target_pairs={{0,2},{1,3},{2,0},{3,1},{4,6},{5,7},{6,4},{7,5},{8,10},{9,11},{10,... | collective-permute-start | bytes 1769480 | tf_op jit(solution)/shard_map/ppermute | solution.py:641
  22.0 12.4 %collective-permute-start = (bf16[256,384]{1,0:T(8,128)(2,1)}, bf16[256,384]{1,0:T(8,128)(2,1)}, u32[]{:S(2)}, u32[]{:S(2)}) collective-permute-start(bf16[256,384]{1,0:T(8,128)(2,1)} %get-tuple-element.118), channel_id=1, source_target_pairs={{0,3},{1,2},{2,1},{3,0},{4,7},{5,6},{6,5},{7,4},{8,11},{9,10},{10,... | collective-permute-start | bytes 589832 | tf_op jit(solution)/shard_map/ppermute | solution.py:641
  23.5 14.2 %collective-permute-start.1 = (bf16[256,384]{1,0:T(8,128)(2,1)}, bf16[256,384]{1,0:T(8,128)(2,1)}, u32[]{:S(2)}, u32[]{:S(2)}) collective-permute-start(bf16[256,384]{1,0:T(8,128)(2,1)} %get-tuple-element.140), channel_id=1, source_target_pairs={{0,2},{1,3},{2,0},{3,1},{4,6},{5,7},{6,4},{7,5},{8,10},{9,11},{10,... | collective-permute-start | bytes 589832 | tf_op jit(solution)/shard_map/ppermute | solution.py:641
  24.9 14.3 %collective-permute-start.2 = (bf16[256,384]{1,0:T(8,128)(2,1)}, bf16[256,384]{1,0:T(8,128)(2,1)}, u32[]{:S(2)}, u32[]{:S(2)}) collective-permute-start(bf16[256,384]{1,0:T(8,128)(2,1)} %get-tuple-element.139), channel_id=1, source_target_pairs={{0,1},{1,0},{2,3},{3,2},{4,5},{5,4},{6,7},{7,6},{8,9},{9,8},{10,11... | collective-permute-start | bytes 589832 | tf_op jit(solution)/shard_map/ppermute | solution.py:641
  37.7 11.6 %collective-permute-start.4 = (bf16[6,32,192]{2,1,0:T(8,128)(2,1)}, bf16[6,32,192]{2,1,0:T(8,128)(2,1)S(1)}, u32[]{:S(2)}, u32[]{:S(2)}) collective-permute-start(bf16[6,32,192]{2,1,0:T(8,128)(2,1)} %fusion.3), channel_id=1, source_target_pairs={{0,3},{1,2},{2,1},{3,0},{4,7},{5,6},{6,5},{7,4},{8,11},{9,10},{10,... | collective-permute-start | bytes 221192 | tf_op jit(solution)/shard_map/ppermute | solution.py:641
  42.0 18.0 %collective-permute-start.25 = (bf16[256,768]{1,0:T(8,128)(2,1)S(1)}, bf16[256,768]{1,0:T(8,128)(2,1)S(1)}, u32[]{:S(2)}, u32[]{:S(2)}) collective-permute-start(bf16[256,768]{1,0:T(8,128)(2,1)S(1)} %pad_maximum_fusion.5.rest_10_.rest_5_.go_ref), channel_id=1, source_target_pairs={{0,1},{1,0},{2,3},{3,2},{4,5},{5,4},{6,7},{7,6},{8,9},{9,8},{10,11... | collective-permute-start | bytes 1179656 | tf_op jit(solution)/shard_map/ppermute | solution.py:641
  44.7 11.4 %collective-permute-start.6 = (bf16[6,32,192]{2,1,0:T(8,128)(2,1)}, bf16[6,32,192]{2,1,0:T(8,128)(2,1)S(1)}, u32[]{:S(2)}, u32[]{:S(2)}) collective-permute-start(bf16[6,32,192]{2,1,0:T(8,128)(2,1)} %fusion.3), channel_id=1, source_target_pairs={{0,1},{1,0},{2,3},{3,2},{4,5},{5,4},{6,7},{7,6},{8,9},{9,8},{10,11... | collective-permute-start | bytes 221192 | tf_op jit(solution)/shard_map/ppermute | solution.py:641
  45.9 14.5 %collective-permute-start.9 = (bf16[192,768]{1,0:T(8,128)(2,1)}, bf16[192,768]{1,0:T(8,128)(2,1)S(1)}, u32[]{:S(2)}, u32[]{:S(2)}) collective-permute-start(bf16[192,768]{1,0:T(8,128)(2,1)} %slice.281), channel_id=1, source_target_pairs={{0,2},{1,3},{2,0},{3,1},{4,6},{5,7},{6,4},{7,5},{8,10},{9,11},{10,... | collective-permute-start | bytes 884744 | tf_op jit(solution)/shard_map/ppermute | solution.py:641
  49.3 11.3 %collective-permute-start.10 = (bf16[192,768]{1,0:T(8,128)(2,1)}, bf16[192,768]{1,0:T(8,128)(2,1)}, u32[]{:S(2)}, u32[]{:S(2)}) collective-permute-start(bf16[192,768]{1,0:T(8,128)(2,1)} %slice.282), channel_id=1, source_target_pairs={{0,1},{1,0},{2,3},{3,2},{4,5},{5,4},{6,7},{7,6},{8,9},{9,8},{10,11... | collective-permute-start | bytes 884744 | tf_op jit(solution)/shard_map/ppermute | solution.py:641
  53.4 19.2 %collective-permute-start.11 = (bf16[384,768]{1,0:T(8,128)(2,1)S(1)}, bf16[384,768]{1,0:T(8,128)(2,1)S(1)}, u32[]{:S(2)}, u32[]{:S(2)}) collective-permute-start(bf16[384,768]{1,0:T(8,128)(2,1)S(1)} %collective-permute-done.7.rest_1_), channel_id=1, source_target_pairs={{0,4},{4,0},{1,5},{5,1},{2,6},{6,2},{3,7},{7,3},{8,12},{12,8},{9,1... | collective-permute-start | bytes 1769480 | tf_op jit(solution)/shard_map/ppermute | solution.py:644
  56.1 18.1 %collective-permute-start.12 = (bf16[384,768]{1,0:T(8,128)(2,1)}, bf16[384,768]{1,0:T(8,128)(2,1)S(1)}, u32[]{:S(2)}, u32[]{:S(2)}) collective-permute-start(bf16[384,768]{1,0:T(8,128)(2,1)} %collective-permute-done.8.rest_2_), channel_id=1, source_target_pairs={{0,4},{4,0},{1,5},{5,1},{2,6},{6,2},{3,7},{7,3},{8,12},{12,8},{9,1... | collective-permute-start | bytes 1769480 | tf_op jit(solution)/shard_map/ppermute | solution.py:644
  60.0 11.5 %collective-permute-start.26 = (bf16[256,768]{1,0:T(8,128)(2,1)S(1)}, bf16[256,768]{1,0:T(8,128)(2,1)S(1)}, u32[]{:S(2)}, u32[]{:S(2)}) collective-permute-start(bf16[256,768]{1,0:T(8,128)(2,1)S(1)} %pad_maximum_fusion.5.rest_10_.rest_5_.go_ref), channel_id=1, source_target_pairs={{0,2},{1,3},{2,0},{3,1},{4,6},{5,7},{6,4},{7,5},{8,10},{9,11},{10,... | collective-permute-start | bytes 1179656 | tf_op jit(solution)/shard_map/ppermute | solution.py:641
  60.3 13.9 %collective-permute-start.13 = (bf16[192,768]{1,0:T(8,128)(2,1)S(1)}, bf16[192,768]{1,0:T(8,128)(2,1)S(1)}, u32[]{:S(2)}, u32[]{:S(2)}) collective-permute-start(bf16[192,768]{1,0:T(8,128)(2,1)S(1)} %collective-permute-done.9.rest_3_), channel_id=1, source_target_pairs={{0,4},{4,0},{1,5},{5,1},{2,6},{6,2},{3,7},{7,3},{8,12},{12,8},{9,1... | collective-permute-start | bytes 884744 | tf_op jit(solution)/shard_map/ppermute | solution.py:644
  60.6 14.4 %collective-permute-start.14 = (bf16[192,768]{1,0:T(8,128)(2,1)}, bf16[192,768]{1,0:T(8,128)(2,1)S(1)}, u32[]{:S(2)}, u32[]{:S(2)}) collective-permute-start(bf16[192,768]{1,0:T(8,128)(2,1)} %collective-permute-done.10.rest_4_), channel_id=1, source_target_pairs={{0,4},{4,0},{1,5},{5,1},{2,6},{6,2},{3,7},{7,3},{8,12},{12,8},{9,1... | collective-permute-start | bytes 884744 | tf_op jit(solution)/shard_map/ppermute | solution.py:644
  71.5 19.2 %collective-permute-start.27 = (bf16[128,768]{1,0:T(8,128)(2,1)S(1)}, bf16[128,768]{1,0:T(8,128)(2,1)S(1)}, u32[]{:S(2)}, u32[]{:S(2)}) collective-permute-start(bf16[128,768]{1,0:T(8,128)(2,1)S(1)} %slice.290), channel_id=1, source_target_pairs={{0,2},{1,3},{2,0},{3,1},{4,6},{5,7},{6,4},{7,5},{8,10},{9,11},{10,... | collective-permute-start | bytes 589832 | tf_op jit(solution)/shard_map/ppermute | solution.py:641
  72.5 18.6 %collective-permute-start.28 = (bf16[128,768]{1,0:T(8,128)(2,1)}, bf16[128,768]{1,0:T(8,128)(2,1)S(1)}, u32[]{:S(2)}, u32[]{:S(2)}) collective-permute-start(bf16[128,768]{1,0:T(8,128)(2,1)} %slice.291), channel_id=1, source_target_pairs={{0,1},{1,0},{2,3},{3,2},{4,5},{5,4},{6,7},{7,6},{8,9},{9,8},{10,11... | collective-permute-start | bytes 589832 | tf_op jit(solution)/shard_map/ppermute | solution.py:641
  86.4 10.4 %collective-permute-start.16 = (bf16[256,768]{1,0:T(8,128)(2,1)}, bf16[256,768]{1,0:T(8,128)(2,1)S(1)}, u32[]{:S(2)}, u32[]{:S(2)}) collective-permute-start(bf16[256,768]{1,0:T(8,128)(2,1)} %get-tuple-element.45.rest_0_), channel_id=1, source_target_pairs={{0,1},{1,0},{2,3},{3,2},{4,5},{5,4},{6,7},{7,6},{8,9},{9,8},{10,11... | collective-permute-start | bytes 1179656 | tf_op jit(solution)/shard_map/ppermute | solution.py:641
  86.8 10.2 %collective-permute-start.17 = (bf16[256,768]{1,0:T(8,128)(2,1)}, bf16[256,768]{1,0:T(8,128)(2,1)S(1)}, u32[]{:S(2)}, u32[]{:S(2)}) collective-permute-start(bf16[256,768]{1,0:T(8,128)(2,1)} %get-tuple-element.45.rest_0_), channel_id=1, source_target_pairs={{0,2},{1,3},{2,0},{3,1},{4,6},{5,7},{6,4},{7,5},{8,10},{9,11},{10,... | collective-permute-start | bytes 1179656 | tf_op jit(solution)/shard_map/ppermute | solution.py:641
  97.4 9.9 %collective-permute-start.20 = (bf16[256,768]{1,0:T(8,128)(2,1)}, bf16[256,768]{1,0:T(8,128)(2,1)S(1)}, u32[]{:S(2)}, u32[]{:S(2)}) collective-permute-start(bf16[256,768]{1,0:T(8,128)(2,1)} %get-tuple-element.45.rest_0_), channel_id=1, source_target_pairs={{0,4},{4,0},{1,5},{5,1},{2,6},{6,2},{3,7},{7,3},{8,12},{12,8},{9,1... | collective-permute-start | bytes 1179656 | tf_op jit(solution)/shard_map/ppermute | solution.py:644
  148.5 230.2 %reduce-scatter.6.cloned.1.call-start = ((), (), s32[]{:S(2)}) async-start(), calls=%async_computation.4 | async-start | bytes 2949120 | tf_op jit(solution)/shard_map/reduce_scatter | solution.py:740
  149.3 240.8 %reduce-scatter.4.cloned.1.call-start = ((), (), s32[]{:S(2)}) async-start(), calls=%async_computation.3 | async-start | bytes 5898240 | tf_op jit(solution)/shard_map/reduce_scatter | solution.py:740
  166.3 44.0 %collective-permute-start.34 = (bf16[1024,768]{1,0:T(8,128)(2,1)}, bf16[1024,768]{1,0:T(8,128)(2,1)}, u32[]{:S(2)}, u32[]{:S(2)}) collective-permute-start(bf16[1024,768]{1,0:T(8,128)(2,1)} %get-tuple-element.54), channel_id=1, source_target_pairs={{0,4},{4,0},{1,5},{5,1},{2,6},{6,2},{3,7},{7,3},{8,12},{12,8},{9,1... | collective-permute-start | bytes 4718600 | tf_op jit(solution)/shard_map/ppermute | solution.py:644
  193.0 26.0 %collective-permute-start.41 = (bf16[1024,768]{1,0:T(8,128)(2,1)}, bf16[1024,768]{1,0:T(8,128)(2,1)}, u32[]{:S(2)}, u32[]{:S(2)}) collective-permute-start(bf16[1024,768]{1,0:T(8,128)(2,1)} %get-tuple-element.61), channel_id=1, source_target_pairs={{0,4},{4,0},{1,5},{5,1},{2,6},{6,2},{3,7},{7,3},{8,12},{12,8},{9,1... | collective-permute-start | bytes 4718600 | tf_op jit(solution)/shard_map/ppermute | solution.py:644
  210.2 109.7 %collective-permute-start.62 = (f32[1,4,96,1536]{3,2,1,0:T(8,128)}, f32[1,4,96,1536]{3,2,1,0:T(8,128)}, u32[]{:S(2)}, u32[]{:S(2)}) collective-permute-start(f32[1,4,96,1536]{3,2,1,0:T(8,128)} %get-tuple-element.72), channel_id=1, source_target_pairs={{0,4},{4,0},{1,5},{5,1},{2,6},{6,2},{3,7},{7,3},{8,12},{12,8},{9,1... | collective-permute-start | bytes 7077896 | tf_op jit(solution)/shard_map/ppermute | solution.py:644
  215.4 13.0 %collective-permute-start.37 = (bf16[256,768]{1,0:T(8,128)(2,1)S(1)}, bf16[256,768]{1,0:T(8,128)(2,1)S(1)}, u32[]{:S(2)}, u32[]{:S(2)}) collective-permute-start(bf16[256,768]{1,0:T(8,128)(2,1)S(1)} %get-tuple-element.130), channel_id=1, source_target_pairs={{0,3},{1,2},{2,1},{3,0},{4,7},{5,6},{6,5},{7,4},{8,11},{9,10},{10,... | collective-permute-start | bytes 1179656 | tf_op jit(solution)/shard_map/ppermute | solution.py:641
  217.0 19.9 %collective-permute-start.36 = (bf16[256,768]{1,0:T(8,128)(2,1)S(1)}, bf16[256,768]{1,0:T(8,128)(2,1)S(1)}, u32[]{:S(2)}, u32[]{:S(2)}) collective-permute-start(bf16[256,768]{1,0:T(8,128)(2,1)S(1)} %get-tuple-element.131), channel_id=1, source_target_pairs={{0,2},{1,3},{2,0},{3,1},{4,6},{5,7},{6,4},{7,5},{8,10},{9,11},{10,... | collective-permute-start | bytes 1179656 | tf_op jit(solution)/shard_map/ppermute | solution.py:641
  218.4 19.9 %collective-permute-start.35 = (bf16[256,768]{1,0:T(8,128)(2,1)S(1)}, bf16[256,768]{1,0:T(8,128)(2,1)S(1)}, u32[]{:S(2)}, u32[]{:S(2)}) collective-permute-start(bf16[256,768]{1,0:T(8,128)(2,1)S(1)} %get-tuple-element.129), channel_id=1, source_target_pairs={{0,1},{1,0},{2,3},{3,2},{4,5},{5,4},{6,7},{7,6},{8,9},{9,8},{10,11... | collective-permute-start | bytes 1179656 | tf_op jit(solution)/shard_map/ppermute | solution.py:641
  222.1 23.3 %collective-permute-start.44 = (bf16[256,768]{1,0:T(8,128)(2,1)}, bf16[256,768]{1,0:T(8,128)(2,1)}, u32[]{:S(2)}, u32[]{:S(2)}) collective-permute-start(bf16[256,768]{1,0:T(8,128)(2,1)} %get-tuple-element.127), channel_id=1, source_target_pairs={{0,3},{1,2},{2,1},{3,0},{4,7},{5,6},{6,5},{7,4},{8,11},{9,10},{10,... | collective-permute-start | bytes 1179656 | tf_op jit(solution)/shard_map/ppermute | solution.py:641
  228.4 25.4 %collective-permute-start.43 = (bf16[256,768]{1,0:T(8,128)(2,1)}, bf16[256,768]{1,0:T(8,128)(2,1)}, u32[]{:S(2)}, u32[]{:S(2)}) collective-permute-start(bf16[256,768]{1,0:T(8,128)(2,1)} %get-tuple-element.128), channel_id=1, source_target_pairs={{0,2},{1,3},{2,0},{3,1},{4,6},{5,7},{6,4},{7,5},{8,10},{9,11},{10,... | collective-permute-start | bytes 1179656 | tf_op jit(solution)/shard_map/ppermute | solution.py:641
  236.9 18.3 %collective-permute-start.42 = (bf16[256,768]{1,0:T(8,128)(2,1)S(1)}, bf16[256,768]{1,0:T(8,128)(2,1)}, u32[]{:S(2)}, u32[]{:S(2)}) collective-permute-start(bf16[256,768]{1,0:T(8,128)(2,1)S(1)} %get-tuple-element.126), channel_id=1, source_target_pairs={{0,1},{1,0},{2,3},{3,2},{4,5},{5,4},{6,7},{7,6},{8,9},{9,8},{10,11... | collective-permute-start | bytes 1179656 | tf_op jit(solution)/shard_map/ppermute | solution.py:641
  244.0 39.5 %collective-permute-start.38 = (bf16[256,192]{1,0:T(8,128)(2,1)}, bf16[256,192]{1,0:T(8,128)(2,1)}, u32[]{:S(2)}, u32[]{:S(2)}) collective-permute-start(bf16[256,192]{1,0:T(8,128)(2,1)} %get-tuple-element.162), channel_id=1, source_target_pairs={{0,3},{1,2},{2,1},{3,0},{4,7},{5,6},{6,5},{7,4},{8,11},{9,10},{10,... | collective-permute-start | bytes 294920 | tf_op jit(solution)/shard_map/ppermute | solution.py:641
  245.4 39.9 %collective-permute-start.39 = (bf16[256,192]{1,0:T(8,128)(2,1)}, bf16[256,192]{1,0:T(8,128)(2,1)}, u32[]{:S(2)}, u32[]{:S(2)}) collective-permute-start(bf16[256,192]{1,0:T(8,128)(2,1)} %get-tuple-element.109), channel_id=1, source_target_pairs={{0,2},{1,3},{2,0},{3,1},{4,6},{5,7},{6,4},{7,5},{8,10},{9,11},{10,... | collective-permute-start | bytes 294920 | tf_op jit(solution)/shard_map/ppermute | solution.py:641
  253.8 32.6 %collective-permute-start.40 = (bf16[256,192]{1,0:T(8,128)(2,1)}, bf16[256,192]{1,0:T(8,128)(2,1)}, u32[]{:S(2)}, u32[]{:S(2)}) collective-permute-start(bf16[256,192]{1,0:T(8,128)(2,1)} %get-tuple-element.161), channel_id=1, source_target_pairs={{0,1},{1,0},{2,3},{3,2},{4,5},{5,4},{6,7},{7,6},{8,9},{9,8},{10,11... | collective-permute-start | bytes 294920 | tf_op jit(solution)/shard_map/ppermute | solution.py:641
  292.0 43.0 %collective-permute-start.55 = (bf16[4,4,96,768]{3,2,1,0:T(8,128)(2,1)}, bf16[4,4,96,768]{3,2,1,0:T(8,128)(2,1)S(1)}, u32[]{:S(2)}, u32[]{:S(2)}) collective-permute-start(bf16[4,4,96,768]{3,2,1,0:T(8,128)(2,1)} %get-tuple-element.70), channel_id=1, source_target_pairs={{0,4},{4,0},{1,5},{5,1},{2,6},{6,2},{3,7},{7,3},{8,12},{12,8},{9,1... | collective-permute-start | bytes 7077896 | tf_op jit(solution)/shard_map/ppermute | solution.py:644
  299.7 12.8 %collective-permute-start.51 = (bf16[224,192]{1,0:T(8,128)(2,1)S(1)}, bf16[224,192]{1,0:T(8,128)(2,1)S(1)}, u32[]{:S(2)}, u32[]{:S(2)}) collective-permute-start(bf16[224,192]{1,0:T(8,128)(2,1)S(1)} %get-tuple-element.178), channel_id=1, source_target_pairs={{0,8},{8,0},{16,24},{24,16},{1,9},{9,1},{17,25},{25,17},{2,10},{10... | collective-permute-start | bytes 258056 | tf_op jit(solution)/shard_map/ppermute | solution.py:713
  301.3 18.3 %collective-permute-start.52 = (bf16[224,192]{1,0:T(8,128)(2,1)S(1)}, bf16[224,192]{1,0:T(8,128)(2,1)S(1)}, u32[]{:S(2)}, u32[]{:S(2)}) collective-permute-start(bf16[224,192]{1,0:T(8,128)(2,1)S(1)} %get-tuple-element.179), channel_id=1, source_target_pairs={{0,16},{8,24},{16,0},{24,8},{1,17},{9,25},{17,1},{25,9},{2,18},{10... | collective-permute-start | bytes 258056 | tf_op jit(solution)/shard_map/ppermute | solution.py:713
  303.9 15.7 %collective-permute-start.53 = (bf16[224,192]{1,0:T(8,128)(2,1)S(1)}, bf16[224,192]{1,0:T(8,128)(2,1)S(1)}, u32[]{:S(2)}, u32[]{:S(2)}) collective-permute-start(bf16[224,192]{1,0:T(8,128)(2,1)S(1)} %get-tuple-element.180), channel_id=1, source_target_pairs={{0,24},{8,16},{16,8},{24,0},{1,25},{9,17},{17,9},{25,1},{2,26},{10... | collective-permute-start | bytes 258056 | tf_op jit(solution)/shard_map/ppermute | solution.py:713
  319.7 14.0 %collective-permute-start.54 = (bf16[4,224,192]{2,1,0:T(8,128)(2,1)S(1)}, bf16[4,224,192]{2,1,0:T(8,128)(2,1)S(1)}, u32[]{:S(2)}, u32[]{:S(2)}) collective-permute-start(bf16[4,224,192]{2,1,0:T(8,128)(2,1)S(1)} %pad_maximum_fusion.3), channel_id=1, source_target_pairs={{0,4},{4,0},{1,5},{5,1},{2,6},{6,2},{3,7},{7,3},{8,12},{12,8},{9,1... | collective-permute-start | bytes 1032200 | tf_op jit(solution)/shard_map/ppermute | solution.py:644
  322.3 18.4 %collective-permute-start.65 = (bf16[96,1536]{1,0:T(8,128)(2,1)S(1)}, bf16[96,1536]{1,0:T(8,128)(2,1)S(1)}, u32[]{:S(2)}, u32[]{:S(2)}) collective-permute-start(bf16[96,1536]{1,0:T(8,128)(2,1)S(1)} %get-tuple-element.135), channel_id=1, source_target_pairs={{0,24},{8,16},{16,8},{24,0},{1,25},{9,17},{17,9},{25,1},{2,26},{10... | collective-permute-start | bytes 884744 | tf_op jit(solution)/shard_map/ppermute | solution.py:747
  326.6 41.6 %collective-permute-start.64 = (bf16[96,1536]{1,0:T(8,128)(2,1)S(1)}, bf16[96,1536]{1,0:T(8,128)(2,1)S(1)}, u32[]{:S(2)}, u32[]{:S(2)}) collective-permute-start(bf16[96,1536]{1,0:T(8,128)(2,1)S(1)} %get-tuple-element.136), channel_id=1, source_target_pairs={{0,16},{8,24},{16,0},{24,8},{1,17},{9,25},{17,1},{25,9},{2,18},{10... | collective-permute-start | bytes 884744 | tf_op jit(solution)/shard_map/ppermute | solution.py:747
  333.3 34.9 %collective-permute-start.63 = (bf16[96,1536]{1,0:T(8,128)(2,1)S(1)}, bf16[96,1536]{1,0:T(8,128)(2,1)S(1)}, u32[]{:S(2)}, u32[]{:S(2)}) collective-permute-start(bf16[96,1536]{1,0:T(8,128)(2,1)S(1)} %get-tuple-element.134), channel_id=1, source_target_pairs={{0,8},{8,0},{16,24},{24,16},{1,9},{9,1},{17,25},{25,17},{2,10},{10... | collective-permute-start | bytes 884744 | tf_op jit(solution)/shard_map/ppermute | solution.py:747
  336.0 33.2 %collective-permute-start.58 = (bf16[4,96,768]{2,1,0:T(8,128)(2,1)S(1)}, bf16[4,96,768]{2,1,0:T(8,128)(2,1)S(1)}, u32[]{:S(2)}, u32[]{:S(2)}) collective-permute-start(bf16[4,96,768]{2,1,0:T(8,128)(2,1)S(1)} %get-tuple-element.124), channel_id=1, source_target_pairs={{0,3},{1,2},{2,1},{3,0},{4,7},{5,6},{6,5},{7,4},{8,11},{9,10},{10,... | collective-permute-start | bytes 1769480 | tf_op jit(solution)/shard_map/ppermute | solution.py:641
  338.6 30.6 %collective-permute-start.57 = (bf16[4,96,768]{2,1,0:T(8,128)(2,1)S(1)}, bf16[4,96,768]{2,1,0:T(8,128)(2,1)S(1)}, u32[]{:S(2)}, u32[]{:S(2)}) collective-permute-start(bf16[4,96,768]{2,1,0:T(8,128)(2,1)S(1)} %get-tuple-element.125), channel_id=1, source_target_pairs={{0,2},{1,3},{2,0},{3,1},{4,6},{5,7},{6,4},{7,5},{8,10},{9,11},{10,... | collective-permute-start | bytes 1769480 | tf_op jit(solution)/shard_map/ppermute | solution.py:641
  340.7 28.4 %collective-permute-start.56 = (bf16[4,96,768]{2,1,0:T(8,128)(2,1)S(1)}, bf16[4,96,768]{2,1,0:T(8,128)(2,1)S(1)}, u32[]{:S(2)}, u32[]{:S(2)}) collective-permute-start(bf16[4,96,768]{2,1,0:T(8,128)(2,1)S(1)} %get-tuple-element.123), channel_id=1, source_target_pairs={{0,1},{1,0},{2,3},{3,2},{4,5},{5,4},{6,7},{7,6},{8,9},{9,8},{10,11... | collective-permute-start | bytes 1769480 | tf_op jit(solution)/shard_map/ppermute | solution.py:641
  369.5 12.0 %collective-permute-start.61 = (bf16[96,768]{1,0:T(8,128)(2,1)S(1)}, bf16[96,768]{1,0:T(8,128)(2,1)S(1)}, u32[]{:S(2)}, u32[]{:S(2)}) collective-permute-start(bf16[96,768]{1,0:T(8,128)(2,1)S(1)} %get-tuple-element.152), channel_id=1, source_target_pairs={{0,24},{8,16},{16,8},{24,0},{1,25},{9,17},{17,9},{25,1},{2,26},{10... | collective-permute-start | bytes 442376 | tf_op jit(solution)/shard_map/ppermute | solution.py:747
  371.0 17.1 %collective-permute-start.60 = (bf16[96,768]{1,0:T(8,128)(2,1)S(1)}, bf16[96,768]{1,0:T(8,128)(2,1)S(1)}, u32[]{:S(2)}, u32[]{:S(2)}) collective-permute-start(bf16[96,768]{1,0:T(8,128)(2,1)S(1)} %get-tuple-element.153), channel_id=1, source_target_pairs={{0,16},{8,24},{16,0},{24,8},{1,17},{9,25},{17,1},{25,9},{2,18},{10... | collective-permute-start | bytes 442376 | tf_op jit(solution)/shard_map/ppermute | solution.py:747
  (69 other events, 630.7 us)
Sparse Core Ops, SparseCore 0:
  148.6 47.9 reduce-scatter.7
  199.5 47.0 reduce-scatter.5
  249.0 102.5 reduce-scatter.3
